TPU v7x, 768 devices: a whole 4x8x12 slice. The times are simulated.
768 devices in a mesh: space: 48 (over z, y_lo, core), member: 16 (over y_hi, x).
Axes of the slice: x: 4, y: 8 (y_hi: 4, y_lo: 2; y = y_hi * 2 + y_lo), z: 12, core: 2. Of those that a mesh axis runs over, the one named last changes fastest.
Arguments:
- perturbation: float32 [16, 4, 16, 16, 6144], P('member', None, None, None, 'space'), may hold values from -6 to 6
- trajectory: bfloat16 [3, 16, 6, 16, 6144], P(None, 'member', None, None, 'space'), may hold values from -0.5 to 0.5
- site_col: int32 [48, 48, 128], P(None, 'space'), may hold values from 0 to 2047
- site_lev: int32 [48, 48, 128], P(None, 'space'), may hold values from 0 to 15
- obs_counts: int32 [48, 48], P(None, 'space'), may hold values from 0 to 128, as said below
- obs_weights: float32 [48, 48, 4, 128], P('space'), may hold values from -3 to 3
Outputs:
- final_state: float32 [16, 4, 16, 16, 6144], P('member', None, None, None, 'space')
- obs_equiv: float32 [16, 48, 48, 128], P('member', 'space')
Inputs may be any that keep to these rules, and one draw needn't show every extreme that they name: obs_counts[o, s] is the number of live leading slots of owner o in tile s; some pair has exactly 128, and owners differ in load by up to four times.
All inputs are finite; a program needn't handle non-finite values.
Results may differ from a plain program's by a relative error of at most 0.0003.
Values may be sent and summed in bfloat16 or wider, within the bound.
No kernel may reach another device: no remote copies, remote signals or barrier semaphores. Data moves between devices by JAX's collectives and lax.ppermute only.
A program may use at most 64 MiB of HBM per device.

v0:
```python
import jax
import jax.numpy as jnp
from jax import lax
from jax.sharding import PartitionSpec as P


def with_halo(array, sides, width):
    for axis, dim in sides:
        size, length = (lax.axis_size(axis), array.shape[dim])
        up = [(i, (i + 1) % size) for i in range(size)]
        down = [(j, i) for i, j in up]
        last = lax.slice_in_dim(array, length - width, length, axis=dim)
        first = lax.slice_in_dim(array, 0, width, axis=dim)
        before = lax.ppermute(last, axis, up)
        after = lax.ppermute(first, axis, down)
        array = jnp.concatenate([before, array, after], axis=dim)
    return array


def update(state, east, west, coef):
    rows = jnp.pad(state, ((0, 0), (0, 0), (0, 0), (1, 1), (0, 0)))
    north = rows[:, :, :, 2:, :]
    south = rows[:, :, :, :-2, :]
    planes = coef.astype(jnp.float32)
    along = planes[:, 0][None, None]
    across = planes[:, 1][None, None]
    fresh = state - along * (east - west) * 0.5 + 0.5 * along * along * (east - 2.0 * state + west)
    fresh = (
        fresh
        - across * (north - south) * 0.5
        + 0.5 * across * across * (north - 2.0 * state + south)
    )
    wind_u = state[:, 0]
    wind_v = state[:, 1]
    temper = fresh[:, 2] - (planes[:, 2][None] * wind_u + planes[:, 3][None] * wind_v)
    humid = fresh[:, 3] - (planes[:, 4][None] * wind_u + planes[:, 5][None] * wind_v)
    return jnp.stack([fresh[:, 0], fresh[:, 1], temper, humid], axis=1)


def advance(state, coef):
    padded = with_halo(state, (("space", 4),), 1)
    return update(state, padded[..., 2:], padded[..., :-2], coef)


def run_steps(state, get_planes, nsteps):
    for step in range(nsteps):
        state = advance(state, get_planes(step))
    return state


def on_device(perturbation, trajectory, site_col, site_lev, obs_counts, obs_weights):
    state = perturbation
    nsteps = trajectory.shape[0]
    gathered = lax.all_gather(trajectory, "member", axis=1, tiled=True)
    state = run_steps(state, lambda step: gathered[step], nsteps)
    levels = state.shape[2]
    lat_rows = state.shape[3]
    lon_cols = state.shape[4]
    flat = state.reshape(4, levels * lat_rows * lon_cols)
    index = site_lev[:, 0, :] * (lat_rows * lon_cols) + site_col[:, 0, :]
    tiles = index.shape[0]
    slots = index.shape[1]
    picked = jnp.take(flat, index.reshape(-1), axis=1).reshape(4, tiles, slots)
    picked = jnp.transpose(picked, (1, 0, 2))
    live = jnp.arange(slots, dtype=jnp.int32)[None, :] < obs_counts[:, 0][:, None]
    outgoing = jnp.where(live[:, None, :], picked, jnp.float32(0.0))
    received = lax.all_to_all(outgoing, "space", split_axis=0, concat_axis=0, tiled=True)
    summed = jnp.sum(obs_weights[0] * received, axis=1)
    obs_equiv = summed.reshape(1, 1, tiles, slots)
    return (state, obs_equiv)


def solution(mesh):
    in_specs = (
        P("member", None, None, None, "space"),
        P(None, "member", None, None, "space"),
        P(None, "space", None),
        P(None, "space", None),
        P(None, "space"),
        P("space", None, None, None),
    )
    out_specs = (P("member", None, None, None, "space"), P("member", "space", None, None))
    return jax.shard_map(
        on_device, mesh=mesh, in_specs=in_specs, out_specs=out_specs, check_vma=False
    )
```

profile of v0, /device:TPU:1, one launch (start us, length us, event | category | flops | bytes accessed | tf_op | source)
XLA Modules:
  0.0 190.7 jit_solution(10190194803882983097)
XLA Ops:
  7.2 0.7 all-gather.2.cloned.1.call-update
  7.9 1.5 fusion.30
  9.4 4.6 %collective-permute-start.1 = (f32[1,4,16,16,1]{4,3,2,1,0:T(8,128)S(1)}, f32[1,4,16,16,1]{4,3,2,1,0:T(8,128)S(1)}, u32[]{:S(2)}, u32[]{:S(2)}) collective-permute-start(f32[1,4,16,16,1]{4,3,2,1,0:T(8,128)S(1)} %get-tuple-element.29), channel_id=1, source_target_pairs={{0,16},{16,32},{32,48},{48,64},{64,80},{80,96},{96,112},{112,128},... | collective-permute-start | bytes 12296 | tf_op jit(solution)/shard_map/ppermute | solution.py:14
  14.1 9.8 %collective-permute-start = (f32[1,4,16,16,1]{4,3,2,1,0:T(8,128)S(1)}, f32[1,4,16,16,1]{4,3,2,1,0:T(8,128)S(1)}, u32[]{:S(2)}, u32[]{:S(2)}) collective-permute-start(f32[1,4,16,16,1]{4,3,2,1,0:T(8,128)S(1)} %get-tuple-element.30), channel_id=1, source_target_pairs={{16,0},{32,16},{48,32},{64,48},{80,64},{96,80},{112,96},{128,112},... | collective-permute-start | bytes 12296 | tf_op jit(solution)/shard_map/ppermute | solution.py:15
  23.8 0.8 compare_select_fusion
  24.6 0.7 iota_compare_fusion
  26.0 57.4 %all-gather.2.cloned.1.call-done = bf16[3,16,6,16,128]{4,3,1,2,0:T(8,128)(2,1)} async-done(((bf16[3,1,6,16,128]{4,3,1,2,0:T(8,128)(2,1)}), bf16[3,16,6,16,128]{4,3,1,2,0:T(8,128)(2,1)}) %all-gather.2.cloned.1.call-update) | async-done | bytes 1179664 | tf_op jit(solution)/shard_map/all_gather | solution.py:54
  83.4 1.5 fusion.2
  86.0 4.4 %collective-permute-start.3 = (f32[1,4,16,16,1]{4,3,2,1,0:T(8,128)S(1)}, f32[1,4,16,16,1]{4,3,2,1,0:T(8,128)S(1)}, u32[]{:S(2)}, u32[]{:S(2)}) collective-permute-start(f32[1,4,16,16,1]{4,3,2,1,0:T(8,128)S(1)} %get-tuple-element.27), channel_id=1, source_target_pairs={{0,16},{16,32},{32,48},{48,64},{64,80},{80,96},{96,112},{112,128},... | collective-permute-start | bytes 12296 | tf_op jit(solution)/shard_map/ppermute | solution.py:14
  90.4 2.0 %collective-permute-start.2 = (f32[1,4,16,16,1]{4,3,2,1,0:T(8,128)S(1)}, f32[1,4,16,16,1]{4,3,2,1,0:T(8,128)S(1)}, u32[]{:S(2)}, u32[]{:S(2)}) collective-permute-start(f32[1,4,16,16,1]{4,3,2,1,0:T(8,128)S(1)} %get-tuple-element.28), channel_id=1, source_target_pairs={{16,0},{32,16},{48,32},{64,48},{80,64},{96,80},{112,96},{128,112},... | collective-permute-start | bytes 12296 | tf_op jit(solution)/shard_map/ppermute | solution.py:15
  92.4 4.1 %collective-permute-done.3 = f32[1,4,16,16,1]{4,3,2,1,0:T(8,128)S(1)} collective-permute-done((f32[1,4,16,16,1]{4,3,2,1,0:T(8,128)S(1)}, f32[1,4,16,16,1]{4,3,2,1,0:T(8,128)S(1)}, u32[]{:S(2)}, u32[]{:S(2)}) %collective-permute-start.3) | collective-permute-done | bytes 4128 | tf_op jit(solution)/shard_map/ppermute | solution.py:14
  96.5 9.6 %collective-permute-done.2 = f32[1,4,16,16,1]{4,3,2,1,0:T(8,128)S(1)} collective-permute-done((f32[1,4,16,16,1]{4,3,2,1,0:T(8,128)S(1)}, f32[1,4,16,16,1]{4,3,2,1,0:T(8,128)S(1)}, u32[]{:S(2)}, u32[]{:S(2)}) %collective-permute-start.2) | collective-permute-done | bytes 4128 | tf_op jit(solution)/shard_map/ppermute | solution.py:15
  107.0 1.9 %collective-permute-start.5 = (f32[1,4,16,16,1]{4,3,2,1,0:T(8,128)S(1)}, f32[1,4,16,16,1]{4,3,2,1,0:T(8,128)S(1)}, u32[]{:S(2)}, u32[]{:S(2)}) collective-permute-start(f32[1,4,16,16,1]{4,3,2,1,0:T(8,128)S(1)} %get-tuple-element.25), channel_id=1, source_target_pairs={{0,16},{16,32},{32,48},{48,64},{64,80},{80,96},{96,112},{112,128},... | collective-permute-start | bytes 12296 | tf_op jit(solution)/shard_map/ppermute | solution.py:14
  109.0 2.4 %collective-permute-start.4 = (f32[1,4,16,16,1]{4,3,2,1,0:T(8,128)S(1)}, f32[1,4,16,16,1]{4,3,2,1,0:T(8,128)S(1)}, u32[]{:S(2)}, u32[]{:S(2)}) collective-permute-start(f32[1,4,16,16,1]{4,3,2,1,0:T(8,128)S(1)} %get-tuple-element.26), channel_id=1, source_target_pairs={{16,0},{32,16},{48,32},{64,48},{80,64},{96,80},{112,96},{128,112},... | collective-permute-start | bytes 12296 | tf_op jit(solution)/shard_map/ppermute | solution.py:15
  111.4 9.3 %collective-permute-done.5 = f32[1,4,16,16,1]{4,3,2,1,0:T(8,128)S(1)} collective-permute-done((f32[1,4,16,16,1]{4,3,2,1,0:T(8,128)S(1)}, f32[1,4,16,16,1]{4,3,2,1,0:T(8,128)S(1)}, u32[]{:S(2)}, u32[]{:S(2)}) %collective-permute-start.5) | collective-permute-done | bytes 4128 | tf_op jit(solution)/shard_map/ppermute | solution.py:14
  120.7 1.0 collective-permute-done.4
  123.0 8.5 %copy.17 = f32[4,32768]{0,1:T(8,128)} copy(f32[4,32768]{1,0:T(4,128)S(1)} %pad_maximum_fusion.17) | data formatting | bytes 1048576 | tf_op jit(solution)/shard_map/stack | solution.py:37
  131.5 24.8 %gather_fusion = f32[6144,4]{1,0:T(8,128)S(1)} fusion(f32[4,32768]{0,1:T(8,128)} %copy.17, s32[6144]{0:T(1024)} %broadcast_clamp_fusion), kind=kCustom, calls=%fused_computation | custom fusion | bytes 221184 | tf_op jit(solution)/shard_map/jit(_take)/gather | solution.py:63
  156.2 1.8 copy.18
  158.0 1.6 select_bitcast_fusion
  159.6 10.6 %all-to-all-start = ((f32[48,4,128]{2,1,0:T(4,128)}), f32[48,4,128]{2,1,0:T(4,128)S(1)}, u32[]{:S(2)}, u32[]{:S(2)}) async-start(f32[48,4,128]{2,1,0:T(4,128)} %select_bitcast_fusion), calls=%async_computation | async-start | bytes 196608 | tf_op jit(solution)/shard_map/all_to_all | solution.py:67
  170.3 1.7 pad_maximum_fusion.16
  172.0 10.3 %all-to-all-done = f32[48,4,128]{2,1,0:T(4,128)S(1)} async-done(((f32[48,4,128]{2,1,0:T(4,128)}), f32[48,4,128]{2,1,0:T(4,128)S(1)}, u32[]{:S(2)}, u32[]{:S(2)}) %all-to-all-start) | async-done | bytes 98336 | tf_op jit(solution)/shard_map/all_to_all | solution.py:67
  182.3 1.6 fusion.27
  (29 shorter events, 3.9 us)
Async XLA Ops:
  7.2 76.2 %all-gather.2.cloned.1.call-start = ((), (), s32[]{:S(2)}) async-start(), calls=%async_computation.1 | async-start | bytes 1253376 | tf_op jit(solution)/shard_map/all_gather | solution.py:54
  7.9 77.1 %copy-start = (f32[1,4,16,16,128]{4,3,2,1,0:T(8,128)S(1)}, f32[1,4,16,16,128]{4,3,2,1,0:T(8,128)}, u32[]{:S(2)}) copy-start(f32[1,4,16,16,128]{4,3,2,1,0:T(8,128)} %param.6) | copy-start | bytes 1572868
  9.4 75.5 %collective-permute-start.1 = (f32[1,4,16,16,1]{4,3,2,1,0:T(8,128)S(1)}, f32[1,4,16,16,1]{4,3,2,1,0:T(8,128)S(1)}, u32[]{:S(2)}, u32[]{:S(2)}) collective-permute-start(f32[1,4,16,16,1]{4,3,2,1,0:T(8,128)S(1)} %get-tuple-element.29), channel_id=1, source_target_pairs={{0,16},{16,32},{32,48},{48,64},{64,80},{80,96},{96,112},{112,128},... | collective-permute-start | bytes 12296 | tf_op jit(solution)/shard_map/ppermute | solution.py:14
  14.1 70.9 %collective-permute-start = (f32[1,4,16,16,1]{4,3,2,1,0:T(8,128)S(1)}, f32[1,4,16,16,1]{4,3,2,1,0:T(8,128)S(1)}, u32[]{:S(2)}, u32[]{:S(2)}) collective-permute-start(f32[1,4,16,16,1]{4,3,2,1,0:T(8,128)S(1)} %get-tuple-element.30), channel_id=1, source_target_pairs={{16,0},{32,16},{48,32},{64,48},{80,64},{96,80},{112,96},{128,112},... | collective-permute-start | bytes 12296 | tf_op jit(solution)/shard_map/ppermute | solution.py:15
  86.0 10.5 %collective-permute-start.3 = (f32[1,4,16,16,1]{4,3,2,1,0:T(8,128)S(1)}, f32[1,4,16,16,1]{4,3,2,1,0:T(8,128)S(1)}, u32[]{:S(2)}, u32[]{:S(2)}) collective-permute-start(f32[1,4,16,16,1]{4,3,2,1,0:T(8,128)S(1)} %get-tuple-element.27), channel_id=1, source_target_pairs={{0,16},{16,32},{32,48},{48,64},{64,80},{80,96},{96,112},{112,128},... | collective-permute-start | bytes 12296 | tf_op jit(solution)/shard_map/ppermute | solution.py:14
  90.4 15.7 %collective-permute-start.2 = (f32[1,4,16,16,1]{4,3,2,1,0:T(8,128)S(1)}, f32[1,4,16,16,1]{4,3,2,1,0:T(8,128)S(1)}, u32[]{:S(2)}, u32[]{:S(2)}) collective-permute-start(f32[1,4,16,16,1]{4,3,2,1,0:T(8,128)S(1)} %get-tuple-element.28), channel_id=1, source_target_pairs={{16,0},{32,16},{48,32},{64,48},{80,64},{96,80},{112,96},{128,112},... | collective-permute-start | bytes 12296 | tf_op jit(solution)/shard_map/ppermute | solution.py:15
  107.0 13.6 %collective-permute-start.5 = (f32[1,4,16,16,1]{4,3,2,1,0:T(8,128)S(1)}, f32[1,4,16,16,1]{4,3,2,1,0:T(8,128)S(1)}, u32[]{:S(2)}, u32[]{:S(2)}) collective-permute-start(f32[1,4,16,16,1]{4,3,2,1,0:T(8,128)S(1)} %get-tuple-element.25), channel_id=1, source_target_pairs={{0,16},{16,32},{32,48},{48,64},{64,80},{80,96},{96,112},{112,128},... | collective-permute-start | bytes 12296 | tf_op jit(solution)/shard_map/ppermute | solution.py:14
  109.0 12.7 %collective-permute-start.4 = (f32[1,4,16,16,1]{4,3,2,1,0:T(8,128)S(1)}, f32[1,4,16,16,1]{4,3,2,1,0:T(8,128)S(1)}, u32[]{:S(2)}, u32[]{:S(2)}) collective-permute-start(f32[1,4,16,16,1]{4,3,2,1,0:T(8,128)S(1)} %get-tuple-element.26), channel_id=1, source_target_pairs={{16,0},{32,16},{48,32},{64,48},{80,64},{96,80},{112,96},{128,112},... | collective-permute-start | bytes 12296 | tf_op jit(solution)/shard_map/ppermute | solution.py:15
  122.4 0.6 copy-start.1
  159.6 22.7 %all-to-all-start = ((f32[48,4,128]{2,1,0:T(4,128)}), f32[48,4,128]{2,1,0:T(4,128)S(1)}, u32[]{:S(2)}, u32[]{:S(2)}) async-start(f32[48,4,128]{2,1,0:T(4,128)} %select_bitcast_fusion), calls=%async_computation | async-start | bytes 196608 | tf_op jit(solution)/shard_map/all_to_all | solution.py:67
Sparse Core Ops, SparseCore 0:
  11.6 71.7 all-gather.1
where the time goes:
time: 192 us; the launch traced here: 191 us
  waiting for transfers between devices  92.4 us (48%)
  local copies, waits for them, and re-layouts  37.3 us (19%)
  starting transfers between devices  35.8 us (19%)
  between operations  14.3 us (7%)
  other arithmetic  11 us (6%)
    all_gather x1, waiting for transfers between devices, on_device(): gathered = lax.all_gather(trajectory, 'member', axis=1, tiled=True)  57.4 us
    gather x2, local copies, waits for them, and re-layouts, on_device(): picked = jnp.take(flat, index.reshape(-1), axis=1).reshape(4, tiles, slots)  26.6 us
    ppermute x3, starting transfers between devices, with_halo(): after = lax.ppermute(first, axis, down)  14.2 us
    ppermute x3, waiting for transfers between devices, with_halo(): before = lax.ppermute(last, axis, up)  13.3 us
    ppermute x3, starting transfers between devices, with_halo(): before = lax.ppermute(last, axis, up)  10.9 us
    all_to_all x1, starting transfers between devices, on_device(): lax.all_to_all(outgoing, 'space', split_axis=0, concat_axis=0, tiled=True)  10.6 us
    ppermute x3, waiting for transfers between devices, with_halo(): after = lax.ppermute(first, axis, down)  10.6 us
    all_to_all x1, waiting for transfers between devices, on_device(): lax.all_to_all(outgoing, 'space', split_axis=0, concat_axis=0, tiled=True)  10.3 us
  transfers between devices with their start and end apart: 8, of which 6 were waited for; matrix products, arithmetic and copies ran while one was open for 4% of the time, Pallas kernels for 0%

commit v1 on v0

v1 whole, which is shorter than its diff:
```python
import functools

import jax
import jax.numpy as jnp
from jax import lax
from jax.experimental import pallas as pl
from jax.experimental.pallas import tpu as pltpu
from jax.sharding import PartitionSpec as P

F32 = jnp.float32
BF16 = jnp.bfloat16
VMEM = pl.BlockSpec(memory_space=pltpu.VMEM)
HBM = pl.BlockSpec(memory_space=pltpu.HBM)


def lane_of(shape):
    return lax.broadcasted_iota(jnp.int32, shape, len(shape) - 1)


def spread_kernel(copies, t_ref, out_ref, sems):
    moves = [pltpu.make_async_copy(t_ref, out_ref.at[i], sems.at[i]) for i in range(copies)]
    for move in moves:
        move.start()
    for move in moves:
        move.wait()


def spread(planes, copies):
    return pl.pallas_call(
        functools.partial(spread_kernel, copies),
        out_shape=jax.ShapeDtypeStruct((copies,) + planes.shape, planes.dtype),
        in_specs=[VMEM],
        out_specs=HBM,
        scratch_shapes=[pltpu.SemaphoreType.DMA((copies,))],
        name="spread",
    )(planes)


def pack_kernel(levels, planes, p_ref, t_ref, out_ref):
    group = lane_of((16, 128)) // 8
    for field in range(4):
        packed = jnp.zeros((16, 128), F32)
        for level in range(levels):
            moved = pltpu.roll(p_ref[field, level], (level * 8 + 3) % 128, 1)
            packed = jnp.where(group == level, moved, packed)
        out_ref[field * 16 : field * 16 + 16, :] = packed
    packed = jnp.zeros((16, 128), F32)
    for k in range(planes):
        moved = pltpu.roll(t_ref[k * 16 : k * 16 + 16, :].astype(F32), (k * 8 + 3) % 128, 1)
        packed = jnp.where(group == k, moved, packed)
    out_ref[64:80, :] = packed


def pack_edges(state, planes):
    return pl.pallas_call(
        functools.partial(pack_kernel, 16, 12),
        out_shape=jax.ShapeDtypeStruct((80, 128), F32),
        in_specs=[VMEM, VMEM],
        out_specs=VMEM,
        name="pack_edges",
    )(state, planes)


def spread_edges_kernel(copies, west_ref, east_ref, out_ref):
    from_west = lane_of((16, 128)) % 8 < 3
    edge = jnp.where(from_west, west_ref[64:80, :], east_ref[64:80, :]).astype(BF16)
    for i in range(copies):
        out_ref[i] = edge


def spread_edges(west, east, copies):
    return pl.pallas_call(
        functools.partial(spread_edges_kernel, copies),
        out_shape=jax.ShapeDtypeStruct((copies, 16, 128), BF16),
        in_specs=[VMEM, VMEM],
        out_specs=VMEM,
        name="spread_edges",
    )(west, east)


def stencil_weights(planes):
    a, b = planes[0], planes[1]
    aa, bb = a * a, b * b
    return (
        1.0 - aa - bb,
        0.5 * (aa - a),
        0.5 * (aa + a),
        0.5 * (bb - b),
        0.5 * (bb + b),
    )


def apply_stencil(weights, planes, p, e, w, n, s):
    c0, ce, cw, cn, cs = weights
    new = [
        c0 * p[f] + ce * e[f] + cw * w[f] + cn * n[f] + cs * s[f]
        for f in range(4)
    ]
    new[2] = new[2] - (planes[2] * p[0] + planes[3] * p[1])
    new[3] = new[3] - (planes[4] * p[0] + planes[5] * p[1])
    return new


def north_south(p, first, last):
    north = [jnp.where(last, 0.0, pltpu.roll(x, 15, 0)) for x in p]
    south = [jnp.where(first, 0.0, pltpu.roll(x, 1, 0)) for x in p]
    return north, south


def advance_level(level, state, halo, t_ref, edge_planes):
    shape = (16, 128)
    lane = lane_of(shape)
    row = lax.broadcasted_iota(jnp.int32, shape, 0)
    lane_first, lane_last = lane == 0, lane == 127
    row_first, row_last = row == 0, row == 15
    for k in range(3):
        planes = [t_ref[level, (k * 6 + q) * 16 : (k * 6 + q + 1) * 16, :].astype(F32) for q in range(6)]
        east = [pltpu.roll(x, 127, 1) for x in state]
        west = [pltpu.roll(x, 1, 1) for x in state]
        halo_east = [pltpu.roll(x, 127, 1) for x in halo]
        halo_west = [pltpu.roll(x, 1, 1) for x in halo]
        north, south = north_south(state, row_first, row_last)
        new = apply_stencil(
            stencil_weights(planes),
            planes,
            state,
            [jnp.where(lane_last, h, x) for x, h in zip(east, halo_east)],
            [jnp.where(lane_first, h, x) for x, h in zip(west, halo_west)],
            north,
            south,
        )
        if k < 2:
            side = [pltpu.roll(edge_planes, (125 - (k * 6 + q) * 8) % 128, 1) for q in range(6)]
            north, south = north_south(halo, row_first, row_last)
            halo = apply_stencil(
                stencil_weights(side),
                side,
                halo,
                [jnp.where(lane_last, x, h) for x, h in zip(east, halo_east)],
                [jnp.where(lane_first, x, h) for x, h in zip(west, halo_west)],
                north,
                south,
            )
        state = new
    return state


def main_kernel(
    p_ref, t_ref, e_ref, west_ref, east_ref, row_ref, col_ref, out_ref, val_ref, halo_ref, high_ref, low_ref
):
    levels = p_ref.shape[1]
    owners = row_ref.shape[0]
    from_west = lane_of((64, 128)) % 8 < 3
    halo_ref[...] = jnp.where(from_west, west_ref[0:64, :], east_ref[0:64, :])

    def one_level(level, carry):
        shift = lax.rem(253 - level * 8, 128)
        state = [p_ref[f, level] for f in range(4)]
        halo = [pltpu.roll(halo_ref[f * 16 : f * 16 + 16, :], shift, 1) for f in range(4)]
        state = advance_level(level, state, halo, t_ref, e_ref[level].astype(F32))
        for f in range(4):
            out_ref[f, level] = state[f]
        return carry

    lax.fori_loop(0, levels, one_level, 0)

    for f in range(4):
        for half in range(2):
            block = out_ref[f, half * 8 : half * 8 + 8].reshape(128, 128)
            block = jnp.transpose(block)
            high = block.astype(BF16)
            low = (block - high.astype(F32)).astype(BF16)
            high_ref[f * 128 : f * 128 + 128, half * 128 : half * 128 + 128] = high
            low_ref[f * 128 : f * 128 + 128, half * 128 : half * 128 + 128] = low

    line = lax.broadcasted_iota(jnp.int32, (256, 128), 0)
    lon = lax.broadcasted_iota(jnp.int32, (128, 128), 0)

    def two_owners(i, carry):
        picks = []
        for o in range(2):
            hit = line == row_ref[pl.ds(2 * i + o, 1), :]
            picks.append(jnp.where(hit, 1.0, 0.0).astype(BF16))
        pick = jnp.concatenate(picks, axis=1)
        lines = jnp.dot(high_ref[...], pick, preferred_element_type=F32)
        lines = lines + jnp.dot(low_ref[...], pick, preferred_element_type=F32)
        for o in range(2):
            hit = lon == col_ref[pl.ds(2 * i + o, 1), :]
            for f in range(4):
                part = lines[f * 128 : f * 128 + 128, o * 128 : o * 128 + 128]
                val_ref[2 * i + o, f : f + 1, :] = jnp.sum(jnp.where(hit, part, 0.0), axis=0, keepdims=True)
        return carry

    lax.fori_loop(0, owners // 2, two_owners, 0)


def advance_and_pick(state, planes, edges, west, east, rows, cols):
    owners = rows.shape[0]
    return pl.pallas_call(
        main_kernel,
        out_shape=(
            jax.ShapeDtypeStruct(state.shape, F32),
            jax.ShapeDtypeStruct((owners, 4, 128), F32),
        ),
        in_specs=[VMEM] * 7,
        out_specs=(VMEM, VMEM),
        scratch_shapes=[
            pltpu.VMEM((64, 128), F32),
            pltpu.VMEM((512, 256), BF16),
            pltpu.VMEM((512, 256), BF16),
        ],
        name="advance_and_pick",
    )(state, planes, edges, west, east, rows, cols)


def on_device(perturbation, trajectory, site_col, site_lev, obs_counts, obs_weights):
    tiles, slots = site_col.shape[0], site_col.shape[2]
    members = lax.axis_size("member")
    state = perturbation[0]
    local = trajectory.reshape(288, 128)
    planes = lax.all_to_all(spread(local, members), "member", 0, 0, tiled=True)

    edges = pack_edges(state, local)
    up = [(i, (i + 1) % tiles) for i in range(tiles)]
    down = [(j, i) for i, j in up]
    west = lax.ppermute(edges, "space", up)
    east = lax.ppermute(edges, "space", down)
    side = lax.all_to_all(spread_edges(west, east, members), "member", 0, 0, tiled=True)

    live = jnp.arange(slots, dtype=jnp.int32)[None, :] < obs_counts
    rows = jnp.where(live, site_lev[:, 0, :] * 16 + site_col[:, 0, :] // 128, -1)
    cols = site_col[:, 0, :] % 128
    final, values = advance_and_pick(state, planes, side, west, east, rows, cols)
    received = lax.all_to_all(values, "space", 0, 0, tiled=True)
    summed = jnp.sum(obs_weights[0] * received, axis=1)
    return (final[None], summed.reshape(1, 1, tiles, slots))


def solution(mesh):
    in_specs = (
        P("member", None, None, None, "space"),
        P(None, "member", None, None, "space"),
        P(None, "space", None),
        P(None, "space", None),
        P(None, "space"),
        P("space", None, None, None),
    )
    out_specs = (P("member", None, None, None, "space"), P("member", "space", None, None))
    return jax.shard_map(
        on_device, mesh=mesh, in_specs=in_specs, out_specs=out_specs, check_vma=False
    )
```

time: 192 us -> 117 us (0.61)
  waiting for transfers between devices: 92.4 us -> 24.3 us
  blocking collectives: 0 us -> 45.9 us
  local copies, waits for them, and re-layouts: 37.3 us -> 2.27 us
  Pallas kernels: 0 us -> 20.9 us
  starting transfers between devices: 35.8 us -> 21.5 us
  between operations: 14.3 us -> 0.75 us
  other arithmetic: 11 us -> 1.35 us
    all_gather x1 -> x0, waiting for transfers between devices: 57.4 us -> none  [on_device(): gathered = lax.all_gather(trajectory, 'member', axis=1, tiled=True)]
    all_to_all x0 -> x1, blocking collectives: none -> 45.9 us  [on_device(): received = lax.all_to_all(values, 'space', 0, 0, tiled=True)]
    gather x2 -> x0, local copies, waits for them, and re-layouts: 26.6 us -> none  [on_device(): picked = jnp.take(flat, index.reshape(-1), axis=1).reshape(4, tiles, slots)]
    ppermute x6 -> x2, waiting for transfers between devices: 23.9 us -> 1.04 us  [the longest x1 1.04 us: on_device(): east = lax.ppermute(edges, 'space', down)]
    pallas_call x0 -> x4, Pallas kernels: none -> 20.9 us  [the longest x1 15.5 us: advance_and_pick(): pl.pallas_call(main_kernel, out_shape=(jax.ShapeDtypeStruct(state.shape,...]
    all_to_all x1 -> x2, waiting for transfers between devices: 10.3 us -> 23.3 us  [the longest x1 16.3 us: on_device(): planes = lax.all_to_all(spread(local, members), 'member', 0, 0, tiled=True)]
    ppermute x6 -> x2, starting transfers between devices: 25.1 us -> 14.3 us  [the longest x1 9.75 us: on_device(): east = lax.ppermute(edges, 'space', down)]
    another operation x2 -> x0, local copies, waits for them, and re-layouts: 8.63 us -> none  [update(): return jnp.stack([fresh[:, 0], fresh[:, 1], temper, humid], axis=1)]
  transfers between devices with their start and end apart: 8 -> 4, of which waited for: 6 -> 3; matrix products, arithmetic and copies ran while one was open for 4% -> 1% of each run, Pallas kernels for 0% -> 2%
where the time goes in v1:
time: 117 us
  blocking collectives  45.9 us (39%)
  waiting for transfers between devices  24.3 us (21%)
  starting transfers between devices  21.5 us (18%)
  Pallas kernels  20.9 us (18%)
  local copies, waits for them, and re-layouts  2.27 us (2%)
  other arithmetic  1.35 us (1%)
    all_to_all x1, blocking collectives, on_device(): received = lax.all_to_all(values, 'space', 0, 0, tiled=True)  45.9 us
    all_to_all x1, waiting for transfers between devices, on_device(): planes = lax.all_to_all(spread(local, members), 'member', 0, 0, tiled=True)  16.3 us
    pallas_call x1, Pallas kernels, advance_and_pick(): pl.pallas_call(main_kernel, out_shape=(jax.ShapeDtypeStruct(state.shape,...  15.5 us
    ppermute x1, starting transfers between devices, on_device(): east = lax.ppermute(edges, 'space', down)  9.75 us
    all_to_all x1, waiting for transfers between devices, on_device(): lax.all_to_all(spread_edges(west, east, members), 'member', 0, 0, tiled=T...  6.91 us
    ppermute x1, starting transfers between devices, on_device(): west = lax.ppermute(edges, 'space', up)  4.58 us
    all_to_all x1, starting transfers between devices, on_device(): planes = lax.all_to_all(spread(local, members), 'member', 0, 0, tiled=True)  3.7 us
    all_to_all x1, starting transfers between devices, on_device(): lax.all_to_all(spread_edges(west, east, members), 'member', 0, 0, tiled=T...  3.5 us
  transfers between devices with their start and end apart: 4, of which 3 were waited for; matrix products, arithmetic and copies ran while one was open for 1% of the time, Pallas kernels for 2%

profile of v1, /device:TPU:1, one launch (start us, length us, event | category | flops | bytes accessed | tf_op | source)
XLA Modules:
  0.0 116.9 jit_solution(10316694701405388391)
XLA Ops:
  0.6 1.9 %pack_edges.1 = f32[80,128]{1,0:T(8,128)} custom-call(f32[4,16,16,128]{3,2,1,0:T(8,128)} %bitcast.13, bf16[288,128]{1,0:T(8,128)(2,1)} %bitcast.15), custom_call_target="tpu_custom_call" | custom-call | tf_op jit(solution)/shard_map/pack_edges/pallas_call | solution.py:55
  2.5 4.6 %collective-permute-start = (f32[80,128]{1,0:T(8,128)}, f32[80,128]{1,0:T(8,128)S(1)}, u32[]{:S(2)}, u32[]{:S(2)}) collective-permute-start(f32[80,128]{1,0:T(8,128)} %pack_edges.1), channel_id=1, source_target_pairs={{0,16},{16,32},{32,48},{48,64},{64,80},{80,96},{96,112},{112,128},... | collective-permute-start | bytes 122888 | tf_op jit(solution)/shard_map/ppermute | solution.py:226
  7.1 9.8 %collective-permute-start.1 = (f32[80,128]{1,0:T(8,128)}, f32[80,128]{1,0:T(8,128)S(1)}, u32[]{:S(2)}, u32[]{:S(2)}) collective-permute-start(f32[80,128]{1,0:T(8,128)} %pack_edges.1), channel_id=1, source_target_pairs={{16,0},{32,16},{48,32},{64,48},{80,64},{96,80},{112,96},{128,112},... | collective-permute-start | bytes 122888 | tf_op jit(solution)/shard_map/ppermute | solution.py:227
  16.9 0.0 collective-permute-done.west_ref
  16.9 0.0 copy-start.2
  16.9 1.0 collective-permute-done.1.east_ref
  17.9 0.0 copy-done.2
  17.9 0.6 copy-done.3
  18.5 1.4 %spread_edges.1 = bf16[16,16,128]{2,1,0:T(8,128)(2,1)} custom-call(f32[80,128]{1,0:T(8,128)} %copy-done.2, f32[80,128]{1,0:T(8,128)} %copy-done.3), custom_call_target="tpu_custom_call" | custom-call | tf_op jit(solution)/shard_map/spread_edges/pallas_call | solution.py:72
  20.0 3.5 %all-to-all-start.1 = ((bf16[16,16,128]{2,1,0:T(8,128)(2,1)}), bf16[16,16,128]{2,1,0:T(8,128)(2,1)S(1)}, u32[]{:S(2)}, u32[]{:S(2)}) async-start(bf16[16,16,128]{2,1,0:T(8,128)(2,1)} %spread_edges.1), calls=%async_computation.1 | async-start | bytes 131072 | tf_op jit(solution)/shard_map/all_to_all | solution.py:228
  23.5 2.1 %spread.1 = bf16[16,288,128]{2,1,0:T(8,128)(2,1)} custom-call(bf16[288,128]{1,0:T(8,128)(2,1)} %bitcast.16), custom_call_target="tpu_custom_call" | custom-call | tf_op jit(solution)/shard_map/spread/pallas_call | solution.py:29
  25.5 0.0 copy-start.5
  25.5 0.0 copy-start.6
  25.6 0.0 copy-start.7
  25.6 6.9 %all-to-all-done.1.e_ref = bf16[16,16,128]{2,1,0:T(8,128)(2,1)S(1)} async-done(((bf16[16,16,128]{2,1,0:T(8,128)(2,1)}), bf16[16,16,128]{2,1,0:T(8,128)(2,1)S(1)}, u32[]{:S(2)}, u32[]{:S(2)}) %all-to-all-start.1) | async-done | bytes 65568 | tf_op jit(solution)/shard_map/all_to_all | solution.py:228
  32.5 0.6 copy-done.1
  33.1 3.7 %all-to-all-start = ((bf16[16,288,128]{2,1,0:T(8,128)(2,1)}), bf16[16,288,128]{2,1,0:T(8,128)(2,1)S(1)}, u32[]{:S(2)}, u32[]{:S(2)}) async-start(bf16[16,288,128]{2,1,0:T(8,128)(2,1)} %spread.1), calls=%async_computation | async-start | bytes 2359296 | tf_op jit(solution)/shard_map/all_to_all | solution.py:221
  36.8 0.0 copy-start.4
  36.8 0.7 add_select_fusion
  37.5 16.3 %all-to-all-done.t_ref = bf16[16,288,128]{2,1,0:T(8,128)(2,1)S(1)} async-done(((bf16[16,288,128]{2,1,0:T(8,128)(2,1)}), bf16[16,288,128]{2,1,0:T(8,128)(2,1)S(1)}, u32[]{:S(2)}, u32[]{:S(2)}) %all-to-all-start) | async-done | bytes 1179680 | tf_op jit(solution)/shard_map/all_to_all | solution.py:221
  53.9 1.0 copy-done
  54.9 15.5 %advance_and_pick.1 = (f32[4,16,16,128]{3,2,1,0:T(8,128)}, f32[48,4,128]{2,1,0:T(4,128)}) custom-call(f32[4,16,16,128]{3,2,1,0:T(8,128)} %bitcast.14, bf16[16,288,128]{2,1,0:T(8,128)(2,1)} %copy-done, bf16[16,16,128]{2,1,0:T(8,128)(2,1)} %copy-done.1, f32[80,128]{1,0:T(8,128)} %copy-done.2, f32[80,128]{1,0:T(8,128)} %copy-done.3, ...), custom_call_target="tpu_custom_call" | custom-call | tf_op jit(solution)/shard_map/advance_and_pick/pallas_call | solution.py:199
  70.4 45.9 %all_to_all.15 = f32[48,4,128]{2,1,0:T(4,128)S(1)} all-to-all(f32[48,4,128]{2,1,0:T(4,128)} %get-tuple-element.5), channel_id=1, replica_groups=mesh['space'=48,'member'=16] {'space'}, dimensions={0} | all-to-all | bytes 196608 | tf_op jit(solution)/shard_map/all_to_all | solution.py:234
  116.3 0.7 fusion
  (7 shorter events, 0.0 us)
Async XLA Ops:
  2.5 14.4 %collective-permute-start = (f32[80,128]{1,0:T(8,128)}, f32[80,128]{1,0:T(8,128)S(1)}, u32[]{:S(2)}, u32[]{:S(2)}) collective-permute-start(f32[80,128]{1,0:T(8,128)} %pack_edges.1), channel_id=1, source_target_pairs={{0,16},{16,32},{32,48},{48,64},{64,80},{80,96},{96,112},{112,128},... | collective-permute-start | bytes 122888 | tf_op jit(solution)/shard_map/ppermute | solution.py:226
  7.1 10.8 %collective-permute-start.1 = (f32[80,128]{1,0:T(8,128)}, f32[80,128]{1,0:T(8,128)S(1)}, u32[]{:S(2)}, u32[]{:S(2)}) collective-permute-start(f32[80,128]{1,0:T(8,128)} %pack_edges.1), channel_id=1, source_target_pairs={{16,0},{32,16},{48,32},{64,48},{80,64},{96,80},{112,96},{128,112},... | collective-permute-start | bytes 122888 | tf_op jit(solution)/shard_map/ppermute | solution.py:227
  16.9 1.1 copy-start.2
  17.9 0.6 copy-start.3
  20.0 12.5 %all-to-all-start.1 = ((bf16[16,16,128]{2,1,0:T(8,128)(2,1)}), bf16[16,16,128]{2,1,0:T(8,128)(2,1)S(1)}, u32[]{:S(2)}, u32[]{:S(2)}) async-start(bf16[16,16,128]{2,1,0:T(8,128)(2,1)} %spread_edges.1), calls=%async_computation.1 | async-start | bytes 131072 | tf_op jit(solution)/shard_map/all_to_all | solution.py:228
  25.5 11.3 %copy-start.5 = (s32[48,1,128]{2,1,0:T(1,128)S(1)}, s32[48,1,128]{2,1,0:T(1,128)}, u32[]{:S(2)}) copy-start(s32[48,1,128]{2,1,0:T(1,128)} %param.8) | copy-start | bytes 73732
  25.5 11.3 %copy-start.6 = (s32[48,1,128]{2,1,0:T(1,128)S(1)}, s32[48,1,128]{2,1,0:T(1,128)}, u32[]{:S(2)}) copy-start(s32[48,1,128]{2,1,0:T(1,128)} %param.9) | copy-start | bytes 73732
  25.6 11.3 %copy-start.7 = (s32[48,1]{0,1:T(1,128)S(1)}, s32[48,1]{0,1:T(1,128)}, u32[]{:S(2)}) copy-start(s32[48,1]{0,1:T(1,128)} %param.10) | copy-start | bytes 580
  32.5 0.6 copy-start.1
  33.1 20.8 %all-to-all-start = ((bf16[16,288,128]{2,1,0:T(8,128)(2,1)}), bf16[16,288,128]{2,1,0:T(8,128)(2,1)S(1)}, u32[]{:S(2)}, u32[]{:S(2)}) async-start(bf16[16,288,128]{2,1,0:T(8,128)(2,1)} %spread.1), calls=%async_computation | async-start | bytes 2359296 | tf_op jit(solution)/shard_map/all_to_all | solution.py:221
  36.8 79.5 %copy-start.4 = (f32[1,48,4,128]{3,2,1,0:T(4,128)S(1)}, f32[1,48,4,128]{3,2,1,0:T(4,128)}, u32[]{:S(2)}) copy-start(f32[1,48,4,128]{3,2,1,0:T(4,128)} %param.11) | copy-start | bytes 294916
  53.9 1.0 copy-start

commit v2 on v1

--- a/solution.py
+++ b/solution.py
@@ -18,7 +18,10 @@
 
 
 def spread_kernel(copies, t_ref, out_ref, sems):
-    moves = [pltpu.make_async_copy(t_ref, out_ref.at[i], sems.at[i]) for i in range(copies)]
+    rows = t_ref.shape[0]
+    moves = [
+        pltpu.make_async_copy(t_ref, out_ref.at[i, pl.ds(0, rows)], sems.at[i]) for i in range(copies)
+    ]
     for move in moves:
         move.start()
     for move in moves:
@@ -28,7 +31,7 @@
 def spread(planes, copies):
     return pl.pallas_call(
         functools.partial(spread_kernel, copies),
-        out_shape=jax.ShapeDtypeStruct((copies,) + planes.shape, planes.dtype),
+        out_shape=jax.ShapeDtypeStruct((copies, planes.shape[0] + 16, 128), planes.dtype),
         in_specs=[VMEM],
         out_specs=HBM,
         scratch_shapes=[pltpu.SemaphoreType.DMA((copies,))],
@@ -36,46 +39,70 @@
     )(planes)
 
 
-def pack_kernel(levels, planes, p_ref, t_ref, out_ref):
+def pack_state_kernel(p_ref, out_ref):
     group = lane_of((16, 128)) // 8
     for field in range(4):
         packed = jnp.zeros((16, 128), F32)
-        for level in range(levels):
+        for level in range(p_ref.shape[1]):
             moved = pltpu.roll(p_ref[field, level], (level * 8 + 3) % 128, 1)
             packed = jnp.where(group == level, moved, packed)
         out_ref[field * 16 : field * 16 + 16, :] = packed
+
+
+def pack_state(state):
+    return pl.pallas_call(
+        pack_state_kernel,
+        out_shape=jax.ShapeDtypeStruct((64, 128), F32),
+        in_specs=[VMEM],
+        out_specs=VMEM,
+        name="pack_state",
+    )(state)
+
+
+def pack_planes_kernel(t_ref, out_ref):
+    group = lane_of((16, 128)) // 8
     packed = jnp.zeros((16, 128), F32)
-    for k in range(planes):
+    for k in range(12):
         moved = pltpu.roll(t_ref[k * 16 : k * 16 + 16, :].astype(F32), (k * 8 + 3) % 128, 1)
         packed = jnp.where(group == k, moved, packed)
-    out_ref[64:80, :] = packed
-
-
-def pack_edges(state, planes):
-    return pl.pallas_call(
-        functools.partial(pack_kernel, 16, 12),
-        out_shape=jax.ShapeDtypeStruct((80, 128), F32),
-        in_specs=[VMEM, VMEM],
+    out_ref[...] = packed.astype(BF16)
+
+
+def pack_planes(planes):
+    return pl.pallas_call(
+        pack_planes_kernel,
+        out_shape=jax.ShapeDtypeStruct((16, 128), BF16),
+        in_specs=[VMEM],
         out_specs=VMEM,
-        name="pack_edges",
-    )(state, planes)
-
-
-def spread_edges_kernel(copies, west_ref, east_ref, out_ref):
-    from_west = lane_of((16, 128)) % 8 < 3
-    edge = jnp.where(from_west, west_ref[64:80, :], east_ref[64:80, :]).astype(BF16)
-    for i in range(copies):
-        out_ref[i] = edge
-
-
-def spread_edges(west, east, copies):
-    return pl.pallas_call(
-        functools.partial(spread_edges_kernel, copies),
-        out_shape=jax.ShapeDtypeStruct((copies, 16, 128), BF16),
-        in_specs=[VMEM, VMEM],
-        out_specs=VMEM,
-        name="spread_edges",
-    )(west, east)
+        name="pack_planes",
+    )(planes)
+
+
+def from_partner(shape, odd):
+    return (lane_of(shape) % 8 < 3) == (odd == 1)
+
+
+def fill_kernel(odd_ref, near_ref, far_ref, whole_ref, out_ref, edge_ref, sem):
+    near, far = near_ref[...].astype(F32), far_ref[...].astype(F32)
+    edge = jnp.where(from_partner((16, 128), odd_ref[0]), near, far).astype(BF16)
+    for i in range(edge_ref.shape[0]):
+        edge_ref[i] = edge
+    rows = out_ref.shape[1] - 16
+    move = pltpu.make_async_copy(edge_ref, out_ref.at[:, pl.ds(rows, 16)], sem)
+    move.start()
+    move.wait()
+
+
+def fill_edges(odd, near, far, whole):
+    return pl.pallas_call(
+        fill_kernel,
+        out_shape=jax.ShapeDtypeStruct(whole.shape, whole.dtype),
+        in_specs=[pl.BlockSpec(memory_space=pltpu.SMEM), VMEM, VMEM, HBM],
+        out_specs=HBM,
+        scratch_shapes=[pltpu.VMEM((whole.shape[0], 16, 128), BF16), pltpu.SemaphoreType.DMA],
+        input_output_aliases={3: 0},
+        name="fill_edges",
+    )(odd, near, far, whole)
 
 
 def stencil_weights(planes):
@@ -146,23 +173,22 @@
 
 
 def main_kernel(
-    p_ref, t_ref, e_ref, west_ref, east_ref, row_ref, col_ref, out_ref, val_ref, halo_ref, high_ref, low_ref
+    odd_ref, p_ref, t_ref, near_ref, far_ref, row_ref, col_ref, out_ref, val_ref, halo_ref, high_ref, low_ref
 ):
     levels = p_ref.shape[1]
     owners = row_ref.shape[0]
-    from_west = lane_of((64, 128)) % 8 < 3
-    halo_ref[...] = jnp.where(from_west, west_ref[0:64, :], east_ref[0:64, :])
+    halo_ref[...] = jnp.where(from_partner((64, 128), odd_ref[0]), near_ref[...], far_ref[...])
 
     def one_level(level, carry):
         shift = lax.rem(253 - level * 8, 128)
         state = [p_ref[f, level] for f in range(4)]
         halo = [pltpu.roll(halo_ref[f * 16 : f * 16 + 16, :], shift, 1) for f in range(4)]
-        state = advance_level(level, state, halo, t_ref, e_ref[level].astype(F32))
+        state = advance_level(level, state, halo, t_ref, t_ref[level, 288:304, :].astype(F32))
         for f in range(4):
             out_ref[f, level] = state[f]
         return carry
 
-    lax.fori_loop(0, levels, one_level, 0)
+    lax.fori_loop(0, levels, one_level, 0, unroll=2)
 
     for f in range(4):
         for half in range(2):
@@ -191,10 +217,10 @@
                 val_ref[2 * i + o, f : f + 1, :] = jnp.sum(jnp.where(hit, part, 0.0), axis=0, keepdims=True)
         return carry
 
-    lax.fori_loop(0, owners // 2, two_owners, 0)
-
-
-def advance_and_pick(state, planes, edges, west, east, rows, cols):
+    lax.fori_loop(0, owners // 2, two_owners, 0, unroll=2)
+
+
+def advance_and_pick(odd, state, planes, near, far, rows, cols):
     owners = rows.shape[0]
     return pl.pallas_call(
         main_kernel,
@@ -202,7 +228,7 @@
             jax.ShapeDtypeStruct(state.shape, F32),
             jax.ShapeDtypeStruct((owners, 4, 128), F32),
         ),
-        in_specs=[VMEM] * 7,
+        in_specs=[pl.BlockSpec(memory_space=pltpu.SMEM)] + [VMEM] * 6,
         out_specs=(VMEM, VMEM),
         scratch_shapes=[
             pltpu.VMEM((64, 128), F32),
@@ -210,7 +236,7 @@
             pltpu.VMEM((512, 256), BF16),
         ],
         name="advance_and_pick",
-    )(state, planes, edges, west, east, rows, cols)
+    )(odd, state, planes, near, far, rows, cols)
 
 
 def on_device(perturbation, trajectory, site_col, site_lev, obs_counts, obs_weights):
@@ -218,19 +244,28 @@
     members = lax.axis_size("member")
     state = perturbation[0]
     local = trajectory.reshape(288, 128)
-    planes = lax.all_to_all(spread(local, members), "member", 0, 0, tiled=True)
-
-    edges = pack_edges(state, local)
-    up = [(i, (i + 1) % tiles) for i in range(tiles)]
-    down = [(j, i) for i, j in up]
-    west = lax.ppermute(edges, "space", up)
-    east = lax.ppermute(edges, "space", down)
-    side = lax.all_to_all(spread_edges(west, east, members), "member", 0, 0, tiled=True)
+    odd = (lax.axis_index("space") % 2).astype(jnp.int32).reshape(1)
+    pairs = [(i, i ^ 1) for i in range(tiles)]
+    crossed = [(i, (i + 1) % tiles if i % 2 else (i - 1) % tiles) for i in range(tiles)]
+
+    edge = pack_planes(local)
+    far = lax.ppermute(edge, "space", crossed)
+    near = lax.ppermute(edge, "space", pairs)
+    copies = fill_edges(odd, near, far, spread(local, members))
+    planes = lax.all_to_all(copies, "member", 0, 0, tiled=True)
+
+    state_late, _ = lax.optimization_barrier((state, copies))
+    edge = pack_state(state_late)
+    far = lax.ppermute(edge, "space", crossed)
+    near = lax.ppermute(edge, "space", pairs)
 
     live = jnp.arange(slots, dtype=jnp.int32)[None, :] < obs_counts
     rows = jnp.where(live, site_lev[:, 0, :] * 16 + site_col[:, 0, :] // 128, -1)
     cols = site_col[:, 0, :] % 128
-    final, values = advance_and_pick(state, planes, side, west, east, rows, cols)
+    planes = pltpu.with_memory_space_constraint(planes, pltpu.VMEM)
+    near = pltpu.with_memory_space_constraint(near, pltpu.VMEM)
+    far = pltpu.with_memory_space_constraint(far, pltpu.VMEM)
+    final, values = advance_and_pick(odd, state, planes, near, far, rows, cols)
     received = lax.all_to_all(values, "space", 0, 0, tiled=True)
     summed = jnp.sum(obs_weights[0] * received, axis=1)
     return (final[None], summed.reshape(1, 1, tiles, slots))

time: 117 us -> 98.3 us (0.84)
  blocking collectives: 45.9 us -> 30.1 us
  starting transfers between devices: 21.5 us -> 30.8 us
  waiting for transfers between devices: 24.3 us -> 16.1 us
  Pallas kernels: 20.9 us -> 17.9 us
  local copies, waits for them, and re-layouts: 2.27 us -> 0.62 us
    all_to_all x2 -> x1, waiting for transfers between devices: 23.3 us -> 6.05 us  [on_device(): planes = lax.all_to_all(copies, 'member', 0, 0, tiled=True)]
    all_to_all x1, blocking collectives: 45.9 us -> 30.1 us  [on_device(): received = lax.all_to_all(values, 'space', 0, 0, tiled=True)]
    ppermute x2 -> x4, starting transfers between devices: 14.3 us -> 26.9 us  [the longest x2 23.1 us: on_device(): near = lax.ppermute(edge, 'space', pairs)]
    ppermute x2 -> x4, waiting for transfers between devices: 1.04 us -> 10.1 us  [the longest x2 10.1 us: on_device(): far = lax.ppermute(edge, 'space', crossed)]
    pallas_call x1, Pallas kernels: 15.5 us -> 11 us  [advance_and_pick(): pl.pallas_call(main_kernel, out_shape=(jax.ShapeDtypeStruct(state.shape,...]
    all_to_all x2 -> x1, starting transfers between devices: 7.2 us -> 3.84 us  [on_device(): planes = lax.all_to_all(copies, 'member', 0, 0, tiled=True)]
    unnamed x16 -> x12, local copies, waits for them, and re-layouts: 2.27 us -> 0.62 us
    pallas_call x2 -> x3, Pallas kernels: 3.31 us -> 4.8 us  [the longest x1 1.89 us: pack_state(): pl.pallas_call(pack_state_kernel, out_shape=jax.ShapeDtypeStruct((64, 128...]
  transfers between devices with their start and end apart: 4 -> 5, of which waited for: 3 -> 3; matrix products, arithmetic and copies ran while one was open for 1% -> 1% of each run, Pallas kernels for 2% -> 4%
where the time goes in v2:
time: 98.3 us; the launch traced here: 97.7 us
  starting transfers between devices  30.8 us (31%)
  blocking collectives  30.1 us (31%)
  Pallas kernels  17.9 us (18%)
  waiting for transfers between devices  16.1 us (16%)
  other arithmetic  1.35 us (1%)
    all_to_all x1, blocking collectives, on_device(): received = lax.all_to_all(values, 'space', 0, 0, tiled=True)  30.1 us
    ppermute x2, starting transfers between devices, on_device(): near = lax.ppermute(edge, 'space', pairs)  23.1 us
    pallas_call x1, Pallas kernels, advance_and_pick(): pl.pallas_call(main_kernel, out_shape=(jax.ShapeDtypeStruct(state.shape,...  11 us
    ppermute x2, waiting for transfers between devices, on_device(): far = lax.ppermute(edge, 'space', crossed)  10.1 us
    all_to_all x1, waiting for transfers between devices, on_device(): planes = lax.all_to_all(copies, 'member', 0, 0, tiled=True)  6.05 us
    all_to_all x1, starting transfers between devices, on_device(): planes = lax.all_to_all(copies, 'member', 0, 0, tiled=True)  3.84 us
    ppermute x2, starting transfers between devices, on_device(): far = lax.ppermute(edge, 'space', crossed)  3.84 us
    pallas_call x1, Pallas kernels, spread(): pl.pallas_call(functools.partial(spread_kernel, copies), out_shape=jax.Sh...  2.08 us
  transfers between devices with their start and end apart: 5, of which 3 were waited for; matrix products, arithmetic and copies ran while one was open for 1% of the time, Pallas kernels for 4%

profile of v2, /device:TPU:1, one launch (start us, length us, event | category | flops | bytes accessed | tf_op | source)
XLA Modules:
  0.0 97.7 jit_solution(374564792517268976)
XLA Ops:
  0.6 1.6 %pack_planes.1 = bf16[16,128]{1,0:T(8,128)(2,1)} custom-call(bf16[288,128]{1,0:T(8,128)(2,1)} %bitcast.16), custom_call_target="tpu_custom_call" | custom-call | tf_op jit(solution)/shard_map/pack_planes/pallas_call | solution.py:72
  2.2 12.4 %collective-permute-start = (bf16[16,128]{1,0:T(8,128)(2,1)}, bf16[16,128]{1,0:T(8,128)(2,1)S(1)}, u32[]{:S(2)}, u32[]{:S(2)}) collective-permute-start(bf16[16,128]{1,0:T(8,128)(2,1)} %pack_planes.1), channel_id=1, source_target_pairs={{0,16},{16,0},{32,48},{48,32},{64,80},{80,64},{96,112},{112,96},{1... | collective-permute-start | bytes 12296 | tf_op jit(solution)/shard_map/ppermute | solution.py:253
  14.6 1.9 %collective-permute-start.1 = (bf16[16,128]{1,0:T(8,128)(2,1)}, bf16[16,128]{1,0:T(8,128)(2,1)S(1)}, u32[]{:S(2)}, u32[]{:S(2)}) collective-permute-start(bf16[16,128]{1,0:T(8,128)(2,1)} %pack_planes.1), channel_id=1, source_target_pairs={{0,752},{16,32},{32,16},{48,64},{64,48},{80,96},{96,80},{112,128},... | collective-permute-start | bytes 12296 | tf_op jit(solution)/shard_map/ppermute | solution.py:252
  16.6 2.1 %spread.1.whole_ref = bf16[16,304,128]{2,1,0:T(8,128)(2,1)} custom-call(bf16[288,128]{1,0:T(8,128)(2,1)} %bitcast.17), custom_call_target="tpu_custom_call" | custom-call | tf_op jit(solution)/shard_map/spread/pallas_call | solution.py:32
  18.6 0.0 collective-permute-done.near_ref
  18.7 0.0 copy-start.3
  18.7 1.1 %collective-permute-done.1.far_ref = bf16[16,128]{1,0:T(8,128)(2,1)S(1)} collective-permute-done((bf16[16,128]{1,0:T(8,128)(2,1)}, bf16[16,128]{1,0:T(8,128)(2,1)S(1)}, u32[]{:S(2)}, u32[]{:S(2)}) %collective-permute-start.1) | collective-permute-done | bytes 4128 | tf_op jit(solution)/shard_map/ppermute | solution.py:252
  19.8 0.6 copy-done.4
  20.3 1.3 %fill_edges.1 = bf16[16,304,128]{2,1,0:T(8,128)(2,1)} custom-call(s32[1]{0:T(128)} %bitcast.odd_ref, bf16[16,128]{1,0:T(8,128)(2,1)} %copy-done.3, bf16[16,128]{1,0:T(8,128)(2,1)} %copy-done.4, bf16[16,304,128]{2,1,0:T(8,128)(2,1)} %spread.1.whole_ref), custom_call_target="tpu_custom_call", output_to_operand_aliasing={{}: (3, {})} | custom-call | tf_op jit(solution)/shard_map/fill_edges/pallas_call | solution.py:97
  21.7 0.0 copy-start.1
  21.7 0.0 copy-start.2
  21.7 0.0 copy-start.5
  21.7 3.8 %all-to-all-start = ((bf16[16,304,128]{2,1,0:T(8,128)(2,1)}), bf16[16,304,128]{2,1,0:T(8,128)(2,1)S(1)}, u32[]{:S(2)}, u32[]{:S(2)}) async-start(bf16[16,304,128]{2,1,0:T(8,128)(2,1)} %fill_edges.1), calls=%async_computation | async-start | bytes 2490368 | tf_op jit(solution)/shard_map/all_to_all | solution.py:255
  25.6 0.0 copy-start
  25.6 1.9 %pack_state.1 = f32[64,128]{1,0:T(8,128)} custom-call(f32[4,16,16,128]{3,2,1,0:T(8,128)} %bitcast.14), custom_call_target="tpu_custom_call" | custom-call | tf_op jit(solution)/shard_map/pack_state/pallas_call | solution.py:53
  27.5 10.7 %collective-permute-start.2 = (f32[64,128]{1,0:T(8,128)}, f32[64,128]{1,0:T(8,128)S(1)}, u32[]{:S(2)}, u32[]{:S(2)}) collective-permute-start(f32[64,128]{1,0:T(8,128)} %pack_state.1), channel_id=1, source_target_pairs={{0,16},{16,0},{32,48},{48,32},{64,80},{80,64},{96,112},{112,96},{1... | collective-permute-start | bytes 98312 | tf_op jit(solution)/shard_map/ppermute | solution.py:260
  38.2 1.9 %collective-permute-start.3 = (f32[64,128]{1,0:T(8,128)}, f32[64,128]{1,0:T(8,128)S(1)}, u32[]{:S(2)}, u32[]{:S(2)}) collective-permute-start(f32[64,128]{1,0:T(8,128)} %pack_state.1), channel_id=1, source_target_pairs={{0,752},{16,32},{32,16},{48,64},{64,48},{80,96},{96,80},{112,128},... | collective-permute-start | bytes 98312 | tf_op jit(solution)/shard_map/ppermute | solution.py:259
  40.1 0.7 add_select_fusion
  40.8 0.0 collective-permute-done.2.near_ref
  40.8 9.0 %collective-permute-done.3.far_ref = f32[64,128]{1,0:T(8,128)S(1)} collective-permute-done((f32[64,128]{1,0:T(8,128)}, f32[64,128]{1,0:T(8,128)S(1)}, u32[]{:S(2)}, u32[]{:S(2)}) %collective-permute-start.3) | collective-permute-done | bytes 32800 | tf_op jit(solution)/shard_map/ppermute | solution.py:259
  49.8 6.1 %all-to-all-done.t_ref = bf16[16,304,128]{2,1,0:T(8,128)(2,1)S(1)} async-done(((bf16[16,304,128]{2,1,0:T(8,128)(2,1)}), bf16[16,304,128]{2,1,0:T(8,128)(2,1)S(1)}, u32[]{:S(2)}, u32[]{:S(2)}) %all-to-all-start) | async-done | bytes 1245216 | tf_op jit(solution)/shard_map/all_to_all | solution.py:255
  55.9 11.0 %advance_and_pick.1 = (f32[4,16,16,128]{3,2,1,0:T(8,128)}, f32[48,4,128]{2,1,0:T(4,128)}) custom-call(s32[1]{0:T(128)} %bitcast.odd_ref, f32[4,16,16,128]{3,2,1,0:T(8,128)} %bitcast.15, bf16[16,304,128]{2,1,0:T(8,128)(2,1)S(1)} %all-to-all-done.t_ref, f32[64,128]{1,0:T(8,128)S(1)} %collective-permute-done.2.near_ref, ...), custom_call_target="tpu_custom_call" | custom-call | tf_op jit(solution)/shard_map/advance_and_pick/pallas_call | solution.py:225
  66.9 30.1 %all_to_all.10 = f32[48,4,128]{2,1,0:T(4,128)S(1)} all-to-all(f32[48,4,128]{2,1,0:T(4,128)} %get-tuple-element.7), channel_id=1, replica_groups=mesh['space'=48,'member'=16] {'space'}, dimensions={0} | all-to-all | bytes 196608 | tf_op jit(solution)/shard_map/all_to_all | solution.py:269
  97.0 0.7 fusion
  (6 shorter events, 0.0 us)
Async XLA Ops:
  2.2 16.5 %collective-permute-start = (bf16[16,128]{1,0:T(8,128)(2,1)}, bf16[16,128]{1,0:T(8,128)(2,1)S(1)}, u32[]{:S(2)}, u32[]{:S(2)}) collective-permute-start(bf16[16,128]{1,0:T(8,128)(2,1)} %pack_planes.1), channel_id=1, source_target_pairs={{0,16},{16,0},{32,48},{48,32},{64,80},{80,64},{96,112},{112,96},{1... | collective-permute-start | bytes 12296 | tf_op jit(solution)/shard_map/ppermute | solution.py:253
  14.6 5.1 %collective-permute-start.1 = (bf16[16,128]{1,0:T(8,128)(2,1)}, bf16[16,128]{1,0:T(8,128)(2,1)S(1)}, u32[]{:S(2)}, u32[]{:S(2)}) collective-permute-start(bf16[16,128]{1,0:T(8,128)(2,1)} %pack_planes.1), channel_id=1, source_target_pairs={{0,752},{16,32},{32,16},{48,64},{64,48},{80,96},{96,80},{112,128},... | collective-permute-start | bytes 12296 | tf_op jit(solution)/shard_map/ppermute | solution.py:252
  18.7 1.1 %copy-start.3 = (bf16[16,128]{1,0:T(8,128)(2,1)}, bf16[16,128]{1,0:T(8,128)(2,1)S(1)}, u32[]{:S(2)}) copy-start(bf16[16,128]{1,0:T(8,128)(2,1)S(1)} %collective-permute-done.near_ref) | copy-start | bytes 12292
  19.7 0.6 copy-start.4
  21.7 18.4 %copy-start.1 = (s32[48,1,128]{2,1,0:T(1,128)S(1)}, s32[48,1,128]{2,1,0:T(1,128)}, u32[]{:S(2)}) copy-start(s32[48,1,128]{2,1,0:T(1,128)} %param.8) | copy-start | bytes 73732
  21.7 18.4 %copy-start.2 = (s32[48,1,128]{2,1,0:T(1,128)S(1)}, s32[48,1,128]{2,1,0:T(1,128)}, u32[]{:S(2)}) copy-start(s32[48,1,128]{2,1,0:T(1,128)} %param.9) | copy-start | bytes 73732
  21.7 18.4 %copy-start.5 = (s32[48,1]{0,1:T(1,128)S(1)}, s32[48,1]{0,1:T(1,128)}, u32[]{:S(2)}) copy-start(s32[48,1]{0,1:T(1,128)} %param.10) | copy-start | bytes 580
  21.7 34.1 %all-to-all-start = ((bf16[16,304,128]{2,1,0:T(8,128)(2,1)}), bf16[16,304,128]{2,1,0:T(8,128)(2,1)S(1)}, u32[]{:S(2)}, u32[]{:S(2)}) async-start(bf16[16,304,128]{2,1,0:T(8,128)(2,1)} %fill_edges.1), calls=%async_computation | async-start | bytes 2490368 | tf_op jit(solution)/shard_map/all_to_all | solution.py:255
  25.6 71.5 %copy-start = (f32[1,48,4,128]{3,2,1,0:T(4,128)S(1)}, f32[1,48,4,128]{3,2,1,0:T(4,128)}, u32[]{:S(2)}) copy-start(f32[1,48,4,128]{3,2,1,0:T(4,128)} %param.11) | copy-start | bytes 294916
  27.5 13.3 %collective-permute-start.2 = (f32[64,128]{1,0:T(8,128)}, f32[64,128]{1,0:T(8,128)S(1)}, u32[]{:S(2)}, u32[]{:S(2)}) collective-permute-start(f32[64,128]{1,0:T(8,128)} %pack_state.1), channel_id=1, source_target_pairs={{0,16},{16,0},{32,48},{48,32},{64,80},{80,64},{96,112},{112,96},{1... | collective-permute-start | bytes 98312 | tf_op jit(solution)/shard_map/ppermute | solution.py:260
  38.2 11.6 %collective-permute-start.3 = (f32[64,128]{1,0:T(8,128)}, f32[64,128]{1,0:T(8,128)S(1)}, u32[]{:S(2)}, u32[]{:S(2)}) collective-permute-start(f32[64,128]{1,0:T(8,128)} %pack_state.1), channel_id=1, source_target_pairs={{0,752},{16,32},{32,16},{48,64},{64,48},{80,96},{96,80},{112,128},... | collective-permute-start | bytes 98312 | tf_op jit(solution)/shard_map/ppermute | solution.py:259

commit v3 on v0

v3 whole, which is shorter than its diff:
```python
import functools

import jax
import jax.numpy as jnp
import numpy as np
from jax import lax
from jax.experimental import pallas as pl
from jax.experimental.pallas import tpu as pltpu
from jax.sharding import Mesh
from jax.sharding import PartitionSpec as P

F32 = jnp.float32
BF16 = jnp.bfloat16
VMEM = pl.BlockSpec(memory_space=pltpu.VMEM)
SMEM = pl.BlockSpec(memory_space=pltpu.SMEM)
HBM = pl.BlockSpec(memory_space=pltpu.HBM)
TILE = (16, 128)


def lane_of(shape):
    return lax.broadcasted_iota(jnp.int32, shape, len(shape) - 1)


def pack_kernel(pos_ref, p_ref, t_ref, edge_ref, copies_ref, s1_ref, s2_ref, s3_ref, copy_sems, send_sems):
    x = pos_ref[1]
    moves = []
    for i in range(copies_ref.shape[0]):
        moves.append(pltpu.make_async_copy(t_ref, copies_ref.at[i, pl.ds(0, 288)], copy_sems.at[i]))
    for k, send in enumerate((s1_ref, s2_ref, s3_ref)):
        peer = lax.rem(x + k + 1, 4)
        for f in range(4):
            moves.append(
                pltpu.make_async_copy(p_ref.at[f, :, peer], send.at[pl.ds(4 * f, 4)], send_sems.at[k, f])
            )
    for move in moves:
        move.start()
    group = lane_of(TILE) // 8
    for x_of in range(4):
        packed = jnp.zeros(TILE, F32)
        for g in range(16):
            moved = pltpu.roll(p_ref[g // 4, g % 4, x_of], (g * 8 + 3) % 128, 1)
            packed = jnp.where(group == g, moved, packed)
        edge_ref[x_of * 16 : x_of * 16 + 16, :] = packed
    packed = jnp.zeros(TILE, F32)
    for k in range(12):
        moved = pltpu.roll(t_ref[k * 16 : k * 16 + 16, :].astype(F32), (k * 8 + 3) % 128, 1)
        packed = jnp.where(group == k, moved, packed)
    edge_ref[64:80, :] = packed
    for move in moves:
        move.wait()


def pack(pos, state, planes):
    send = jax.ShapeDtypeStruct((17,) + TILE, F32)
    return pl.pallas_call(
        pack_kernel,
        out_shape=(
            jax.ShapeDtypeStruct((80, 128), F32),
            jax.ShapeDtypeStruct((4, 304, 128), BF16),
            send,
            send,
            send,
        ),
        in_specs=[SMEM, VMEM, VMEM],
        out_specs=(VMEM, HBM, HBM, HBM, HBM),
        scratch_shapes=[pltpu.SemaphoreType.DMA((4,)), pltpu.SemaphoreType.DMA((3, 4))],
        name="pack",
    )(pos, state, planes)


def fill_kernel(
    pos_ref, near_ref, far_ref, c_in, s1_in, s2_in, s3_in, own_ref, c_ref, s1_ref, s2_ref, s3_ref, all_ref, side_ref, sems
):
    odd, x = pos_ref[0], pos_ref[1]
    from_near = (lane_of((80, 128)) % 8 < 3) == (odd == 1)
    edge = jnp.where(from_near, near_ref[...], far_ref[...])
    for i in range(4):
        all_ref[i] = edge[i * 16 : i * 16 + 16]
        side_ref[i] = edge[64:80].astype(BF16)
    moves = [pltpu.make_async_copy(side_ref, c_ref.at[:, pl.ds(288, 16)], sems.at[0])]
    for k, send in enumerate((s1_ref, s2_ref, s3_ref)):
        moves.append(pltpu.make_async_copy(all_ref.at[lax.rem(x + k + 1, 4)], send.at[16], sems.at[k + 1]))
    for move in moves:
        move.start()
    own_ref[...] = all_ref[x]
    for move in moves:
        move.wait()


def fill(pos, near, far, copies, sends):
    send = jax.ShapeDtypeStruct((17,) + TILE, F32)
    near = pltpu.with_memory_space_constraint(near, pltpu.VMEM)
    far = pltpu.with_memory_space_constraint(far, pltpu.VMEM)
    return pl.pallas_call(
        fill_kernel,
        out_shape=(jax.ShapeDtypeStruct(TILE, F32), jax.ShapeDtypeStruct(copies.shape, BF16), send, send, send),
        in_specs=[SMEM, VMEM, VMEM, HBM, HBM, HBM, HBM],
        out_specs=(VMEM, HBM, HBM, HBM, HBM),
        scratch_shapes=[
            pltpu.VMEM((4,) + TILE, F32),
            pltpu.VMEM((4,) + TILE, BF16),
            pltpu.SemaphoreType.DMA((4,)),
        ],
        input_output_aliases={3: 1, 4: 2, 5: 3, 6: 4},
        name="fill",
    )(pos, near, far, copies, *sends)


def weights_of(planes, first, last):
    a, b = planes[0], planes[1]
    aa, bb = a * a, b * b
    return [
        1.0 - aa - bb,
        0.5 * (aa - a),
        0.5 * (aa + a),
        jnp.where(last, 0.0, 0.5 * (bb - b)),
        jnp.where(first, 0.0, 0.5 * (bb + b)),
    ] + planes[2:]


def apply_stencil(w_ref, k, p, east, west):
    new = []
    for f in range(4):
        north, south = pltpu.roll(p[f], 15, 0), pltpu.roll(p[f], 1, 0)
        new.append(
            (w_ref[k, 0] * p[f] + w_ref[k, 1] * east[f])
            + (w_ref[k, 2] * west[f] + (w_ref[k, 3] * north + w_ref[k, 4] * south))
        )
    new[2] = new[2] - (w_ref[k, 5] * p[0] + w_ref[k, 6] * p[1])
    new[3] = new[3] - (w_ref[k, 7] * p[0] + w_ref[k, 8] * p[1])
    return new


def advance_kernel(pos_ref, p_ref, own_ref, r1_ref, r2_ref, r3_ref, t_ref, out_ref, w_ref, h_ref):
    x = pos_ref[1]
    lane = lane_of(TILE)
    row = lax.broadcasted_iota(jnp.int32, TILE, 0)
    lane_first, lane_last = lane == 0, lane == 127
    row_first, row_last = row == 0, row == 15

    def one_level(y, carry):
        side = t_ref[y, 288:304, :].astype(F32)
        for k in range(3):
            planes = [t_ref[y, (k * 6 + q) * 16 : (k * 6 + q + 1) * 16, :].astype(F32) for q in range(6)]
            for i, weight in enumerate(weights_of(planes, row_first, row_last)):
                w_ref[k, i] = weight
            if k < 2:
                planes = [pltpu.roll(side, (125 - (k * 6 + q) * 8) % 128, 1) for q in range(6)]
                for i, weight in enumerate(weights_of(planes, row_first, row_last)):
                    h_ref[k, i] = weight
        for m, source in enumerate((None, r1_ref, r2_ref, r3_ref)):
            if source is None:
                state = [p_ref[f, y, x] for f in range(4)]
                edge = own_ref[...]
            else:
                state = [source[4 * f + y] for f in range(4)]
                edge = source[16]
            halo = [pltpu.roll(edge, lax.rem(253 - (4 * f + y) * 8, 128), 1) for f in range(4)]
            for k in range(3):
                east = [pltpu.roll(v, 127, 1) for v in state]
                west = [pltpu.roll(v, 1, 1) for v in state]
                halo_east = [pltpu.roll(v, 127, 1) for v in halo]
                halo_west = [pltpu.roll(v, 1, 1) for v in halo]
                new = apply_stencil(
                    w_ref,
                    k,
                    state,
                    [jnp.where(lane_last, h, v) for v, h in zip(east, halo_east)],
                    [jnp.where(lane_first, h, v) for v, h in zip(west, halo_west)],
                )
                if k < 2:
                    halo = apply_stencil(
                        h_ref,
                        k,
                        halo,
                        [jnp.where(lane_last, v, h) for v, h in zip(east, halo_east)],
                        [jnp.where(lane_first, v, h) for v, h in zip(west, halo_west)],
                    )
                state = new
            for f in range(4):
                out_ref[lax.rem(x + 4 - m, 4), f, y] = state[f]
        return carry

    lax.fori_loop(0, 4, one_level, 0)


def advance(pos, state, own, received, planes):
    received = [pltpu.with_memory_space_constraint(r, pltpu.VMEM) for r in received]
    planes = pltpu.with_memory_space_constraint(planes, pltpu.VMEM)
    return pl.pallas_call(
        advance_kernel,
        out_shape=jax.ShapeDtypeStruct((4, 4, 4) + TILE, F32),
        in_specs=[SMEM] + [VMEM] * 6,
        out_specs=VMEM,
        scratch_shapes=[pltpu.VMEM((3, 9) + TILE, F32), pltpu.VMEM((2, 9) + TILE, F32)],
        name="advance",
    )(pos, state, own, *received, planes)


def pick_kernel(b_ref, row_ref, col_ref, out_ref, val_ref, high_ref, low_ref, sems):
    owners = row_ref.shape[0]
    moves = [pltpu.make_async_copy(b_ref.at[x], out_ref.at[:, :, x], sems.at[x]) for x in range(4)]
    for move in moves:
        move.start()
    for f in range(4):
        for half in range(2):
            block = jnp.concatenate(
                [b_ref[2 * half, f].reshape(64, 128), b_ref[2 * half + 1, f].reshape(64, 128)], axis=0
            )
            block = jnp.transpose(block)
            high = block.astype(BF16)
            low = (block - high.astype(F32)).astype(BF16)
            high_ref[f * 128 : f * 128 + 128, half * 128 : half * 128 + 128] = high
            low_ref[f * 128 : f * 128 + 128, half * 128 : half * 128 + 128] = low

    line = lax.broadcasted_iota(jnp.int32, (256, 128), 0)
    lon = lax.broadcasted_iota(jnp.int32, (128, 128), 0)

    def two_owners(i, carry):
        picks = []
        for o in range(2):
            hit = line == row_ref[pl.ds(2 * i + o, 1), :]
            picks.append(jnp.where(hit, 1.0, 0.0).astype(BF16))
        pick = jnp.concatenate(picks, axis=1)
        lines = jnp.dot(high_ref[...], pick, preferred_element_type=F32)
        lines = lines + jnp.dot(low_ref[...], pick, preferred_element_type=F32)
        for o in range(2):
            hit = lon == col_ref[pl.ds(2 * i + o, 1), :]
            for f in range(4):
                part = lines[f * 128 : f * 128 + 128, o * 128 : o * 128 + 128]
                val_ref[2 * i + o, f : f + 1, :] = jnp.sum(jnp.where(hit, part, 0.0), axis=0, keepdims=True)
        return carry

    lax.fori_loop(0, owners // 2, two_owners, 0, unroll=2)
    for move in moves:
        move.wait()


def pick(blocks, rows, cols):
    owners = rows.shape[0]
    blocks = pltpu.with_memory_space_constraint(blocks, pltpu.VMEM)
    return pl.pallas_call(
        pick_kernel,
        out_shape=(
            jax.ShapeDtypeStruct((4, 4, 4) + TILE, F32),
            jax.ShapeDtypeStruct((owners, 4, 128), F32),
        ),
        in_specs=[VMEM] * 3,
        out_specs=(HBM, VMEM),
        scratch_shapes=[
            pltpu.VMEM((512, 256), BF16),
            pltpu.VMEM((512, 256), BF16),
            pltpu.SemaphoreType.DMA((4,)),
        ],
        name="pick",
    )(blocks, rows, cols)


def on_device(perturbation, trajectory, site_col, site_lev, obs_counts, obs_weights):
    tiles, slots = site_col.shape[0], site_col.shape[2]
    state = perturbation.reshape((4, 4, 4) + TILE)
    local = trajectory.reshape(288, 128)
    pos = jnp.stack([lax.axis_index("space") % 2, lax.axis_index("x")]).astype(jnp.int32)
    pairs = [(i, i ^ 1) for i in range(tiles)]
    crossed = [(i, (i + 1) % tiles if i % 2 else (i - 1) % tiles) for i in range(tiles)]

    edge, copies, *sends = pack(pos, state, local)
    far = lax.ppermute(edge, "space", crossed)
    near = lax.ppermute(edge, "space", pairs)
    own, copies, *sends = fill(pos, near, far, copies, sends)
    planes = lax.all_to_all(copies, "yhi", 0, 0, tiled=True)
    received = [
        lax.ppermute(send, "x", [(i, (i + k + 1) % 4) for i in range(4)]) for k, send in enumerate(sends)
    ]
    blocks = advance(pos, state, own, received, planes)
    blocks = lax.all_to_all(blocks, "x", 0, 0, tiled=True)

    live = jnp.arange(slots, dtype=jnp.int32)[None, :] < obs_counts
    level, col = site_lev[:, 0, :], site_col[:, 0, :]
    rows = jnp.where(live, (level % 4) * 64 + (level // 4) * 16 + col // 128, -1)
    final, values = pick(blocks, rows, col % 128)
    received = lax.all_to_all(values, "space", 0, 0, tiled=True)
    summed = jnp.sum(obs_weights[0] * received, axis=1)
    return (final.reshape(perturbation.shape), summed.reshape(1, 1, tiles, slots))


def solution(mesh):
    member = ("yhi", "x")
    fine = Mesh(np.asarray(mesh.devices).reshape(mesh.shape["space"], 4, 4), ("space",) + member)
    in_specs = (
        P(member, None, None, None, "space"),
        P(None, member, None, None, "space"),
        P(None, "space", None),
        P(None, "space", None),
        P(None, "space"),
        P("space", None, None, None),
    )
    out_specs = (P(member, None, None, None, "space"), P(member, "space", None, None))
    return jax.shard_map(
        on_device, mesh=fine, in_specs=in_specs, out_specs=out_specs, check_vma=False
    )
```

time: 192 us -> 94.3 us (0.49)
  waiting for transfers between devices: 92.4 us -> 12.4 us
  local copies, waits for them, and re-layouts: 37.3 us -> 0.66 us
  blocking collectives: 0 us -> 30.2 us
  Pallas kernels: 0 us -> 17.6 us
  between operations: 14.3 us -> 0.83 us
  other arithmetic: 11 us -> 2 us
  starting transfers between devices: 35.8 us -> 30 us
    all_gather x1 -> x0, waiting for transfers between devices: 57.4 us -> none  [on_device(): gathered = lax.all_gather(trajectory, 'member', axis=1, tiled=True)]
    all_to_all x0 -> x1, blocking collectives: none -> 30.2 us  [on_device(): received = lax.all_to_all(values, 'space', 0, 0, tiled=True)]
    gather x2 -> x0, local copies, waits for them, and re-layouts: 26.6 us -> none  [on_device(): picked = jnp.take(flat, index.reshape(-1), axis=1).reshape(4, tiles, slots)]
    pallas_call x0 -> x4, Pallas kernels: none -> 17.6 us  [the longest x1 7.31 us: pick(): pl.pallas_call(pick_kernel, out_shape=(jax.ShapeDtypeStruct((4, 4, 4) + T...]
    ppermute x6 -> x5, waiting for transfers between devices: 23.9 us -> 6.88 us  [the longest x1 3.59 us: on_device(): far = lax.ppermute(edge, 'space', crossed)]
    another operation x2 -> x0, local copies, waits for them, and re-layouts: 8.63 us -> none  [update(): return jnp.stack([fresh[:, 0], fresh[:, 1], temper, humid], axis=1)]
    all_to_all x1 -> x2, waiting for transfers between devices: 10.3 us -> 5.57 us  [the longest x1 5.56 us: on_device(): blocks = lax.all_to_all(blocks, 'x', 0, 0, tiled=True)]
    all_to_all x1 -> x2, starting transfers between devices: 10.6 us -> 7.2 us  [the longest x1 3.6 us: on_device(): blocks = lax.all_to_all(blocks, 'x', 0, 0, tiled=True)]
  transfers between devices with their start and end apart: 8 -> 7, of which waited for: 6 -> 4; matrix products, arithmetic and copies ran while one was open for 4% -> 1% of each run, Pallas kernels for 0% -> 0%
where the time goes in v3:
time: 94.3 us; the launch traced here: 93.6 us
  blocking collectives  30.2 us (32%)
  starting transfers between devices  30 us (32%)
  Pallas kernels  17.6 us (19%)
  waiting for transfers between devices  12.4 us (13%)
  other arithmetic  2 us (2%)
    all_to_all x1, blocking collectives, on_device(): received = lax.all_to_all(values, 'space', 0, 0, tiled=True)  30.2 us
    ppermute x1, starting transfers between devices, on_device(): near = lax.ppermute(edge, 'space', pairs)  12.4 us
    ppermute x3, starting transfers between devices, on_device(): lax.ppermute(send, 'x', [(i, (i + k + 1) % 4) for i in range(4)])  8.41 us
    pallas_call x1, Pallas kernels, pick(): pl.pallas_call(pick_kernel, out_shape=(jax.ShapeDtypeStruct((4, 4, 4) + T...  7.31 us
    pallas_call x1, Pallas kernels, advance(): pl.pallas_call(advance_kernel, out_shape=jax.ShapeDtypeStruct((4, 4, 4) +...  5.6 us
    all_to_all x1, waiting for transfers between devices, on_device(): blocks = lax.all_to_all(blocks, 'x', 0, 0, tiled=True)  5.56 us
    all_to_all x1, starting transfers between devices, on_device(): blocks = lax.all_to_all(blocks, 'x', 0, 0, tiled=True)  3.6 us
    all_to_all x1, starting transfers between devices, on_device(): planes = lax.all_to_all(copies, 'yhi', 0, 0, tiled=True)  3.6 us
  transfers between devices with their start and end apart: 7, of which 4 were waited for; matrix products, arithmetic and copies ran while one was open for 1% of the time, Pallas kernels for 0%

profile of v3, /device:TPU:1, one launch (start us, length us, event | category | flops | bytes accessed | tf_op | source)
XLA Modules:
  0.0 93.6 jit_solution(15275120125503450960)
XLA Ops:
  0.6 0.6 pad_add_fusion.pos_ref
  1.3 2.7 %pack.1 = (f32[80,128]{1,0:T(8,128)}, bf16[4,304,128]{2,1,0:T(8,128)(2,1)}, f32[17,16,128]{2,1,0:T(8,128)}, f32[17,16,128]{2,1,0:T(8,128)}, f32[17,16,128]{2,1,0:T(8,128)}) custom-call(s32[2]{0:T(128)} %pad_add_fusion.pos_ref, f32[4,4,4,16,128]{4,3,2,1,0:T(8,128)} %bitcast.13, bf16[288,128]{1,0:T(8,128)(2,1)} %bitcast.15), custom_call_target="tpu_custom_call" | custom-call | tf_op jit(solution)/shard_map/pack/pallas_call | solution.py:55
  4.0 12.4 %collective-permute-start = (f32[80,128]{1,0:T(8,128)}, f32[80,128]{1,0:T(8,128)S(1)}, u32[]{:S(2)}, u32[]{:S(2)}) collective-permute-start(f32[80,128]{1,0:T(8,128)} %get-tuple-element.14), channel_id=1, source_target_pairs={{0,16},{16,0},{32,48},{48,32},{64,80},{80,64},{96,112},{112,96},{1... | collective-permute-start | bytes 122888 | tf_op jit(solution)/shard_map/ppermute | solution.py:269
  16.5 1.9 %collective-permute-start.1 = (f32[80,128]{1,0:T(8,128)}, f32[80,128]{1,0:T(8,128)S(1)}, u32[]{:S(2)}, u32[]{:S(2)}) collective-permute-start(f32[80,128]{1,0:T(8,128)} %get-tuple-element.14), channel_id=1, source_target_pairs={{0,752},{16,32},{32,16},{48,64},{64,48},{80,96},{96,80},{112,128},... | collective-permute-start | bytes 122888 | tf_op jit(solution)/shard_map/ppermute | solution.py:268
  18.4 0.0 collective-permute-done.near_ref
  18.4 3.6 %collective-permute-done.1.far_ref = f32[80,128]{1,0:T(8,128)S(1)} collective-permute-done((f32[80,128]{1,0:T(8,128)}, f32[80,128]{1,0:T(8,128)S(1)}, u32[]{:S(2)}, u32[]{:S(2)}) %collective-permute-start.1) | collective-permute-done | bytes 40992 | tf_op jit(solution)/shard_map/ppermute | solution.py:268
  22.0 1.9 %fill.1 = (f32[16,128]{1,0:T(8,128)}, bf16[4,304,128]{2,1,0:T(8,128)(2,1)}, f32[17,16,128]{2,1,0:T(8,128)}, f32[17,16,128]{2,1,0:T(8,128)}, f32[17,16,128]{2,1,0:T(8,128)}) custom-call(s32[2]{0:T(128)} %pad_add_fusion.pos_ref, f32[80,128]{1,0:T(8,128)S(1)} %collective-permute-done.near_ref, ...), custom_call_target="tpu_custom_call", output_to_operand_aliasing={{1}: (3, {}), {2}: (4, {}), {3}: (5, {}), {4}: (6, {})} | custom-call | tf_op jit(solution)/shard_map/fill/pallas_call | solution.py:94
  24.0 3.6 %all-to-all-start = ((bf16[4,304,128]{2,1,0:T(8,128)(2,1)}), bf16[4,304,128]{2,1,0:T(8,128)(2,1)S(1)}, u32[]{:S(2)}, u32[]{:S(2)}) async-start(bf16[4,304,128]{2,1,0:T(8,128)(2,1)} %get-tuple-element.23), calls=%async_computation | async-start | bytes 622592 | tf_op jit(solution)/shard_map/all_to_all | solution.py:271
  27.6 1.9 %collective-permute-start.2 = (f32[17,16,128]{2,1,0:T(8,128)S(1)}, f32[17,16,128]{2,1,0:T(8,128)S(1)}, u32[]{:S(2)}, u32[]{:S(2)}) collective-permute-start(f32[17,16,128]{2,1,0:T(8,128)S(1)} %copy-done), channel_id=1, source_target_pairs={{0,1},{1,2},{2,3},{3,0},{4,5},{5,6},{6,7},{7,4},{8,9},{9,10},{10,1... | collective-permute-start | bytes 417800 | tf_op jit(solution)/shard_map/ppermute | solution.py:273
  29.5 1.9 %collective-permute-start.3 = (f32[17,16,128]{2,1,0:T(8,128)S(1)}, f32[17,16,128]{2,1,0:T(8,128)S(1)}, u32[]{:S(2)}, u32[]{:S(2)}) collective-permute-start(f32[17,16,128]{2,1,0:T(8,128)S(1)} %copy-done.1), channel_id=1, source_target_pairs={{0,2},{1,3},{2,0},{3,1},{4,6},{5,7},{6,4},{7,5},{8,10},{9,11},{10,... | collective-permute-start | bytes 417800 | tf_op jit(solution)/shard_map/ppermute | solution.py:273
  31.4 4.6 %collective-permute-start.4 = (f32[17,16,128]{2,1,0:T(8,128)S(1)}, f32[17,16,128]{2,1,0:T(8,128)S(1)}, u32[]{:S(2)}, u32[]{:S(2)}) collective-permute-start(f32[17,16,128]{2,1,0:T(8,128)S(1)} %copy-done.2), channel_id=1, source_target_pairs={{0,3},{1,0},{2,1},{3,2},{4,7},{5,4},{6,5},{7,6},{8,11},{9,8},{10,9... | collective-permute-start | bytes 417800 | tf_op jit(solution)/shard_map/ppermute | solution.py:273
  36.0 0.0 collective-permute-done.2.r1_ref
  36.0 0.8 collective-permute-done.3.r2_ref
  36.8 2.5 %collective-permute-done.4.r3_ref = f32[17,16,128]{2,1,0:T(8,128)S(1)} collective-permute-done((f32[17,16,128]{2,1,0:T(8,128)S(1)}, f32[17,16,128]{2,1,0:T(8,128)S(1)}, u32[]{:S(2)}, u32[]{:S(2)}) %collective-permute-start.4) | collective-permute-done | bytes 139296 | tf_op jit(solution)/shard_map/ppermute | solution.py:273
  39.3 5.6 %advance.1 = f32[4,4,4,16,128]{4,3,2,1,0:T(8,128)} custom-call(s32[2]{0:T(128)} %pad_add_fusion.pos_ref, f32[4,4,4,16,128]{4,3,2,1,0:T(8,128)} %bitcast.14, f32[16,128]{1,0:T(8,128)} %get-tuple-element.19.own_ref, f32[17,16,128]{2,1,0:T(8,128)S(1)} %collective-permute-done.2.r1_ref, f32[17,16,128]{2,1,0:T(8,128)S(1)} %collective-permute-done.3.r2_ref, ...), custom_call_target="tpu_custom_call" | custom-call | tf_op jit(solution)/shard_map/advance/pallas_call | solution.py:190
  44.9 3.6 %all-to-all-start.1 = ((f32[4,4,4,16,128]{4,3,2,1,0:T(8,128)}), f32[4,4,4,16,128]{4,3,2,1,0:T(8,128)S(1)}, u32[]{:S(2)}, u32[]{:S(2)}) async-start(f32[4,4,4,16,128]{4,3,2,1,0:T(8,128)} %advance.1), calls=%async_computation.1 | async-start | bytes 1048576 | tf_op jit(solution)/shard_map/all_to_all | solution.py:276
  48.5 0.0 copy-start.6
  48.6 0.6 copy-done.6
  49.2 0.7 add_select_fusion
  49.9 5.6 %all-to-all-done.1.b_ref = f32[4,4,4,16,128]{4,3,2,1,0:T(8,128)S(1)} async-done(((f32[4,4,4,16,128]{4,3,2,1,0:T(8,128)}), f32[4,4,4,16,128]{4,3,2,1,0:T(8,128)S(1)}, u32[]{:S(2)}, u32[]{:S(2)}) %all-to-all-start.1) | async-done | bytes 524320 | tf_op jit(solution)/shard_map/all_to_all | solution.py:276
  55.4 7.3 %pick.1 = (f32[4,4,4,16,128]{4,3,2,1,0:T(8,128)}, f32[48,4,128]{2,1,0:T(4,128)}) custom-call(f32[4,4,4,16,128]{4,3,2,1,0:T(8,128)S(1)} %all-to-all-done.1.b_ref, s32[48,128]{1,0:T(8,128)} %get-tuple-element.27.row_ref, s32[48,128]{1,0:T(8,128)} %get-tuple-element.26.col_ref), custom_call_target="tpu_custom_call" | custom-call | tf_op jit(solution)/shard_map/pick/pallas_call | solution.py:242
  62.8 0.0 copy-start.3
  62.8 30.2 %all_to_all.15 = f32[48,4,128]{2,1,0:T(4,128)S(1)} all-to-all(f32[48,4,128]{2,1,0:T(4,128)} %get-tuple-element.25), channel_id=1, replica_groups=mesh['space'=48,'yhi'=4,'x'=4] {'space'}, dimensions={0} | all-to-all | bytes 196608 | tf_op jit(solution)/shard_map/all_to_all | solution.py:282
  93.0 0.7 fusion
  (12 shorter events, 0.0 us)
Async XLA Ops:
  4.0 14.4 %collective-permute-start = (f32[80,128]{1,0:T(8,128)}, f32[80,128]{1,0:T(8,128)S(1)}, u32[]{:S(2)}, u32[]{:S(2)}) collective-permute-start(f32[80,128]{1,0:T(8,128)} %get-tuple-element.14), channel_id=1, source_target_pairs={{0,16},{16,0},{32,48},{48,32},{64,80},{80,64},{96,112},{112,96},{1... | collective-permute-start | bytes 122888 | tf_op jit(solution)/shard_map/ppermute | solution.py:269
  16.5 5.5 %collective-permute-start.1 = (f32[80,128]{1,0:T(8,128)}, f32[80,128]{1,0:T(8,128)S(1)}, u32[]{:S(2)}, u32[]{:S(2)}) collective-permute-start(f32[80,128]{1,0:T(8,128)} %get-tuple-element.14), channel_id=1, source_target_pairs={{0,752},{16,32},{32,16},{48,64},{64,48},{80,96},{96,80},{112,128},... | collective-permute-start | bytes 122888 | tf_op jit(solution)/shard_map/ppermute | solution.py:268
  23.9 3.6 %copy-start = (f32[17,16,128]{2,1,0:T(8,128)S(1)}, f32[17,16,128]{2,1,0:T(8,128)}, u32[]{:S(2)}) copy-start(f32[17,16,128]{2,1,0:T(8,128)} %get-tuple-element.20) | copy-start | bytes 417796
  23.9 5.6 %copy-start.1 = (f32[17,16,128]{2,1,0:T(8,128)S(1)}, f32[17,16,128]{2,1,0:T(8,128)}, u32[]{:S(2)}) copy-start(f32[17,16,128]{2,1,0:T(8,128)} %get-tuple-element.21) | copy-start | bytes 417796
  23.9 7.5 %copy-start.2 = (f32[17,16,128]{2,1,0:T(8,128)S(1)}, f32[17,16,128]{2,1,0:T(8,128)}, u32[]{:S(2)}) copy-start(f32[17,16,128]{2,1,0:T(8,128)} %get-tuple-element.22) | copy-start | bytes 417796
  24.0 15.4 %all-to-all-start = ((bf16[4,304,128]{2,1,0:T(8,128)(2,1)}), bf16[4,304,128]{2,1,0:T(8,128)(2,1)S(1)}, u32[]{:S(2)}, u32[]{:S(2)}) async-start(bf16[4,304,128]{2,1,0:T(8,128)(2,1)} %get-tuple-element.23), calls=%async_computation | async-start | bytes 622592 | tf_op jit(solution)/shard_map/all_to_all | solution.py:271
  27.6 8.5 %collective-permute-start.2 = (f32[17,16,128]{2,1,0:T(8,128)S(1)}, f32[17,16,128]{2,1,0:T(8,128)S(1)}, u32[]{:S(2)}, u32[]{:S(2)}) collective-permute-start(f32[17,16,128]{2,1,0:T(8,128)S(1)} %copy-done), channel_id=1, source_target_pairs={{0,1},{1,2},{2,3},{3,0},{4,5},{5,6},{6,7},{7,4},{8,9},{9,10},{10,1... | collective-permute-start | bytes 417800 | tf_op jit(solution)/shard_map/ppermute | solution.py:273
  29.5 7.3 %collective-permute-start.3 = (f32[17,16,128]{2,1,0:T(8,128)S(1)}, f32[17,16,128]{2,1,0:T(8,128)S(1)}, u32[]{:S(2)}, u32[]{:S(2)}) collective-permute-start(f32[17,16,128]{2,1,0:T(8,128)S(1)} %copy-done.1), channel_id=1, source_target_pairs={{0,2},{1,3},{2,0},{3,1},{4,6},{5,7},{6,4},{7,5},{8,10},{9,11},{10,... | collective-permute-start | bytes 417800 | tf_op jit(solution)/shard_map/ppermute | solution.py:273
  31.4 7.9 %collective-permute-start.4 = (f32[17,16,128]{2,1,0:T(8,128)S(1)}, f32[17,16,128]{2,1,0:T(8,128)S(1)}, u32[]{:S(2)}, u32[]{:S(2)}) collective-permute-start(f32[17,16,128]{2,1,0:T(8,128)S(1)} %copy-done.2), channel_id=1, source_target_pairs={{0,3},{1,0},{2,1},{3,2},{4,7},{5,4},{6,5},{7,6},{8,11},{9,8},{10,9... | collective-permute-start | bytes 417800 | tf_op jit(solution)/shard_map/ppermute | solution.py:273
  44.9 3.6 %copy-start.4 = (s32[48,1,128]{2,1,0:T(1,128)S(1)}, s32[48,1,128]{2,1,0:T(1,128)}, u32[]{:S(2)}) copy-start(s32[48,1,128]{2,1,0:T(1,128)} %param.8) | copy-start | bytes 73732
  44.9 3.6 %copy-start.5 = (s32[48,1,128]{2,1,0:T(1,128)S(1)}, s32[48,1,128]{2,1,0:T(1,128)}, u32[]{:S(2)}) copy-start(s32[48,1,128]{2,1,0:T(1,128)} %param.9) | copy-start | bytes 73732
  44.9 10.5 %all-to-all-start.1 = ((f32[4,4,4,16,128]{4,3,2,1,0:T(8,128)}), f32[4,4,4,16,128]{4,3,2,1,0:T(8,128)S(1)}, u32[]{:S(2)}, u32[]{:S(2)}) async-start(f32[4,4,4,16,128]{4,3,2,1,0:T(8,128)} %advance.1), calls=%async_computation.1 | async-start | bytes 1048576 | tf_op jit(solution)/shard_map/all_to_all | solution.py:276
  48.5 0.7 copy-start.6
  62.8 30.2 %copy-start.3 = (f32[1,48,4,128]{3,2,1,0:T(4,128)S(1)}, f32[1,48,4,128]{3,2,1,0:T(4,128)}, u32[]{:S(2)}) copy-start(f32[1,48,4,128]{3,2,1,0:T(4,128)} %param.11) | copy-start | bytes 294916

commit v4 on v3

--- a/solution.py
+++ b/solution.py
@@ -12,98 +12,97 @@
 F32 = jnp.float32
 BF16 = jnp.bfloat16
 VMEM = pl.BlockSpec(memory_space=pltpu.VMEM)
-SMEM = pl.BlockSpec(memory_space=pltpu.SMEM)
 HBM = pl.BlockSpec(memory_space=pltpu.HBM)
 TILE = (16, 128)
 
 
+axis_index = lax.axis_index
+
+
 def lane_of(shape):
     return lax.broadcasted_iota(jnp.int32, shape, len(shape) - 1)
 
 
-def pack_kernel(pos_ref, p_ref, t_ref, edge_ref, copies_ref, s1_ref, s2_ref, s3_ref, copy_sems, send_sems):
-    x = pos_ref[1]
-    moves = []
-    for i in range(copies_ref.shape[0]):
-        moves.append(pltpu.make_async_copy(t_ref, copies_ref.at[i, pl.ds(0, 288)], copy_sems.at[i]))
-    for k, send in enumerate((s1_ref, s2_ref, s3_ref)):
-        peer = lax.rem(x + k + 1, 4)
-        for f in range(4):
-            moves.append(
-                pltpu.make_async_copy(p_ref.at[f, :, peer], send.at[pl.ds(4 * f, 4)], send_sems.at[k, f])
-            )
+def send_kernel(p_ref, t_ref, blocks_ref, copies_ref, edge_ref, block_sems, copy_sems):
+    moves = [pltpu.make_async_copy(p_ref.at[:, :, x], blocks_ref.at[x], block_sems.at[x]) for x in range(4)]
+    moves += [
+        pltpu.make_async_copy(t_ref, copies_ref.at[i, pl.ds(0, 288)], copy_sems.at[i]) for i in range(4)
+    ]
     for move in moves:
         move.start()
     group = lane_of(TILE) // 8
-    for x_of in range(4):
-        packed = jnp.zeros(TILE, F32)
-        for g in range(16):
-            moved = pltpu.roll(p_ref[g // 4, g % 4, x_of], (g * 8 + 3) % 128, 1)
-            packed = jnp.where(group == g, moved, packed)
-        edge_ref[x_of * 16 : x_of * 16 + 16, :] = packed
     packed = jnp.zeros(TILE, F32)
     for k in range(12):
         moved = pltpu.roll(t_ref[k * 16 : k * 16 + 16, :].astype(F32), (k * 8 + 3) % 128, 1)
         packed = jnp.where(group == k, moved, packed)
-    edge_ref[64:80, :] = packed
+    edge_ref[...] = packed.astype(BF16)
     for move in moves:
         move.wait()
 
 
-def pack(pos, state, planes):
-    send = jax.ShapeDtypeStruct((17,) + TILE, F32)
+def send(state, planes):
+    return pl.pallas_call(
+        send_kernel,
+        out_shape=(
+            jax.ShapeDtypeStruct((4, 4, 4) + TILE, F32),
+            jax.ShapeDtypeStruct((4, 304, 128), BF16),
+            jax.ShapeDtypeStruct(TILE, BF16),
+        ),
+        in_specs=[HBM, VMEM],
+        out_specs=(HBM, HBM, VMEM),
+        scratch_shapes=[pltpu.SemaphoreType.DMA((4,)), pltpu.SemaphoreType.DMA((4,))],
+        name="send",
+    )(state, planes)
+
+
+def merge(near, far):
+    odd = axis_index("space") % 2
+    return jnp.where((lane_of(near.shape) % 8 < 3) == (odd == 1), near, far)
+
+
+def fill_kernel(near_ref, far_ref, c_in, c_ref, side_ref, sem):
+    edge = merge(near_ref[...].astype(F32), far_ref[...].astype(F32)).astype(BF16)
+    for i in range(4):
+        side_ref[i] = edge
+    move = pltpu.make_async_copy(side_ref, c_ref.at[:, pl.ds(288, 16)], sem)
+    move.start()
+    move.wait()
+
+
+def in_vmem(x):
+    return pltpu.with_memory_space_constraint(x, pltpu.VMEM)
+
+
+def fill(near, far, copies):
+    return pl.pallas_call(
+        fill_kernel,
+        out_shape=jax.ShapeDtypeStruct(copies.shape, BF16),
+        in_specs=[VMEM, VMEM, HBM],
+        out_specs=HBM,
+        scratch_shapes=[pltpu.VMEM((4,) + TILE, BF16), pltpu.SemaphoreType.DMA],
+        input_output_aliases={2: 0},
+        name="fill",
+    )(in_vmem(near), in_vmem(far), copies)
+
+
+def pack_kernel(p_ref, edge_ref):
+    group = lane_of(TILE) // 8
+    for m in range(4):
+        packed = jnp.zeros(TILE, F32)
+        for g in range(16):
+            moved = pltpu.roll(p_ref[m, g // 4, g % 4], (g * 8 + 3) % 128, 1)
+            packed = jnp.where(group == g, moved, packed)
+        edge_ref[m] = packed
+
+
+def pack(states):
     return pl.pallas_call(
         pack_kernel,
-        out_shape=(
-            jax.ShapeDtypeStruct((80, 128), F32),
-            jax.ShapeDtypeStruct((4, 304, 128), BF16),
-            send,
-            send,
-            send,
-        ),
-        in_specs=[SMEM, VMEM, VMEM],
-        out_specs=(VMEM, HBM, HBM, HBM, HBM),
-        scratch_shapes=[pltpu.SemaphoreType.DMA((4,)), pltpu.SemaphoreType.DMA((3, 4))],
+        out_shape=jax.ShapeDtypeStruct((4,) + TILE, F32),
+        in_specs=[VMEM],
+        out_specs=VMEM,
         name="pack",
-    )(pos, state, planes)
-
-
-def fill_kernel(
-    pos_ref, near_ref, far_ref, c_in, s1_in, s2_in, s3_in, own_ref, c_ref, s1_ref, s2_ref, s3_ref, all_ref, side_ref, sems
-):
-    odd, x = pos_ref[0], pos_ref[1]
-    from_near = (lane_of((80, 128)) % 8 < 3) == (odd == 1)
-    edge = jnp.where(from_near, near_ref[...], far_ref[...])
-    for i in range(4):
-        all_ref[i] = edge[i * 16 : i * 16 + 16]
-        side_ref[i] = edge[64:80].astype(BF16)
-    moves = [pltpu.make_async_copy(side_ref, c_ref.at[:, pl.ds(288, 16)], sems.at[0])]
-    for k, send in enumerate((s1_ref, s2_ref, s3_ref)):
-        moves.append(pltpu.make_async_copy(all_ref.at[lax.rem(x + k + 1, 4)], send.at[16], sems.at[k + 1]))
-    for move in moves:
-        move.start()
-    own_ref[...] = all_ref[x]
-    for move in moves:
-        move.wait()
-
-
-def fill(pos, near, far, copies, sends):
-    send = jax.ShapeDtypeStruct((17,) + TILE, F32)
-    near = pltpu.with_memory_space_constraint(near, pltpu.VMEM)
-    far = pltpu.with_memory_space_constraint(far, pltpu.VMEM)
-    return pl.pallas_call(
-        fill_kernel,
-        out_shape=(jax.ShapeDtypeStruct(TILE, F32), jax.ShapeDtypeStruct(copies.shape, BF16), send, send, send),
-        in_specs=[SMEM, VMEM, VMEM, HBM, HBM, HBM, HBM],
-        out_specs=(VMEM, HBM, HBM, HBM, HBM),
-        scratch_shapes=[
-            pltpu.VMEM((4,) + TILE, F32),
-            pltpu.VMEM((4,) + TILE, BF16),
-            pltpu.SemaphoreType.DMA((4,)),
-        ],
-        input_output_aliases={3: 1, 4: 2, 5: 3, 6: 4},
-        name="fill",
-    )(pos, near, far, copies, *sends)
+    )(in_vmem(states))
 
 
 def weights_of(planes, first, last):
@@ -131,12 +130,12 @@
     return new
 
 
-def advance_kernel(pos_ref, p_ref, own_ref, r1_ref, r2_ref, r3_ref, t_ref, out_ref, w_ref, h_ref):
-    x = pos_ref[1]
+def advance_kernel(p_ref, near_ref, far_ref, t_ref, out_ref, w_ref, h_ref, edge_ref):
     lane = lane_of(TILE)
     row = lax.broadcasted_iota(jnp.int32, TILE, 0)
     lane_first, lane_last = lane == 0, lane == 127
     row_first, row_last = row == 0, row == 15
+    edge_ref[...] = merge(near_ref[...], far_ref[...])
 
     def one_level(y, carry):
         side = t_ref[y, 288:304, :].astype(F32)
@@ -148,13 +147,9 @@
                 planes = [pltpu.roll(side, (125 - (k * 6 + q) * 8) % 128, 1) for q in range(6)]
                 for i, weight in enumerate(weights_of(planes, row_first, row_last)):
                     h_ref[k, i] = weight
-        for m, source in enumerate((None, r1_ref, r2_ref, r3_ref)):
-            if source is None:
-                state = [p_ref[f, y, x] for f in range(4)]
-                edge = own_ref[...]
-            else:
-                state = [source[4 * f + y] for f in range(4)]
-                edge = source[16]
+        for m in range(4):
+            state = [p_ref[m, f, y] for f in range(4)]
+            edge = edge_ref[m]
             halo = [pltpu.roll(edge, lax.rem(253 - (4 * f + y) * 8, 128), 1) for f in range(4)]
             for k in range(3):
                 east = [pltpu.roll(v, 127, 1) for v in state]
@@ -178,23 +173,25 @@
                     )
                 state = new
             for f in range(4):
-                out_ref[lax.rem(x + 4 - m, 4), f, y] = state[f]
+                out_ref[m, f, y] = state[f]
         return carry
 
     lax.fori_loop(0, 4, one_level, 0)
 
 
-def advance(pos, state, own, received, planes):
-    received = [pltpu.with_memory_space_constraint(r, pltpu.VMEM) for r in received]
-    planes = pltpu.with_memory_space_constraint(planes, pltpu.VMEM)
+def advance(states, near, far, planes):
     return pl.pallas_call(
         advance_kernel,
-        out_shape=jax.ShapeDtypeStruct((4, 4, 4) + TILE, F32),
-        in_specs=[SMEM] + [VMEM] * 6,
+        out_shape=pltpu.VMEM((4, 4, 4) + TILE, F32),
+        in_specs=[VMEM] * 4,
         out_specs=VMEM,
-        scratch_shapes=[pltpu.VMEM((3, 9) + TILE, F32), pltpu.VMEM((2, 9) + TILE, F32)],
+        scratch_shapes=[
+            pltpu.VMEM((3, 9) + TILE, F32),
+            pltpu.VMEM((2, 9) + TILE, F32),
+            pltpu.VMEM((4,) + TILE, F32),
+        ],
         name="advance",
-    )(pos, state, own, *received, planes)
+    )(in_vmem(states), in_vmem(near), in_vmem(far), in_vmem(planes))
 
 
 def pick_kernel(b_ref, row_ref, col_ref, out_ref, val_ref, high_ref, low_ref, sems):
@@ -238,7 +235,6 @@
 
 def pick(blocks, rows, cols):
     owners = rows.shape[0]
-    blocks = pltpu.with_memory_space_constraint(blocks, pltpu.VMEM)
     return pl.pallas_call(
         pick_kernel,
         out_shape=(
@@ -253,26 +249,28 @@
             pltpu.SemaphoreType.DMA((4,)),
         ],
         name="pick",
-    )(blocks, rows, cols)
+    )(in_vmem(blocks), rows, cols)
 
 
 def on_device(perturbation, trajectory, site_col, site_lev, obs_counts, obs_weights):
     tiles, slots = site_col.shape[0], site_col.shape[2]
     state = perturbation.reshape((4, 4, 4) + TILE)
     local = trajectory.reshape(288, 128)
-    pos = jnp.stack([lax.axis_index("space") % 2, lax.axis_index("x")]).astype(jnp.int32)
     pairs = [(i, i ^ 1) for i in range(tiles)]
     crossed = [(i, (i + 1) % tiles if i % 2 else (i - 1) % tiles) for i in range(tiles)]
 
-    edge, copies, *sends = pack(pos, state, local)
+    blocks, copies, edge = send(state, local)
+    states = lax.all_to_all(blocks, "x", 0, 0, tiled=True)
     far = lax.ppermute(edge, "space", crossed)
     near = lax.ppermute(edge, "space", pairs)
-    own, copies, *sends = fill(pos, near, far, copies, sends)
+    copies = fill(near, far, copies)
     planes = lax.all_to_all(copies, "yhi", 0, 0, tiled=True)
-    received = [
-        lax.ppermute(send, "x", [(i, (i + k + 1) % 4) for i in range(4)]) for k, send in enumerate(sends)
-    ]
-    blocks = advance(pos, state, own, received, planes)
+
+    late, _ = lax.optimization_barrier((states, copies))
+    edge = pack(late)
+    far = lax.ppermute(edge, "space", crossed)
+    near = lax.ppermute(edge, "space", pairs)
+    blocks = advance(states, near, far, planes)
     blocks = lax.all_to_all(blocks, "x", 0, 0, tiled=True)
 
     live = jnp.arange(slots, dtype=jnp.int32)[None, :] < obs_counts

time: 94.3 us -> 108 us (1.15)
  Pallas kernels: 17.6 us -> 31.8 us
  blocking collectives: 30.2 us -> 23.5 us
  starting transfers between devices: 30 us -> 36.2 us
    pallas_call x3 -> x4, Pallas kernels: 10.2 us -> 24.5 us  [the longest x1 18.5 us: send(): pl.pallas_call(send_kernel, out_shape=(jax.ShapeDtypeStruct((4, 4, 4) + T...]
    ppermute x3 -> x0, starting transfers between devices: 8.41 us -> none  [on_device(): lax.ppermute(send, 'x', [(i, (i + k + 1) % 4) for i in range(4)])]
    ppermute x1 -> x2, starting transfers between devices: 12.4 us -> 19.4 us  [on_device(): near = lax.ppermute(edge, 'space', pairs)]
    all_to_all x1, blocking collectives: 30.2 us -> 23.5 us  [on_device(): received = lax.all_to_all(values, 'space', 0, 0, tiled=True)]
    all_to_all x0 -> x1, starting transfers between devices: none -> 4.85 us  [on_device(): states = lax.all_to_all(blocks, 'x', 0, 0, tiled=True)]
    ppermute x1 -> x2, waiting for transfers between devices: 3.59 us -> 7.08 us  [on_device(): far = lax.ppermute(edge, 'space', crossed)]
    ppermute x3 -> x0, waiting for transfers between devices: 3.28 us -> none  [on_device(): lax.ppermute(send, 'x', [(i, (i + k + 1) % 4) for i in range(4)])]
    ppermute x1 -> x2, starting transfers between devices: 1.92 us -> 3.84 us  [on_device(): far = lax.ppermute(edge, 'space', crossed)]
  transfers between devices with their start and end apart: 7 -> 7, of which waited for: 4 -> 3; matrix products, arithmetic and copies ran while one was open for 1% -> 1% of each run, Pallas kernels for 0% -> 1%
where the time goes in v4:
time: 108 us; the launch traced here: 107 us
  starting transfers between devices  36.2 us (34%)
  Pallas kernels  31.8 us (29%)
  blocking collectives  23.5 us (22%)
  waiting for transfers between devices  12.9 us (12%)
  other arithmetic  1.35 us (1%)
    all_to_all x1, blocking collectives, on_device(): received = lax.all_to_all(values, 'space', 0, 0, tiled=True)  23.5 us
    ppermute x2, starting transfers between devices, on_device(): near = lax.ppermute(edge, 'space', pairs)  19.4 us
    pallas_call x1, Pallas kernels, send(): pl.pallas_call(send_kernel, out_shape=(jax.ShapeDtypeStruct((4, 4, 4) + T...  18.5 us
    pallas_call x1, Pallas kernels, pick(): pl.pallas_call(pick_kernel, out_shape=(jax.ShapeDtypeStruct((4, 4, 4) + T...  7.31 us
    ppermute x2, waiting for transfers between devices, on_device(): far = lax.ppermute(edge, 'space', crossed)  7.08 us
    all_to_all x1, waiting for transfers between devices, on_device(): blocks = lax.all_to_all(blocks, 'x', 0, 0, tiled=True)  5.77 us
    all_to_all x1, starting transfers between devices, on_device(): states = lax.all_to_all(blocks, 'x', 0, 0, tiled=True)  4.85 us
    all_to_all x1, starting transfers between devices, on_device(): blocks = lax.all_to_all(blocks, 'x', 0, 0, tiled=True)  4.65 us
  transfers between devices with their start and end apart: 7, of which 3 were waited for; matrix products, arithmetic and copies ran while one was open for 1% of the time, Pallas kernels for 1%

profile of v4, /device:TPU:1, one launch (start us, length us, event | category | flops | bytes accessed | tf_op | source)
XLA Modules:
  0.0 107.2 jit_solution(12643289878641592814)
XLA Ops:
  0.6 18.5 %send.1 = (f32[4,4,4,16,128]{4,3,2,1,0:T(8,128)}, bf16[4,304,128]{2,1,0:T(8,128)(2,1)}, bf16[16,128]{1,0:T(8,128)(2,1)}) custom-call(f32[4,4,4,16,128]{4,3,2,1,0:T(8,128)} %bitcast.11, bf16[288,128]{1,0:T(8,128)(2,1)} %bitcast.12), custom_call_target="tpu_custom_call" | custom-call | tf_op jit(solution)/shard_map/send/pallas_call | solution.py:44
  19.2 0.0 copy-start.4
  19.2 4.9 %all-to-all-start = ((f32[4,4,4,16,128]{4,3,2,1,0:T(8,128)}), f32[4,4,4,16,128]{4,3,2,1,0:T(8,128)S(1)}, u32[]{:S(2)}, u32[]{:S(2)}) async-start(f32[4,4,4,16,128]{4,3,2,1,0:T(8,128)} %get-tuple-element.8), calls=%async_computation | async-start | bytes 1048576 | tf_op jit(solution)/shard_map/all_to_all | solution.py:263
  24.0 11.1 %collective-permute-start = (bf16[16,128]{1,0:T(8,128)(2,1)S(1)}, bf16[16,128]{1,0:T(8,128)(2,1)S(1)}, u32[]{:S(2)}, u32[]{:S(2)}) collective-permute-start(bf16[16,128]{1,0:T(8,128)(2,1)S(1)} %copy-done.4), channel_id=1, source_target_pairs={{0,16},{16,0},{32,48},{48,32},{64,80},{80,64},{96,112},{112,96},{1... | collective-permute-start | bytes 12296 | tf_op jit(solution)/shard_map/ppermute | solution.py:265
  35.1 1.9 %collective-permute-start.1 = (bf16[16,128]{1,0:T(8,128)(2,1)S(1)}, bf16[16,128]{1,0:T(8,128)(2,1)S(1)}, u32[]{:S(2)}, u32[]{:S(2)}) collective-permute-start(bf16[16,128]{1,0:T(8,128)(2,1)S(1)} %copy-done.4), channel_id=1, source_target_pairs={{0,752},{16,32},{32,16},{48,64},{64,48},{80,96},{96,80},{112,128},... | collective-permute-start | bytes 12296 | tf_op jit(solution)/shard_map/ppermute | solution.py:264
  37.0 0.0 collective-permute-done.near_ref
  37.1 3.3 %collective-permute-done.1.far_ref = bf16[16,128]{1,0:T(8,128)(2,1)S(1)} collective-permute-done((bf16[16,128]{1,0:T(8,128)(2,1)S(1)}, bf16[16,128]{1,0:T(8,128)(2,1)S(1)}, u32[]{:S(2)}, u32[]{:S(2)}) %collective-permute-start.1) | collective-permute-done | bytes 4128 | tf_op jit(solution)/shard_map/ppermute | solution.py:264
  40.3 0.6 fill.1
  41.0 0.0 all-to-all-done.p_ref
  41.0 3.5 %all-to-all-start.1 = ((bf16[4,304,128]{2,1,0:T(8,128)(2,1)}), bf16[4,304,128]{2,1,0:T(8,128)(2,1)S(1)}, u32[]{:S(2)}, u32[]{:S(2)}) async-start(bf16[4,304,128]{2,1,0:T(8,128)(2,1)} %fill.1), calls=%async_computation.1 | async-start | bytes 622592 | tf_op jit(solution)/shard_map/all_to_all | solution.py:267
  44.5 0.8 pack.1
  45.3 8.3 %collective-permute-start.2 = (f32[4,16,128]{2,1,0:T(8,128)}, f32[4,16,128]{2,1,0:T(8,128)S(1)}, u32[]{:S(2)}, u32[]{:S(2)}) collective-permute-start(f32[4,16,128]{2,1,0:T(8,128)} %pack.1), channel_id=1, source_target_pairs={{0,16},{16,0},{32,48},{48,32},{64,80},{80,64},{96,112},{112,96},{1... | collective-permute-start | bytes 98312 | tf_op jit(solution)/shard_map/ppermute | solution.py:272
  53.6 1.9 %collective-permute-start.3 = (f32[4,16,128]{2,1,0:T(8,128)}, f32[4,16,128]{2,1,0:T(8,128)S(1)}, u32[]{:S(2)}, u32[]{:S(2)}) collective-permute-start(f32[4,16,128]{2,1,0:T(8,128)} %pack.1), channel_id=1, source_target_pairs={{0,752},{16,32},{32,16},{48,64},{64,48},{80,96},{96,80},{112,128},... | collective-permute-start | bytes 98312 | tf_op jit(solution)/shard_map/ppermute | solution.py:271
  55.5 0.0 collective-permute-done.2.near_ref
  55.5 3.8 %collective-permute-done.3.far_ref = f32[4,16,128]{2,1,0:T(8,128)S(1)} collective-permute-done((f32[4,16,128]{2,1,0:T(8,128)}, f32[4,16,128]{2,1,0:T(8,128)S(1)}, u32[]{:S(2)}, u32[]{:S(2)}) %collective-permute-start.3) | collective-permute-done | bytes 32800 | tf_op jit(solution)/shard_map/ppermute | solution.py:271
  59.3 4.6 %advance.1 = f32[4,4,4,16,128]{4,3,2,1,0:T(8,128)} custom-call(f32[4,4,4,16,128]{4,3,2,1,0:T(8,128)S(1)} %all-to-all-done.p_ref, f32[4,16,128]{2,1,0:T(8,128)S(1)} %collective-permute-done.2.near_ref, f32[4,16,128]{2,1,0:T(8,128)S(1)} %collective-permute-done.3.far_ref, bf16[4,304,128]{2,1,0:T(8,128)(2,1)S(1)} %all-to-all-done.1.t_ref), custom_call_target="tpu_custom_call" | custom-call | tf_op jit(solution)/shard_map/advance/pallas_call | solution.py:183
  63.9 4.6 %all-to-all-start.2 = ((f32[4,4,4,16,128]{4,3,2,1,0:T(8,128)}), f32[4,4,4,16,128]{4,3,2,1,0:T(8,128)S(1)}, u32[]{:S(2)}, u32[]{:S(2)}) async-start(f32[4,4,4,16,128]{4,3,2,1,0:T(8,128)} %advance.1), calls=%async_computation.2 | async-start | bytes 1048576 | tf_op jit(solution)/shard_map/all_to_all | solution.py:274
  68.5 0.6 copy-done.3
  69.2 0.7 add_select_fusion
  69.9 5.8 %all-to-all-done.2.b_ref = f32[4,4,4,16,128]{4,3,2,1,0:T(8,128)S(1)} async-done(((f32[4,4,4,16,128]{4,3,2,1,0:T(8,128)}), f32[4,4,4,16,128]{4,3,2,1,0:T(8,128)S(1)}, u32[]{:S(2)}, u32[]{:S(2)}) %all-to-all-start.2) | async-done | bytes 524320 | tf_op jit(solution)/shard_map/all_to_all | solution.py:274
  75.6 7.3 %pick.1 = (f32[4,4,4,16,128]{4,3,2,1,0:T(8,128)}, f32[48,4,128]{2,1,0:T(4,128)}) custom-call(f32[4,4,4,16,128]{4,3,2,1,0:T(8,128)S(1)} %all-to-all-done.2.b_ref, s32[48,128]{1,0:T(8,128)} %get-tuple-element.15.row_ref, s32[48,128]{1,0:T(8,128)} %get-tuple-element.14.col_ref), custom_call_target="tpu_custom_call" | custom-call | tf_op jit(solution)/shard_map/pick/pallas_call | solution.py:238
  83.0 0.0 copy-start
  83.0 23.5 %all_to_all.20 = f32[48,4,128]{2,1,0:T(4,128)S(1)} all-to-all(f32[48,4,128]{2,1,0:T(4,128)} %get-tuple-element.13), channel_id=1, replica_groups=mesh['space'=48,'yhi'=4,'x'=4] {'space'}, dimensions={0} | all-to-all | bytes 196608 | tf_op jit(solution)/shard_map/all_to_all | solution.py:280
  106.5 0.7 fusion
  (8 shorter events, 0.0 us)
Async XLA Ops:
  19.2 4.9 %copy-start.4 = (bf16[16,128]{1,0:T(8,128)(2,1)S(1)}, bf16[16,128]{1,0:T(8,128)(2,1)}, u32[]{:S(2)}) copy-start(bf16[16,128]{1,0:T(8,128)(2,1)} %get-tuple-element.9) | copy-start | bytes 12292
  19.2 21.8 %all-to-all-start = ((f32[4,4,4,16,128]{4,3,2,1,0:T(8,128)}), f32[4,4,4,16,128]{4,3,2,1,0:T(8,128)S(1)}, u32[]{:S(2)}, u32[]{:S(2)}) async-start(f32[4,4,4,16,128]{4,3,2,1,0:T(8,128)} %get-tuple-element.8), calls=%async_computation | async-start | bytes 1048576 | tf_op jit(solution)/shard_map/all_to_all | solution.py:263
  24.0 13.0 %collective-permute-start = (bf16[16,128]{1,0:T(8,128)(2,1)S(1)}, bf16[16,128]{1,0:T(8,128)(2,1)S(1)}, u32[]{:S(2)}, u32[]{:S(2)}) collective-permute-start(bf16[16,128]{1,0:T(8,128)(2,1)S(1)} %copy-done.4), channel_id=1, source_target_pairs={{0,16},{16,0},{32,48},{48,32},{64,80},{80,64},{96,112},{112,96},{1... | collective-permute-start | bytes 12296 | tf_op jit(solution)/shard_map/ppermute | solution.py:265
  35.1 5.2 %collective-permute-start.1 = (bf16[16,128]{1,0:T(8,128)(2,1)S(1)}, bf16[16,128]{1,0:T(8,128)(2,1)S(1)}, u32[]{:S(2)}, u32[]{:S(2)}) collective-permute-start(bf16[16,128]{1,0:T(8,128)(2,1)S(1)} %copy-done.4), channel_id=1, source_target_pairs={{0,752},{16,32},{32,16},{48,64},{64,48},{80,96},{96,80},{112,128},... | collective-permute-start | bytes 12296 | tf_op jit(solution)/shard_map/ppermute | solution.py:264
  41.0 18.3 %all-to-all-start.1 = ((bf16[4,304,128]{2,1,0:T(8,128)(2,1)}), bf16[4,304,128]{2,1,0:T(8,128)(2,1)S(1)}, u32[]{:S(2)}, u32[]{:S(2)}) async-start(bf16[4,304,128]{2,1,0:T(8,128)(2,1)} %fill.1), calls=%async_computation.1 | async-start | bytes 622592 | tf_op jit(solution)/shard_map/all_to_all | solution.py:267
  45.3 10.2 %collective-permute-start.2 = (f32[4,16,128]{2,1,0:T(8,128)}, f32[4,16,128]{2,1,0:T(8,128)S(1)}, u32[]{:S(2)}, u32[]{:S(2)}) collective-permute-start(f32[4,16,128]{2,1,0:T(8,128)} %pack.1), channel_id=1, source_target_pairs={{0,16},{16,0},{32,48},{48,32},{64,80},{80,64},{96,112},{112,96},{1... | collective-permute-start | bytes 98312 | tf_op jit(solution)/shard_map/ppermute | solution.py:272
  53.6 5.7 %collective-permute-start.3 = (f32[4,16,128]{2,1,0:T(8,128)}, f32[4,16,128]{2,1,0:T(8,128)S(1)}, u32[]{:S(2)}, u32[]{:S(2)}) collective-permute-start(f32[4,16,128]{2,1,0:T(8,128)} %pack.1), channel_id=1, source_target_pairs={{0,752},{16,32},{32,16},{48,64},{64,48},{80,96},{96,80},{112,128},... | collective-permute-start | bytes 98312 | tf_op jit(solution)/shard_map/ppermute | solution.py:271
  63.9 4.7 %copy-start.1 = (s32[48,1,128]{2,1,0:T(1,128)S(1)}, s32[48,1,128]{2,1,0:T(1,128)}, u32[]{:S(2)}) copy-start(s32[48,1,128]{2,1,0:T(1,128)} %param.8) | copy-start | bytes 73732
  63.9 4.7 %copy-start.2 = (s32[48,1,128]{2,1,0:T(1,128)S(1)}, s32[48,1,128]{2,1,0:T(1,128)}, u32[]{:S(2)}) copy-start(s32[48,1,128]{2,1,0:T(1,128)} %param.9) | copy-start | bytes 73732
  63.9 11.8 %all-to-all-start.2 = ((f32[4,4,4,16,128]{4,3,2,1,0:T(8,128)}), f32[4,4,4,16,128]{4,3,2,1,0:T(8,128)S(1)}, u32[]{:S(2)}, u32[]{:S(2)}) async-start(f32[4,4,4,16,128]{4,3,2,1,0:T(8,128)} %advance.1), calls=%async_computation.2 | async-start | bytes 1048576 | tf_op jit(solution)/shard_map/all_to_all | solution.py:274
  68.5 0.7 copy-start.3
  83.0 23.5 %copy-start = (f32[1,48,4,128]{3,2,1,0:T(4,128)S(1)}, f32[1,48,4,128]{3,2,1,0:T(4,128)}, u32[]{:S(2)}) copy-start(f32[1,48,4,128]{3,2,1,0:T(4,128)} %param.11) | copy-start | bytes 294916

commit v5 on v4

--- a/solution.py
+++ b/solution.py
@@ -48,7 +48,7 @@
             jax.ShapeDtypeStruct((4, 304, 128), BF16),
             jax.ShapeDtypeStruct(TILE, BF16),
         ),
-        in_specs=[HBM, VMEM],
+        in_specs=[VMEM, VMEM],
         out_specs=(HBM, HBM, VMEM),
         scratch_shapes=[pltpu.SemaphoreType.DMA((4,)), pltpu.SemaphoreType.DMA((4,))],
         name="send",

time: 108 us -> 91.9 us (0.85)
  Pallas kernels: 31.8 us -> 15.9 us
    pallas_call x1, Pallas kernels: 18.5 us -> 2.59 us  [send(): pl.pallas_call(send_kernel, out_shape=(jax.ShapeDtypeStruct((4, 4, 4) + T...]
  transfers between devices with their start and end apart: 7 -> 7, of which waited for: 3 -> 3; matrix products, arithmetic and copies ran while one was open for 1% -> 1% of each run, Pallas kernels for 1% -> 2%
where the time goes in v5:
time: 91.9 us; the launch traced here: 91.2 us
  starting transfers between devices  36.2 us (39%)
  blocking collectives  23.5 us (26%)
  Pallas kernels  15.9 us (17%)
  waiting for transfers between devices  12.9 us (14%)
  other arithmetic  1.35 us (1%)
    all_to_all x1, blocking collectives, on_device(): received = lax.all_to_all(values, 'space', 0, 0, tiled=True)  23.5 us
    ppermute x2, starting transfers between devices, on_device(): near = lax.ppermute(edge, 'space', pairs)  19.4 us
    pallas_call x1, Pallas kernels, pick(): pl.pallas_call(pick_kernel, out_shape=(jax.ShapeDtypeStruct((4, 4, 4) + T...  7.31 us
    ppermute x2, waiting for transfers between devices, on_device(): far = lax.ppermute(edge, 'space', crossed)  7.08 us
    all_to_all x1, waiting for transfers between devices, on_device(): blocks = lax.all_to_all(blocks, 'x', 0, 0, tiled=True)  5.77 us
    all_to_all x1, starting transfers between devices, on_device(): states = lax.all_to_all(blocks, 'x', 0, 0, tiled=True)  4.85 us
    all_to_all x1, starting transfers between devices, on_device(): blocks = lax.all_to_all(blocks, 'x', 0, 0, tiled=True)  4.65 us
    pallas_call x1, Pallas kernels, advance(): pl.pallas_call(advance_kernel, out_shape=pltpu.VMEM((4, 4, 4) + TILE, F32...  4.56 us
  transfers between devices with their start and end apart: 7, of which 3 were waited for; matrix products, arithmetic and copies ran while one was open for 1% of the time, Pallas kernels for 2%

profile of v5, /device:TPU:1, one launch (start us, length us, event | category | flops | bytes accessed | tf_op | source)
XLA Modules:
  0.0 91.2 jit_solution(11111047673159458052)
XLA Ops:
  0.6 2.6 %send.1 = (f32[4,4,4,16,128]{4,3,2,1,0:T(8,128)}, bf16[4,304,128]{2,1,0:T(8,128)(2,1)}, bf16[16,128]{1,0:T(8,128)(2,1)}) custom-call(f32[4,4,4,16,128]{4,3,2,1,0:T(8,128)} %bitcast.11, bf16[288,128]{1,0:T(8,128)(2,1)} %bitcast.12), custom_call_target="tpu_custom_call" | custom-call | tf_op jit(solution)/shard_map/send/pallas_call | solution.py:44
  3.2 0.0 copy-start.4
  3.2 4.9 %all-to-all-start = ((f32[4,4,4,16,128]{4,3,2,1,0:T(8,128)}), f32[4,4,4,16,128]{4,3,2,1,0:T(8,128)S(1)}, u32[]{:S(2)}, u32[]{:S(2)}) async-start(f32[4,4,4,16,128]{4,3,2,1,0:T(8,128)} %get-tuple-element.8), calls=%async_computation | async-start | bytes 1048576 | tf_op jit(solution)/shard_map/all_to_all | solution.py:263
  8.1 11.1 %collective-permute-start = (bf16[16,128]{1,0:T(8,128)(2,1)S(1)}, bf16[16,128]{1,0:T(8,128)(2,1)S(1)}, u32[]{:S(2)}, u32[]{:S(2)}) collective-permute-start(bf16[16,128]{1,0:T(8,128)(2,1)S(1)} %copy-done.4), channel_id=1, source_target_pairs={{0,16},{16,0},{32,48},{48,32},{64,80},{80,64},{96,112},{112,96},{1... | collective-permute-start | bytes 12296 | tf_op jit(solution)/shard_map/ppermute | solution.py:265
  19.2 1.9 %collective-permute-start.1 = (bf16[16,128]{1,0:T(8,128)(2,1)S(1)}, bf16[16,128]{1,0:T(8,128)(2,1)S(1)}, u32[]{:S(2)}, u32[]{:S(2)}) collective-permute-start(bf16[16,128]{1,0:T(8,128)(2,1)S(1)} %copy-done.4), channel_id=1, source_target_pairs={{0,752},{16,32},{32,16},{48,64},{64,48},{80,96},{96,80},{112,128},... | collective-permute-start | bytes 12296 | tf_op jit(solution)/shard_map/ppermute | solution.py:264
  21.1 0.0 collective-permute-done.near_ref
  21.1 3.3 %collective-permute-done.1.far_ref = bf16[16,128]{1,0:T(8,128)(2,1)S(1)} collective-permute-done((bf16[16,128]{1,0:T(8,128)(2,1)S(1)}, bf16[16,128]{1,0:T(8,128)(2,1)S(1)}, u32[]{:S(2)}, u32[]{:S(2)}) %collective-permute-start.1) | collective-permute-done | bytes 4128 | tf_op jit(solution)/shard_map/ppermute | solution.py:264
  24.4 0.6 fill.1
  25.0 0.0 all-to-all-done.p_ref
  25.0 3.5 %all-to-all-start.1 = ((bf16[4,304,128]{2,1,0:T(8,128)(2,1)}), bf16[4,304,128]{2,1,0:T(8,128)(2,1)S(1)}, u32[]{:S(2)}, u32[]{:S(2)}) async-start(bf16[4,304,128]{2,1,0:T(8,128)(2,1)} %fill.1), calls=%async_computation.1 | async-start | bytes 622592 | tf_op jit(solution)/shard_map/all_to_all | solution.py:267
  28.5 0.8 pack.1
  29.3 8.3 %collective-permute-start.2 = (f32[4,16,128]{2,1,0:T(8,128)}, f32[4,16,128]{2,1,0:T(8,128)S(1)}, u32[]{:S(2)}, u32[]{:S(2)}) collective-permute-start(f32[4,16,128]{2,1,0:T(8,128)} %pack.1), channel_id=1, source_target_pairs={{0,16},{16,0},{32,48},{48,32},{64,80},{80,64},{96,112},{112,96},{1... | collective-permute-start | bytes 98312 | tf_op jit(solution)/shard_map/ppermute | solution.py:272
  37.6 1.9 %collective-permute-start.3 = (f32[4,16,128]{2,1,0:T(8,128)}, f32[4,16,128]{2,1,0:T(8,128)S(1)}, u32[]{:S(2)}, u32[]{:S(2)}) collective-permute-start(f32[4,16,128]{2,1,0:T(8,128)} %pack.1), channel_id=1, source_target_pairs={{0,752},{16,32},{32,16},{48,64},{64,48},{80,96},{96,80},{112,128},... | collective-permute-start | bytes 98312 | tf_op jit(solution)/shard_map/ppermute | solution.py:271
  39.6 3.8 %collective-permute-done.3.far_ref = f32[4,16,128]{2,1,0:T(8,128)S(1)} collective-permute-done((f32[4,16,128]{2,1,0:T(8,128)}, f32[4,16,128]{2,1,0:T(8,128)S(1)}, u32[]{:S(2)}, u32[]{:S(2)}) %collective-permute-start.3) | collective-permute-done | bytes 32800 | tf_op jit(solution)/shard_map/ppermute | solution.py:271
  43.4 0.0 all-to-all-done.1.t_ref
  43.4 4.6 %advance.1 = f32[4,4,4,16,128]{4,3,2,1,0:T(8,128)} custom-call(f32[4,4,4,16,128]{4,3,2,1,0:T(8,128)S(1)} %all-to-all-done.p_ref, f32[4,16,128]{2,1,0:T(8,128)S(1)} %collective-permute-done.2.near_ref, f32[4,16,128]{2,1,0:T(8,128)S(1)} %collective-permute-done.3.far_ref, bf16[4,304,128]{2,1,0:T(8,128)(2,1)S(1)} %all-to-all-done.1.t_ref), custom_call_target="tpu_custom_call" | custom-call | tf_op jit(solution)/shard_map/advance/pallas_call | solution.py:183
  47.9 4.6 %all-to-all-start.2 = ((f32[4,4,4,16,128]{4,3,2,1,0:T(8,128)}), f32[4,4,4,16,128]{4,3,2,1,0:T(8,128)S(1)}, u32[]{:S(2)}, u32[]{:S(2)}) async-start(f32[4,4,4,16,128]{4,3,2,1,0:T(8,128)} %advance.1), calls=%async_computation.2 | async-start | bytes 1048576 | tf_op jit(solution)/shard_map/all_to_all | solution.py:274
  52.6 0.6 copy-done.3
  53.2 0.7 add_select_fusion
  53.9 5.8 %all-to-all-done.2.b_ref = f32[4,4,4,16,128]{4,3,2,1,0:T(8,128)S(1)} async-done(((f32[4,4,4,16,128]{4,3,2,1,0:T(8,128)}), f32[4,4,4,16,128]{4,3,2,1,0:T(8,128)S(1)}, u32[]{:S(2)}, u32[]{:S(2)}) %all-to-all-start.2) | async-done | bytes 524320 | tf_op jit(solution)/shard_map/all_to_all | solution.py:274
  59.7 7.3 %pick.1 = (f32[4,4,4,16,128]{4,3,2,1,0:T(8,128)}, f32[48,4,128]{2,1,0:T(4,128)}) custom-call(f32[4,4,4,16,128]{4,3,2,1,0:T(8,128)S(1)} %all-to-all-done.2.b_ref, s32[48,128]{1,0:T(8,128)} %get-tuple-element.15.row_ref, s32[48,128]{1,0:T(8,128)} %get-tuple-element.14.col_ref), custom_call_target="tpu_custom_call" | custom-call | tf_op jit(solution)/shard_map/pick/pallas_call | solution.py:238
  67.0 0.0 copy-start
  67.0 23.5 %all_to_all.20 = f32[48,4,128]{2,1,0:T(4,128)S(1)} all-to-all(f32[48,4,128]{2,1,0:T(4,128)} %get-tuple-element.13), channel_id=1, replica_groups=mesh['space'=48,'yhi'=4,'x'=4] {'space'}, dimensions={0} | all-to-all | bytes 196608 | tf_op jit(solution)/shard_map/all_to_all | solution.py:280
  90.6 0.7 fusion
  (8 shorter events, 0.0 us)
Async XLA Ops:
  3.2 4.9 %copy-start.4 = (bf16[16,128]{1,0:T(8,128)(2,1)S(1)}, bf16[16,128]{1,0:T(8,128)(2,1)}, u32[]{:S(2)}) copy-start(bf16[16,128]{1,0:T(8,128)(2,1)} %get-tuple-element.9) | copy-start | bytes 12292
  3.2 21.8 %all-to-all-start = ((f32[4,4,4,16,128]{4,3,2,1,0:T(8,128)}), f32[4,4,4,16,128]{4,3,2,1,0:T(8,128)S(1)}, u32[]{:S(2)}, u32[]{:S(2)}) async-start(f32[4,4,4,16,128]{4,3,2,1,0:T(8,128)} %get-tuple-element.8), calls=%async_computation | async-start | bytes 1048576 | tf_op jit(solution)/shard_map/all_to_all | solution.py:263
  8.1 13.0 %collective-permute-start = (bf16[16,128]{1,0:T(8,128)(2,1)S(1)}, bf16[16,128]{1,0:T(8,128)(2,1)S(1)}, u32[]{:S(2)}, u32[]{:S(2)}) collective-permute-start(bf16[16,128]{1,0:T(8,128)(2,1)S(1)} %copy-done.4), channel_id=1, source_target_pairs={{0,16},{16,0},{32,48},{48,32},{64,80},{80,64},{96,112},{112,96},{1... | collective-permute-start | bytes 12296 | tf_op jit(solution)/shard_map/ppermute | solution.py:265
  19.2 5.2 %collective-permute-start.1 = (bf16[16,128]{1,0:T(8,128)(2,1)S(1)}, bf16[16,128]{1,0:T(8,128)(2,1)S(1)}, u32[]{:S(2)}, u32[]{:S(2)}) collective-permute-start(bf16[16,128]{1,0:T(8,128)(2,1)S(1)} %copy-done.4), channel_id=1, source_target_pairs={{0,752},{16,32},{32,16},{48,64},{64,48},{80,96},{96,80},{112,128},... | collective-permute-start | bytes 12296 | tf_op jit(solution)/shard_map/ppermute | solution.py:264
  25.0 18.3 %all-to-all-start.1 = ((bf16[4,304,128]{2,1,0:T(8,128)(2,1)}), bf16[4,304,128]{2,1,0:T(8,128)(2,1)S(1)}, u32[]{:S(2)}, u32[]{:S(2)}) async-start(bf16[4,304,128]{2,1,0:T(8,128)(2,1)} %fill.1), calls=%async_computation.1 | async-start | bytes 622592 | tf_op jit(solution)/shard_map/all_to_all | solution.py:267
  29.3 10.2 %collective-permute-start.2 = (f32[4,16,128]{2,1,0:T(8,128)}, f32[4,16,128]{2,1,0:T(8,128)S(1)}, u32[]{:S(2)}, u32[]{:S(2)}) collective-permute-start(f32[4,16,128]{2,1,0:T(8,128)} %pack.1), channel_id=1, source_target_pairs={{0,16},{16,0},{32,48},{48,32},{64,80},{80,64},{96,112},{112,96},{1... | collective-permute-start | bytes 98312 | tf_op jit(solution)/shard_map/ppermute | solution.py:272
  37.6 5.7 %collective-permute-start.3 = (f32[4,16,128]{2,1,0:T(8,128)}, f32[4,16,128]{2,1,0:T(8,128)S(1)}, u32[]{:S(2)}, u32[]{:S(2)}) collective-permute-start(f32[4,16,128]{2,1,0:T(8,128)} %pack.1), channel_id=1, source_target_pairs={{0,752},{16,32},{32,16},{48,64},{64,48},{80,96},{96,80},{112,128},... | collective-permute-start | bytes 98312 | tf_op jit(solution)/shard_map/ppermute | solution.py:271
  47.9 4.7 %copy-start.1 = (s32[48,1,128]{2,1,0:T(1,128)S(1)}, s32[48,1,128]{2,1,0:T(1,128)}, u32[]{:S(2)}) copy-start(s32[48,1,128]{2,1,0:T(1,128)} %param.8) | copy-start | bytes 73732
  47.9 4.7 %copy-start.2 = (s32[48,1,128]{2,1,0:T(1,128)S(1)}, s32[48,1,128]{2,1,0:T(1,128)}, u32[]{:S(2)}) copy-start(s32[48,1,128]{2,1,0:T(1,128)} %param.9) | copy-start | bytes 73732
  47.9 11.8 %all-to-all-start.2 = ((f32[4,4,4,16,128]{4,3,2,1,0:T(8,128)}), f32[4,4,4,16,128]{4,3,2,1,0:T(8,128)S(1)}, u32[]{:S(2)}, u32[]{:S(2)}) async-start(f32[4,4,4,16,128]{4,3,2,1,0:T(8,128)} %advance.1), calls=%async_computation.2 | async-start | bytes 1048576 | tf_op jit(solution)/shard_map/all_to_all | solution.py:274
  52.6 0.7 copy-start.3
  67.0 23.5 %copy-start = (f32[1,48,4,128]{3,2,1,0:T(4,128)S(1)}, f32[1,48,4,128]{3,2,1,0:T(4,128)}, u32[]{:S(2)}) copy-start(f32[1,48,4,128]{3,2,1,0:T(4,128)} %param.11) | copy-start | bytes 294916

commit v6 on v5

v6 whole, which is shorter than its diff:
```python
import functools

import jax
import jax.numpy as jnp
import numpy as np
from jax import lax
from jax.experimental import pallas as pl
from jax.experimental.pallas import tpu as pltpu
from jax.sharding import Mesh
from jax.sharding import PartitionSpec as P

F32 = jnp.float32
BF16 = jnp.bfloat16
VMEM = pl.BlockSpec(memory_space=pltpu.VMEM)
HBM = pl.BlockSpec(memory_space=pltpu.HBM)
TILE = (16, 128)


axis_index = lax.axis_index


def lane_of(shape):
    return lax.broadcasted_iota(jnp.int32, shape, len(shape) - 1)


def send_kernel(t_ref, copies_ref, edge_ref, copy_sems):
    moves = [
        pltpu.make_async_copy(t_ref, copies_ref.at[i, pl.ds(0, 288)], copy_sems.at[i]) for i in range(4)
    ]
    for move in moves:
        move.start()
    group = lane_of(TILE) // 8
    packed = jnp.zeros(TILE, F32)
    for k in range(12):
        moved = pltpu.roll(t_ref[k * 16 : k * 16 + 16, :].astype(F32), (k * 8 + 3) % 128, 1)
        packed = jnp.where(group == k, moved, packed)
    edge_ref[...] = packed.astype(BF16)
    for move in moves:
        move.wait()


def send(planes):
    return pl.pallas_call(
        send_kernel,
        out_shape=(jax.ShapeDtypeStruct((4, 304, 128), BF16), jax.ShapeDtypeStruct(TILE, BF16)),
        in_specs=[VMEM],
        out_specs=(HBM, VMEM),
        scratch_shapes=[pltpu.SemaphoreType.DMA((4,))],
        name="send",
    )(planes)


def spread_kernel(t_ref, out_ref, sems):
    moves = [pltpu.make_async_copy(t_ref, out_ref.at[i], sems.at[i]) for i in range(4)]
    for move in moves:
        move.start()
    for move in moves:
        move.wait()


def spread(planes):
    return pl.pallas_call(
        spread_kernel,
        out_shape=jax.ShapeDtypeStruct((4,) + planes.shape, BF16),
        in_specs=[VMEM],
        out_specs=HBM,
        scratch_shapes=[pltpu.SemaphoreType.DMA((4,))],
        name="spread",
    )(in_vmem(planes))


def merge(near, far):
    odd = axis_index("space") % 2
    return jnp.where((lane_of(near.shape) % 8 < 3) == (odd == 1), near, far)


def fill_kernel(near_ref, far_ref, c_in, c_ref, side_ref, sem):
    edge = merge(near_ref[...].astype(F32), far_ref[...].astype(F32)).astype(BF16)
    for i in range(4):
        side_ref[i] = edge
    move = pltpu.make_async_copy(side_ref, c_ref.at[:, pl.ds(288, 16)], sem)
    move.start()
    move.wait()


def in_vmem(x):
    return pltpu.with_memory_space_constraint(x, pltpu.VMEM)


def fill(near, far, copies):
    return pl.pallas_call(
        fill_kernel,
        out_shape=jax.ShapeDtypeStruct(copies.shape, BF16),
        in_specs=[VMEM, VMEM, HBM],
        out_specs=HBM,
        scratch_shapes=[pltpu.VMEM((4,) + TILE, BF16), pltpu.SemaphoreType.DMA],
        input_output_aliases={2: 0},
        name="fill",
    )(in_vmem(near), in_vmem(far), copies)


def pack_kernel(p_ref, edge_ref):
    group = lane_of(TILE) // 8
    for f in range(4):
        packed = jnp.zeros(TILE, F32)
        for level in range(16):
            moved = pltpu.roll(p_ref[f, level // 4, level % 4], (level * 8 + 3) % 128, 1)
            packed = jnp.where(group == level, moved, packed)
        edge_ref[f] = packed


def pack(state):
    return pl.pallas_call(
        pack_kernel,
        out_shape=jax.ShapeDtypeStruct((4,) + TILE, F32),
        in_specs=[VMEM],
        out_specs=VMEM,
        name="pack",
    )(in_vmem(state))


def weights_of(planes, first, last):
    a, b = planes[0], planes[1]
    aa, bb = a * a, b * b
    return [
        1.0 - aa - bb,
        0.5 * (aa - a),
        0.5 * (aa + a),
        jnp.where(last, 0.0, 0.5 * (bb - b)),
        jnp.where(first, 0.0, 0.5 * (bb + b)),
    ] + planes[2:]


def apply_stencil(w, p, other, lane_first, lane_last):
    new = []
    for f in range(4):
        east = pltpu.roll(jnp.where(lane_first, other[f], p[f]), 127, 1)
        west = pltpu.roll(jnp.where(lane_last, other[f], p[f]), 1, 1)
        north, south = pltpu.roll(p[f], 15, 0), pltpu.roll(p[f], 1, 0)
        new.append((w[0] * p[f] + w[1] * east) + (w[2] * west + (w[3] * north + w[4] * south)))
    new[2] = new[2] - (w[5] * p[0] + w[6] * p[1])
    new[3] = new[3] - (w[7] * p[0] + w[8] * p[1])
    return new


def advance_level(planes_of, side, state, halo):
    lane = lane_of(TILE)
    row = lax.broadcasted_iota(jnp.int32, TILE, 0)
    ends = lane == 0, lane == 127
    rims = row == 0, row == 15
    for k in range(3):
        new = apply_stencil(weights_of([planes_of(k * 6 + q) for q in range(6)], *rims), state, halo, *ends)
        if k < 2:
            planes = [pltpu.roll(side, (125 - (k * 6 + q) * 8) % 128, 1) for q in range(6)]
            halo = apply_stencil(weights_of(planes, *rims), halo, state, *ends)
        state = new
    return state


def main_kernel(p_ref, near_ref, far_ref, t_ref, row_ref, col_ref, out_ref, val_ref, edge_ref, final_ref, table_ref, sem):
    owners = row_ref.shape[0]
    edge_ref[...] = merge(near_ref[...], far_ref[...])

    def one_level(level, carry):
        y, x = level // 4, lax.rem(level, 4)
        shift = lax.rem(253 - level * 8, 128)
        state = advance_level(
            lambda i: t_ref[x, y, i * 16 : i * 16 + 16, :].astype(F32),
            t_ref[x, y, 288:304, :].astype(F32),
            [p_ref[f, y, x] for f in range(4)],
            [pltpu.roll(edge_ref[f], shift, 1) for f in range(4)],
        )
        for f in range(4):
            final_ref[f, y, x] = state[f]
        return carry

    lax.fori_loop(0, 16, one_level, 0, unroll=2)
    move = pltpu.make_async_copy(final_ref, out_ref, sem)
    move.start()

    for f in range(4):
        for half in range(2):
            block = jnp.transpose(final_ref[f, 2 * half : 2 * half + 2].reshape(128, 128))
            high = block.astype(BF16)
            low = (block - high.astype(F32)).astype(BF16)
            table_ref[f * 128 : f * 128 + 128, half * 128 : half * 128 + 128] = high
            table_ref[f * 128 : f * 128 + 128, 256 + half * 128 : 384 + half * 128] = low

    line = lax.broadcasted_iota(jnp.int32, (256, 128), 0)
    lon = lax.broadcasted_iota(jnp.int32, (128, 128), 0)

    def four_owners(i, carry):
        picks = []
        for o in range(4):
            hit = line == row_ref[pl.ds(4 * i + o, 1), :]
            picks.append(jnp.where(hit, 1.0, 0.0).astype(BF16))
        pick = jnp.concatenate(picks, axis=1)
        pick = jnp.concatenate([pick, pick], axis=0)
        lines = jnp.dot(table_ref[...], pick, preferred_element_type=F32)
        for o in range(4):
            hit = lon == col_ref[pl.ds(4 * i + o, 1), :]
            for f in range(4):
                part = lines[f * 128 : f * 128 + 128, o * 128 : o * 128 + 128]
                val_ref[4 * i + o, f : f + 1, :] = jnp.sum(jnp.where(hit, part, 0.0), axis=0, keepdims=True)
        return carry

    lax.fori_loop(0, owners // 4, four_owners, 0, unroll=2)
    move.wait()


def advance_and_pick(state, near, far, planes, rows, cols):
    owners = rows.shape[0]
    return pl.pallas_call(
        main_kernel,
        out_shape=(
            jax.ShapeDtypeStruct(state.shape, F32),
            jax.ShapeDtypeStruct((owners, 4, 128), F32),
        ),
        in_specs=[VMEM] * 6,
        out_specs=(HBM, VMEM),
        scratch_shapes=[
            pltpu.VMEM((4,) + TILE, F32),
            pltpu.VMEM(state.shape, F32),
            pltpu.VMEM((512, 512), BF16),
            pltpu.SemaphoreType.DMA,
        ],
        name="advance_and_pick",
    )(in_vmem(state), in_vmem(near), in_vmem(far), in_vmem(planes), in_vmem(rows), in_vmem(cols))


def on_device(perturbation, trajectory, site_col, site_lev, obs_counts, obs_weights):
    tiles, slots = site_col.shape[0], site_col.shape[2]
    state = perturbation.reshape((4, 4, 4) + TILE)
    local = trajectory.reshape(288, 128)
    pairs = [(i, i ^ 1) for i in range(tiles)]
    crossed = [(i, (i + 1) % tiles if i % 2 else (i - 1) % tiles) for i in range(tiles)]

    copies, edge = send(local)
    far = lax.ppermute(edge, "space", crossed)
    near = lax.ppermute(edge, "space", pairs)
    copies = fill(near, far, copies)
    planes = lax.all_to_all(copies, "yhi", 0, 0, tiled=True)

    late, _ = lax.optimization_barrier((state, copies))
    edge = pack(late)
    far = lax.ppermute(edge, "space", crossed)
    near = lax.ppermute(edge, "space", pairs)
    planes = lax.all_to_all(spread(planes), "x", 0, 0, tiled=True)

    live = jnp.arange(slots, dtype=jnp.int32)[None, :] < obs_counts
    rows = jnp.where(live, site_lev[:, 0, :] * 16 + site_col[:, 0, :] // 128, -1)
    cols = site_col[:, 0, :] % 128
    final, values = advance_and_pick(state, near, far, planes, rows, cols)
    received = lax.all_to_all(values, "space", 0, 0, tiled=True)
    summed = jnp.sum(obs_weights[0] * received, axis=1)
    return (final.reshape(perturbation.shape), summed.reshape(1, 1, tiles, slots))


def solution(mesh):
    member = ("yhi", "x")
    fine = Mesh(np.asarray(mesh.devices).reshape(mesh.shape["space"], 4, 4), ("space",) + member)
    in_specs = (
        P(member, None, None, None, "space"),
        P(None, member, None, None, "space"),
        P(None, "space", None),
        P(None, "space", None),
        P(None, "space"),
        P("space", None, None, None),
    )
    out_specs = (P(member, None, None, None, "space"), P(member, "space", None, None))
    return jax.shard_map(
        on_device, mesh=fine, in_specs=in_specs, out_specs=out_specs, check_vma=False
    )
```

time: 91.9 us -> 92.6 us (level)
  blocking collectives: 23.5 us -> 40.4 us
  starting transfers between devices: 36.2 us -> 29.7 us
  waiting for transfers between devices: 12.9 us -> 6.91 us
  Pallas kernels: 15.9 us -> 13.5 us
    all_to_all x0 -> x1, blocking collectives: none -> 12.4 us  [on_device(): planes = lax.all_to_all(copies, 'yhi', 0, 0, tiled=True)]
    all_to_all x3 -> x1, starting transfers between devices: 13 us -> 3.68 us  [on_device(): planes = lax.all_to_all(spread(planes), 'x', 0, 0, tiled=True)]
    all_to_all x3 -> x1, waiting for transfers between devices: 5.78 us -> 0.01 us  [on_device(): planes = lax.all_to_all(spread(planes), 'x', 0, 0, tiled=True)]
    all_to_all x1, blocking collectives: 23.5 us -> 28 us  [on_device(): received = lax.all_to_all(values, 'space', 0, 0, tiled=True)]
    ppermute x2, starting transfers between devices: 19.4 us -> 22.2 us  [on_device(): near = lax.ppermute(edge, 'space', pairs)]
    pallas_call x3, Pallas kernels: 14.5 us -> 12.1 us  [the longest x1 8.79 us: advance_and_pick(): pl.pallas_call(main_kernel, out_shape=(jax.ShapeDtypeStruct(state.shape,...]
  transfers between devices with their start and end apart: 7 -> 5, of which waited for: 3 -> 2; matrix products, arithmetic and copies ran while one was open for 1% -> 0% of each run, Pallas kernels for 2% -> 1%
where the time goes in v6:
time: 92.6 us; the launch traced here: 92.1 us
  blocking collectives  40.4 us (44%)
  starting transfers between devices  29.7 us (32%)
  Pallas kernels  13.5 us (15%)
  waiting for transfers between devices  6.91 us (7%)
    all_to_all x1, blocking collectives, on_device(): received = lax.all_to_all(values, 'space', 0, 0, tiled=True)  28 us
    ppermute x2, starting transfers between devices, on_device(): near = lax.ppermute(edge, 'space', pairs)  22.2 us
    all_to_all x1, blocking collectives, on_device(): planes = lax.all_to_all(copies, 'yhi', 0, 0, tiled=True)  12.4 us
    pallas_call x1, Pallas kernels, advance_and_pick(): pl.pallas_call(main_kernel, out_shape=(jax.ShapeDtypeStruct(state.shape,...  8.79 us
    ppermute x2, waiting for transfers between devices, on_device(): far = lax.ppermute(edge, 'space', crossed)  6.9 us
    ppermute x2, starting transfers between devices, on_device(): far = lax.ppermute(edge, 'space', crossed)  3.84 us
    all_to_all x1, starting transfers between devices, on_device(): planes = lax.all_to_all(spread(planes), 'x', 0, 0, tiled=True)  3.68 us
    pallas_call x1, Pallas kernels, send(): pl.pallas_call(send_kernel, out_shape=(jax.ShapeDtypeStruct((4, 304, 128)...  2.21 us
  transfers between devices with their start and end apart: 5, of which 2 were waited for; matrix products, arithmetic and copies ran while one was open for 0% of the time, Pallas kernels for 1%

profile of v6, /device:TPU:1, one launch (start us, length us, event | category | flops | bytes accessed | tf_op | source)
XLA Modules:
  0.0 92.1 jit_solution(9128596558389189927)
XLA Ops:
  0.6 2.2 %send.1 = (bf16[4,304,128]{2,1,0:T(8,128)(2,1)}, bf16[16,128]{1,0:T(8,128)(2,1)}) custom-call(bf16[288,128]{1,0:T(8,128)(2,1)} %bitcast.15), custom_call_target="tpu_custom_call" | custom-call | tf_op jit(solution)/shard_map/send/pallas_call | solution.py:43
  2.9 12.4 %collective-permute-start = (bf16[16,128]{1,0:T(8,128)(2,1)}, bf16[16,128]{1,0:T(8,128)(2,1)S(1)}, u32[]{:S(2)}, u32[]{:S(2)}) collective-permute-start(bf16[16,128]{1,0:T(8,128)(2,1)} %get-tuple-element.7), channel_id=1, source_target_pairs={{0,16},{16,0},{32,48},{48,32},{64,80},{80,64},{96,112},{112,96},{1... | collective-permute-start | bytes 12296 | tf_op jit(solution)/shard_map/ppermute | solution.py:240
  15.3 1.9 %collective-permute-start.1 = (bf16[16,128]{1,0:T(8,128)(2,1)}, bf16[16,128]{1,0:T(8,128)(2,1)S(1)}, u32[]{:S(2)}, u32[]{:S(2)}) collective-permute-start(bf16[16,128]{1,0:T(8,128)(2,1)} %get-tuple-element.7), channel_id=1, source_target_pairs={{0,752},{16,32},{32,16},{48,64},{64,48},{80,96},{96,80},{112,128},... | collective-permute-start | bytes 12296 | tf_op jit(solution)/shard_map/ppermute | solution.py:239
  17.2 0.0 collective-permute-done.near_ref
  17.2 3.2 %collective-permute-done.1.far_ref = bf16[16,128]{1,0:T(8,128)(2,1)S(1)} collective-permute-done((bf16[16,128]{1,0:T(8,128)(2,1)}, bf16[16,128]{1,0:T(8,128)(2,1)S(1)}, u32[]{:S(2)}, u32[]{:S(2)}) %collective-permute-start.1) | collective-permute-done | bytes 4128 | tf_op jit(solution)/shard_map/ppermute | solution.py:239
  20.4 0.6 fill.1
  21.0 12.4 %all_to_all.15.t_ref = bf16[4,304,128]{2,1,0:T(8,128)(2,1)S(1)} all-to-all(bf16[4,304,128]{2,1,0:T(8,128)(2,1)} %fill.1), channel_id=1, replica_groups=mesh['space'=48,'yhi'=4,'x'=4] {'yhi'}, dimensions={0} | all-to-all | bytes 622592 | tf_op jit(solution)/shard_map/all_to_all | solution.py:242
  33.5 1.1 %spread.1 = bf16[4,4,304,128]{3,2,1,0:T(8,128)(2,1)} custom-call(bf16[4,304,128]{2,1,0:T(8,128)(2,1)S(1)} %all_to_all.15.t_ref), custom_call_target="tpu_custom_call" | custom-call | tf_op jit(solution)/shard_map/spread/pallas_call | solution.py:62
  34.6 0.0 copy-start
  34.6 0.0 copy-start.2
  34.6 0.0 copy-start.3
  34.6 0.0 copy-start.4
  34.6 3.7 %all-to-all-start.1 = ((bf16[4,4,304,128]{3,2,1,0:T(8,128)(2,1)}), bf16[4,4,304,128]{3,2,1,0:T(8,128)(2,1)S(1)}, u32[]{:S(2)}, u32[]{:S(2)}) async-start(bf16[4,4,304,128]{3,2,1,0:T(8,128)(2,1)} %spread.1), calls=%async_computation.1 | async-start | bytes 2490368 | tf_op jit(solution)/shard_map/all_to_all | solution.py:248
  38.3 0.0 copy-start.1
  38.3 0.8 pack.1
  39.2 9.7 %collective-permute-start.2 = (f32[4,16,128]{2,1,0:T(8,128)}, f32[4,16,128]{2,1,0:T(8,128)S(1)}, u32[]{:S(2)}, u32[]{:S(2)}) collective-permute-start(f32[4,16,128]{2,1,0:T(8,128)} %pack.1), channel_id=1, source_target_pairs={{0,16},{16,0},{32,48},{48,32},{64,80},{80,64},{96,112},{112,96},{1... | collective-permute-start | bytes 98312 | tf_op jit(solution)/shard_map/ppermute | solution.py:247
  48.9 1.9 %collective-permute-start.3 = (f32[4,16,128]{2,1,0:T(8,128)}, f32[4,16,128]{2,1,0:T(8,128)S(1)}, u32[]{:S(2)}, u32[]{:S(2)}) collective-permute-start(f32[4,16,128]{2,1,0:T(8,128)} %pack.1), channel_id=1, source_target_pairs={{0,752},{16,32},{32,16},{48,64},{64,48},{80,96},{96,80},{112,128},... | collective-permute-start | bytes 98312 | tf_op jit(solution)/shard_map/ppermute | solution.py:246
  50.9 0.1 add_select_fusion
  50.9 0.0 collective-permute-done.2.near_ref
  50.9 3.7 %collective-permute-done.3.far_ref = f32[4,16,128]{2,1,0:T(8,128)S(1)} collective-permute-done((f32[4,16,128]{2,1,0:T(8,128)}, f32[4,16,128]{2,1,0:T(8,128)S(1)}, u32[]{:S(2)}, u32[]{:S(2)}) %collective-permute-start.3) | collective-permute-done | bytes 32800 | tf_op jit(solution)/shard_map/ppermute | solution.py:246
  54.6 0.0 all-to-all-done.1.t_ref
  54.6 8.8 %advance_and_pick.1 = (f32[4,4,4,16,128]{4,3,2,1,0:T(8,128)}, f32[48,4,128]{2,1,0:T(4,128)}) custom-call(f32[4,4,4,16,128]{4,3,2,1,0:T(8,128)S(1)} %bitcast.14, f32[4,16,128]{2,1,0:T(8,128)S(1)} %collective-permute-done.2.near_ref, f32[4,16,128]{2,1,0:T(8,128)S(1)} %collective-permute-done.3.far_ref, bf16[4,4,304,128]{3,2,1,0:T(8,128)(2,1)S(1)} %all-to-all-done.1.t_ref, ...), custom_call_target="tpu_custom_call" | custom-call | tf_op jit(solution)/shard_map/advance_and_pick/pallas_call | solution.py:213
  63.4 28.0 %all_to_all.16 = f32[48,4,128]{2,1,0:T(4,128)S(1)} all-to-all(f32[48,4,128]{2,1,0:T(4,128)} %get-tuple-element.11), channel_id=1, replica_groups=mesh['space'=48,'yhi'=4,'x'=4] {'space'}, dimensions={0} | all-to-all | bytes 196608 | tf_op jit(solution)/shard_map/all_to_all | solution.py:254
  91.4 0.7 fusion
  (5 shorter events, 0.0 us)
Async XLA Ops:
  2.9 14.4 %collective-permute-start = (bf16[16,128]{1,0:T(8,128)(2,1)}, bf16[16,128]{1,0:T(8,128)(2,1)S(1)}, u32[]{:S(2)}, u32[]{:S(2)}) collective-permute-start(bf16[16,128]{1,0:T(8,128)(2,1)} %get-tuple-element.7), channel_id=1, source_target_pairs={{0,16},{16,0},{32,48},{48,32},{64,80},{80,64},{96,112},{112,96},{1... | collective-permute-start | bytes 12296 | tf_op jit(solution)/shard_map/ppermute | solution.py:240
  15.3 5.1 %collective-permute-start.1 = (bf16[16,128]{1,0:T(8,128)(2,1)}, bf16[16,128]{1,0:T(8,128)(2,1)S(1)}, u32[]{:S(2)}, u32[]{:S(2)}) collective-permute-start(bf16[16,128]{1,0:T(8,128)(2,1)} %get-tuple-element.7), channel_id=1, source_target_pairs={{0,752},{16,32},{32,16},{48,64},{64,48},{80,96},{96,80},{112,128},... | collective-permute-start | bytes 12296 | tf_op jit(solution)/shard_map/ppermute | solution.py:239
  34.6 3.7 %copy-start = (f32[1,4,16,16,128]{4,3,2,1,0:T(8,128)S(1)}, f32[1,4,16,16,128]{4,3,2,1,0:T(8,128)}, u32[]{:S(2)}) copy-start(f32[1,4,16,16,128]{4,3,2,1,0:T(8,128)} %param.6) | copy-start | bytes 1572868
  34.6 16.2 %copy-start.2 = (s32[48,1,128]{2,1,0:T(1,128)S(1)}, s32[48,1,128]{2,1,0:T(1,128)}, u32[]{:S(2)}) copy-start(s32[48,1,128]{2,1,0:T(1,128)} %param.8) | copy-start | bytes 73732
  34.6 16.2 %copy-start.3 = (s32[48,1,128]{2,1,0:T(1,128)S(1)}, s32[48,1,128]{2,1,0:T(1,128)}, u32[]{:S(2)}) copy-start(s32[48,1,128]{2,1,0:T(1,128)} %param.9) | copy-start | bytes 73732
  34.6 16.2 %copy-start.4 = (s32[48,1]{0,1:T(1,128)S(1)}, s32[48,1]{0,1:T(1,128)}, u32[]{:S(2)}) copy-start(s32[48,1]{0,1:T(1,128)} %param.10) | copy-start | bytes 580
  34.6 20.0 %all-to-all-start.1 = ((bf16[4,4,304,128]{3,2,1,0:T(8,128)(2,1)}), bf16[4,4,304,128]{3,2,1,0:T(8,128)(2,1)S(1)}, u32[]{:S(2)}, u32[]{:S(2)}) async-start(bf16[4,4,304,128]{3,2,1,0:T(8,128)(2,1)} %spread.1), calls=%async_computation.1 | async-start | bytes 2490368 | tf_op jit(solution)/shard_map/all_to_all | solution.py:248
  38.3 53.1 %copy-start.1 = (f32[1,48,4,128]{3,2,1,0:T(4,128)S(1)}, f32[1,48,4,128]{3,2,1,0:T(4,128)}, u32[]{:S(2)}) copy-start(f32[1,48,4,128]{3,2,1,0:T(4,128)} %param.11) | copy-start | bytes 294916
  39.2 11.8 %collective-permute-start.2 = (f32[4,16,128]{2,1,0:T(8,128)}, f32[4,16,128]{2,1,0:T(8,128)S(1)}, u32[]{:S(2)}, u32[]{:S(2)}) collective-permute-start(f32[4,16,128]{2,1,0:T(8,128)} %pack.1), channel_id=1, source_target_pairs={{0,16},{16,0},{32,48},{48,32},{64,80},{80,64},{96,112},{112,96},{1... | collective-permute-start | bytes 98312 | tf_op jit(solution)/shard_map/ppermute | solution.py:247
  48.9 5.7 %collective-permute-start.3 = (f32[4,16,128]{2,1,0:T(8,128)}, f32[4,16,128]{2,1,0:T(8,128)S(1)}, u32[]{:S(2)}, u32[]{:S(2)}) collective-permute-start(f32[4,16,128]{2,1,0:T(8,128)} %pack.1), channel_id=1, source_target_pairs={{0,752},{16,32},{32,16},{48,64},{64,48},{80,96},{96,80},{112,128},... | collective-permute-start | bytes 98312 | tf_op jit(solution)/shard_map/ppermute | solution.py:246

commit v7 on v6

--- a/solution.py
+++ b/solution.py
@@ -23,31 +23,8 @@
     return lax.broadcasted_iota(jnp.int32, shape, len(shape) - 1)
 
 
-def send_kernel(t_ref, copies_ref, edge_ref, copy_sems):
-    moves = [
-        pltpu.make_async_copy(t_ref, copies_ref.at[i, pl.ds(0, 288)], copy_sems.at[i]) for i in range(4)
-    ]
-    for move in moves:
-        move.start()
-    group = lane_of(TILE) // 8
-    packed = jnp.zeros(TILE, F32)
-    for k in range(12):
-        moved = pltpu.roll(t_ref[k * 16 : k * 16 + 16, :].astype(F32), (k * 8 + 3) % 128, 1)
-        packed = jnp.where(group == k, moved, packed)
-    edge_ref[...] = packed.astype(BF16)
-    for move in moves:
-        move.wait()
-
-
-def send(planes):
-    return pl.pallas_call(
-        send_kernel,
-        out_shape=(jax.ShapeDtypeStruct((4, 304, 128), BF16), jax.ShapeDtypeStruct(TILE, BF16)),
-        in_specs=[VMEM],
-        out_specs=(HBM, VMEM),
-        scratch_shapes=[pltpu.SemaphoreType.DMA((4,))],
-        name="send",
-    )(planes)
+def in_vmem(x):
+    return pltpu.with_memory_space_constraint(x, pltpu.VMEM)
 
 
 def spread_kernel(t_ref, out_ref, sems):
@@ -66,40 +43,10 @@
         out_specs=HBM,
         scratch_shapes=[pltpu.SemaphoreType.DMA((4,))],
         name="spread",
-    )(in_vmem(planes))
-
-
-def merge(near, far):
-    odd = axis_index("space") % 2
-    return jnp.where((lane_of(near.shape) % 8 < 3) == (odd == 1), near, far)
-
-
-def fill_kernel(near_ref, far_ref, c_in, c_ref, side_ref, sem):
-    edge = merge(near_ref[...].astype(F32), far_ref[...].astype(F32)).astype(BF16)
-    for i in range(4):
-        side_ref[i] = edge
-    move = pltpu.make_async_copy(side_ref, c_ref.at[:, pl.ds(288, 16)], sem)
-    move.start()
-    move.wait()
-
-
-def in_vmem(x):
-    return pltpu.with_memory_space_constraint(x, pltpu.VMEM)
-
-
-def fill(near, far, copies):
-    return pl.pallas_call(
-        fill_kernel,
-        out_shape=jax.ShapeDtypeStruct(copies.shape, BF16),
-        in_specs=[VMEM, VMEM, HBM],
-        out_specs=HBM,
-        scratch_shapes=[pltpu.VMEM((4,) + TILE, BF16), pltpu.SemaphoreType.DMA],
-        input_output_aliases={2: 0},
-        name="fill",
-    )(in_vmem(near), in_vmem(far), copies)
-
-
-def pack_kernel(p_ref, edge_ref):
+    )(planes)
+
+
+def pack_kernel(p_ref, t_ref, edge_ref):
     group = lane_of(TILE) // 8
     for f in range(4):
         packed = jnp.zeros(TILE, F32)
@@ -107,16 +54,44 @@
             moved = pltpu.roll(p_ref[f, level // 4, level % 4], (level * 8 + 3) % 128, 1)
             packed = jnp.where(group == level, moved, packed)
         edge_ref[f] = packed
-
-
-def pack(state):
+    for y in range(4):
+        packed = jnp.zeros(TILE, F32)
+        for k in range(12):
+            moved = pltpu.roll(t_ref[y, k * 16 : k * 16 + 16, :].astype(F32), (k * 8 + 3) % 128, 1)
+            packed = jnp.where(group == k, moved, packed)
+        edge_ref[4 + y] = packed
+
+
+def pack(state, planes):
     return pl.pallas_call(
         pack_kernel,
-        out_shape=jax.ShapeDtypeStruct((4,) + TILE, F32),
-        in_specs=[VMEM],
+        out_shape=jax.ShapeDtypeStruct((8,) + TILE, F32),
+        in_specs=[VMEM, VMEM],
         out_specs=VMEM,
         name="pack",
-    )(in_vmem(state))
+    )(in_vmem(state), in_vmem(planes))
+
+
+def merge(near, far):
+    odd = axis_index("space") % 2
+    return jnp.where((lane_of(near.shape) % 8 < 3) == (odd == 1), near, far)
+
+
+def fill_kernel(near_ref, far_ref, halo_ref, side_ref):
+    edge = merge(near_ref[...], far_ref[...])
+    halo_ref[...] = edge[0:4]
+    for i in range(4):
+        side_ref[i] = edge[4:8].astype(BF16)
+
+
+def fill(near, far):
+    return pl.pallas_call(
+        fill_kernel,
+        out_shape=(jax.ShapeDtypeStruct((4,) + TILE, F32), jax.ShapeDtypeStruct((4, 4) + TILE, BF16)),
+        in_specs=[VMEM, VMEM],
+        out_specs=(VMEM, VMEM),
+        name="fill",
+    )(in_vmem(near), in_vmem(far))
 
 
 def weights_of(planes, first, last):
@@ -157,24 +132,56 @@
     return state
 
 
-def main_kernel(p_ref, near_ref, far_ref, t_ref, row_ref, col_ref, out_ref, val_ref, edge_ref, final_ref, table_ref, sem):
+def advance_at(y, x, p_ref, halo_ref, planes_of, side):
+    shift = lax.rem(253 - (4 * y + x) * 8, 128)
+    state = [p_ref[f, y, x] for f in range(4)]
+    halo = [pltpu.roll(halo_ref[f], shift, 1) for f in range(4)]
+    return advance_level(planes_of, side.astype(F32), state, halo)
+
+
+def own_kernel(p_ref, halo_ref, t_ref, side_ref, out_ref):
+    x = axis_index("x")
+
+    def one_level(y, carry):
+        state = advance_at(
+            y, x, p_ref, halo_ref, lambda i: t_ref[y, i * 16 : i * 16 + 16, :].astype(F32), side_ref[0, y]
+        )
+        for f in range(4):
+            out_ref[f, y] = state[f]
+        return carry
+
+    lax.fori_loop(0, 4, one_level, 0, unroll=2)
+
+
+def advance_own(state, halo, planes, side):
+    return pl.pallas_call(
+        own_kernel,
+        out_shape=jax.ShapeDtypeStruct((4, 4) + TILE, F32),
+        in_specs=[VMEM] * 4,
+        out_specs=VMEM,
+        name="advance_own",
+    )(in_vmem(state), halo, in_vmem(planes), side)
+
+
+def main_kernel(
+    p_ref, halo_ref, own_ref, t_ref, side_ref, row_ref, col_ref, out_ref, val_ref, final_ref, table_ref, sem
+):
     owners = row_ref.shape[0]
-    edge_ref[...] = merge(near_ref[...], far_ref[...])
-
-    def one_level(level, carry):
-        y, x = level // 4, lax.rem(level, 4)
-        shift = lax.rem(253 - level * 8, 128)
-        state = advance_level(
-            lambda i: t_ref[x, y, i * 16 : i * 16 + 16, :].astype(F32),
-            t_ref[x, y, 288:304, :].astype(F32),
-            [p_ref[f, y, x] for f in range(4)],
-            [pltpu.roll(edge_ref[f], shift, 1) for f in range(4)],
+    here = axis_index("x")
+
+    def one_level(i, carry):
+        y, x = lax.rem(i, 4), lax.rem(here + 1 + i // 4, 4)
+        state = advance_at(
+            y, x, p_ref, halo_ref, lambda j: t_ref[x, y, j * 16 : j * 16 + 16, :].astype(F32), side_ref[x, y]
         )
         for f in range(4):
             final_ref[f, y, x] = state[f]
         return carry
 
-    lax.fori_loop(0, 16, one_level, 0, unroll=2)
+    lax.fori_loop(0, 12, one_level, 0, unroll=2)
+    for f in range(4):
+        for y in range(4):
+            final_ref[f, y, here] = own_ref[f, y]
     move = pltpu.make_async_copy(final_ref, out_ref, sem)
     move.start()
 
@@ -208,7 +215,7 @@
     move.wait()
 
 
-def advance_and_pick(state, near, far, planes, rows, cols):
+def advance_and_pick(state, halo, own, planes, sides, rows, cols):
     owners = rows.shape[0]
     return pl.pallas_call(
         main_kernel,
@@ -216,16 +223,15 @@
             jax.ShapeDtypeStruct(state.shape, F32),
             jax.ShapeDtypeStruct((owners, 4, 128), F32),
         ),
-        in_specs=[VMEM] * 6,
+        in_specs=[VMEM] * 7,
         out_specs=(HBM, VMEM),
         scratch_shapes=[
-            pltpu.VMEM((4,) + TILE, F32),
             pltpu.VMEM(state.shape, F32),
             pltpu.VMEM((512, 512), BF16),
             pltpu.SemaphoreType.DMA,
         ],
         name="advance_and_pick",
-    )(in_vmem(state), in_vmem(near), in_vmem(far), in_vmem(planes), in_vmem(rows), in_vmem(cols))
+    )(*map(in_vmem, (state, halo, own, planes, sides, rows, cols)))
 
 
 def on_device(perturbation, trajectory, site_col, site_lev, obs_counts, obs_weights):
@@ -235,22 +241,23 @@
     pairs = [(i, i ^ 1) for i in range(tiles)]
     crossed = [(i, (i + 1) % tiles if i % 2 else (i - 1) % tiles) for i in range(tiles)]
 
-    copies, edge = send(local)
+    first = lax.all_to_all(spread(local), "yhi", 0, 0, tiled=True)
+    copies = spread(in_vmem(first))
+    planes = lax.all_to_all(copies, "x", 0, 0, tiled=True)
+
+    late, _ = lax.optimization_barrier((first, copies))
+    edge = pack(state, late)
     far = lax.ppermute(edge, "space", crossed)
     near = lax.ppermute(edge, "space", pairs)
-    copies = fill(near, far, copies)
-    planes = lax.all_to_all(copies, "yhi", 0, 0, tiled=True)
-
-    late, _ = lax.optimization_barrier((state, copies))
-    edge = pack(late)
-    far = lax.ppermute(edge, "space", crossed)
-    near = lax.ppermute(edge, "space", pairs)
-    planes = lax.all_to_all(spread(planes), "x", 0, 0, tiled=True)
+    halo, side = fill(near, far)
+    own = advance_own(state, halo, first, side)
+    side, planes = lax.optimization_barrier((side, planes))
+    sides = lax.all_to_all(side, "x", 0, 0, tiled=True)
 
     live = jnp.arange(slots, dtype=jnp.int32)[None, :] < obs_counts
     rows = jnp.where(live, site_lev[:, 0, :] * 16 + site_col[:, 0, :] // 128, -1)
     cols = site_col[:, 0, :] % 128
-    final, values = advance_and_pick(state, near, far, planes, rows, cols)
+    final, values = advance_and_pick(state, halo, own, planes, sides, rows, cols)
     received = lax.all_to_all(values, "space", 0, 0, tiled=True)
     summed = jnp.sum(obs_weights[0] * received, axis=1)
     return (final.reshape(perturbation.shape), summed.reshape(1, 1, tiles, slots))

time: 92.6 us -> 89.2 us (0.963)
  starting transfers between devices: 29.7 us -> 18.6 us
  blocking collectives: 40.4 us -> 46.6 us
  Pallas kernels: 13.5 us -> 14.6 us
    ppermute x2 -> x1, starting transfers between devices: 22.2 us -> 8.43 us  [on_device(): near = lax.ppermute(edge, 'space', pairs)]
    all_to_all x1, blocking collectives: 12.4 us -> 17.3 us  [on_device(): first = lax.all_to_all(spread(local), 'yhi', 0, 0, tiled=True)]
    all_to_all x1 -> x2, starting transfers between devices: 3.68 us -> 8.2 us  [the longest x1 4.31 us: on_device(): sides = lax.all_to_all(side, 'x', 0, 0, tiled=True)]
    ppermute x2 -> x1, waiting for transfers between devices: 6.9 us -> 4.15 us  [on_device(): far = lax.ppermute(edge, 'space', crossed)]
    all_to_all x1 -> x2, waiting for transfers between devices: 0.01 us -> 2.03 us  [the longest x1 2.02 us: on_device(): sides = lax.all_to_all(side, 'x', 0, 0, tiled=True)]
    ppermute x2 -> x1, starting transfers between devices: 3.84 us -> 1.92 us  [on_device(): far = lax.ppermute(edge, 'space', crossed)]
    pallas_call x1 -> x2, Pallas kernels: 1.09 us -> 2.68 us  [spread(): pl.pallas_call(spread_kernel, out_shape=jax.ShapeDtypeStruct((4,) + plane...]
    all_to_all x1, blocking collectives: 28 us -> 29.4 us  [on_device(): received = lax.all_to_all(values, 'space', 0, 0, tiled=True)]
  transfers between devices with their start and end apart: 5 -> 4, of which waited for: 2 -> 2; matrix products, arithmetic and copies ran while one was open for 0% -> 0% of each run, Pallas kernels for 1% -> 4%
where the time goes in v7:
time: 89.2 us; the launch traced here: 88.4 us
  blocking collectives  46.6 us (52%)
  starting transfers between devices  18.6 us (21%)
  Pallas kernels  14.6 us (16%)
  waiting for transfers between devices  6.18 us (7%)
  local copies, waits for them, and re-layouts  0.94 us (1%)
    all_to_all x1, blocking collectives, on_device(): received = lax.all_to_all(values, 'space', 0, 0, tiled=True)  29.4 us
    all_to_all x1, blocking collectives, on_device(): first = lax.all_to_all(spread(local), 'yhi', 0, 0, tiled=True)  17.3 us
    ppermute x1, starting transfers between devices, on_device(): near = lax.ppermute(edge, 'space', pairs)  8.43 us
    pallas_call x1, Pallas kernels, advance_and_pick(): pl.pallas_call(main_kernel, out_shape=(jax.ShapeDtypeStruct(state.shape,...  8.02 us
    all_to_all x1, starting transfers between devices, on_device(): sides = lax.all_to_all(side, 'x', 0, 0, tiled=True)  4.31 us
    ppermute x1, waiting for transfers between devices, on_device(): far = lax.ppermute(edge, 'space', crossed)  4.15 us
    all_to_all x1, starting transfers between devices, on_device(): planes = lax.all_to_all(copies, 'x', 0, 0, tiled=True)  3.89 us
    pallas_call x2, Pallas kernels, spread(): pl.pallas_call(spread_kernel, out_shape=jax.ShapeDtypeStruct((4,) + plane...  2.68 us
  transfers between devices with their start and end apart: 4, of which 2 were waited for; matrix products, arithmetic and copies ran while one was open for 0% of the time, Pallas kernels for 4%

profile of v7, /device:TPU:1, one launch (start us, length us, event | category | flops | bytes accessed | tf_op | source)
XLA Modules:
  0.0 88.4 jit_solution(4620472731395219030)
XLA Ops:
  0.6 1.6 %spread.2 = bf16[4,288,128]{2,1,0:T(8,128)(2,1)} custom-call(bf16[288,128]{1,0:T(8,128)(2,1)} %bitcast.16), custom_call_target="tpu_custom_call" | custom-call | tf_op jit(solution)/shard_map/spread/pallas_call | solution.py:39
  2.3 17.3 %all_to_all.20.t_ref = bf16[4,288,128]{2,1,0:T(8,128)(2,1)S(1)} all-to-all(bf16[4,288,128]{2,1,0:T(8,128)(2,1)} %spread.2), channel_id=1, replica_groups=mesh['space'=48,'yhi'=4,'x'=4] {'yhi'}, dimensions={0} | all-to-all | bytes 589824 | tf_op jit(solution)/shard_map/all_to_all | solution.py:244
  19.5 1.1 %spread.3 = bf16[4,4,288,128]{3,2,1,0:T(8,128)(2,1)} custom-call(bf16[4,288,128]{2,1,0:T(8,128)(2,1)S(1)} %all_to_all.20.t_ref), custom_call_target="tpu_custom_call" | custom-call | tf_op jit(solution)/shard_map/spread/pallas_call | solution.py:39
  20.6 0.0 copy-start
  20.6 0.0 copy-start.4
  20.6 0.0 copy-start.5
  20.6 0.0 copy-start.6
  20.6 3.9 %all-to-all-start.1 = ((bf16[4,4,288,128]{3,2,1,0:T(8,128)(2,1)}), bf16[4,4,288,128]{3,2,1,0:T(8,128)(2,1)S(1)}, u32[]{:S(2)}, u32[]{:S(2)}) async-start(bf16[4,4,288,128]{3,2,1,0:T(8,128)(2,1)} %spread.3), calls=%async_computation.1 | async-start | bytes 2359296 | tf_op jit(solution)/shard_map/all_to_all | solution.py:246
  24.5 0.0 copy-done
  24.5 0.9 pack.1
  25.4 8.4 %collective-permute-start = (f32[8,16,128]{2,1,0:T(8,128)}, f32[8,16,128]{2,1,0:T(8,128)S(1)}, u32[]{:S(2)}, u32[]{:S(2)}) collective-permute-start(f32[8,16,128]{2,1,0:T(8,128)} %pack.1), channel_id=1, source_target_pairs={{0,16},{16,0},{32,48},{48,32},{64,80},{80,64},{96,112},{112,96},{1... | collective-permute-start | bytes 196616 | tf_op jit(solution)/shard_map/ppermute | solution.py:251
  33.8 1.9 %collective-permute-start.1 = (f32[8,16,128]{2,1,0:T(8,128)}, f32[8,16,128]{2,1,0:T(8,128)S(1)}, u32[]{:S(2)}, u32[]{:S(2)}) collective-permute-start(f32[8,16,128]{2,1,0:T(8,128)} %pack.1), channel_id=1, source_target_pairs={{0,752},{16,32},{32,16},{48,64},{64,48},{80,96},{96,80},{112,128},... | collective-permute-start | bytes 196616 | tf_op jit(solution)/shard_map/ppermute | solution.py:250
  35.8 0.0 collective-permute-done.near_ref
  35.8 4.2 %collective-permute-done.1.far_ref = f32[8,16,128]{2,1,0:T(8,128)S(1)} collective-permute-done((f32[8,16,128]{2,1,0:T(8,128)}, f32[8,16,128]{2,1,0:T(8,128)S(1)}, u32[]{:S(2)}, u32[]{:S(2)}) %collective-permute-start.1) | collective-permute-done | bytes 65568 | tf_op jit(solution)/shard_map/ppermute | solution.py:250
  39.9 0.6 fill.1
  40.6 0.0 all-to-all-done.1.t_ref
  40.6 4.3 %all-to-all-start.2 = ((bf16[4,4,16,128]{3,2,1,0:T(8,128)(2,1)}), bf16[4,4,16,128]{3,2,1,0:T(8,128)(2,1)S(1)}, u32[]{:S(2)}, u32[]{:S(2)}) async-start(bf16[4,4,16,128]{3,2,1,0:T(8,128)(2,1)} %get-tuple-element.13.side_ref), calls=%async_computation.2 | async-start | bytes 131072 | tf_op jit(solution)/shard_map/all_to_all | solution.py:255
  44.9 0.1 add_select_fusion
  45.0 2.4 %advance_own.1.own_ref = f32[4,4,16,128]{3,2,1,0:T(8,128)} custom-call(f32[4,4,4,16,128]{4,3,2,1,0:T(8,128)S(1)} %bitcast.14, f32[4,16,128]{2,1,0:T(8,128)} %get-tuple-element.10.halo_ref, bf16[4,288,128]{2,1,0:T(8,128)(2,1)S(1)} %all_to_all.20.t_ref, bf16[4,4,16,128]{3,2,1,0:T(8,128)(2,1)} %get-tuple-element.13.side_ref), custom_call_target="tpu_custom_call" | custom-call | tf_op jit(solution)/shard_map/advance_own/pallas_call | solution.py:157
  47.4 2.0 %all-to-all-done.2.side_ref = bf16[4,4,16,128]{3,2,1,0:T(8,128)(2,1)S(1)} async-done(((bf16[4,4,16,128]{3,2,1,0:T(8,128)(2,1)}), bf16[4,4,16,128]{3,2,1,0:T(8,128)(2,1)S(1)}, u32[]{:S(2)}, u32[]{:S(2)}) %all-to-all-start.2) | async-done | bytes 65568 | tf_op jit(solution)/shard_map/all_to_all | solution.py:255
  49.4 0.9 %copy-done.1 = f32[4,4,16,128]{3,2,1,0:T(8,128)S(1)} copy-done((f32[4,4,16,128]{3,2,1,0:T(8,128)S(1)}, f32[4,4,16,128]{3,2,1,0:T(8,128)}, u32[]{:S(2)}) %copy-start.1) | copy-done | bytes 131096
  50.3 8.0 %advance_and_pick.1 = (f32[4,4,4,16,128]{4,3,2,1,0:T(8,128)}, f32[48,4,128]{2,1,0:T(4,128)}) custom-call(f32[4,4,4,16,128]{4,3,2,1,0:T(8,128)S(1)} %bitcast.15, f32[4,16,128]{2,1,0:T(8,128)S(1)} %copy-done.2, f32[4,4,16,128]{3,2,1,0:T(8,128)S(1)} %copy-done.1, bf16[4,4,288,128]{3,2,1,0:T(8,128)(2,1)S(1)} %all-to-all-done.1.t_ref, ...), custom_call_target="tpu_custom_call" | custom-call | tf_op jit(solution)/shard_map/advance_and_pick/pallas_call | solution.py:220
  58.3 29.4 %all_to_all.21 = f32[48,4,128]{2,1,0:T(4,128)S(1)} all-to-all(f32[48,4,128]{2,1,0:T(4,128)} %get-tuple-element.15), channel_id=1, replica_groups=mesh['space'=48,'yhi'=4,'x'=4] {'space'}, dimensions={0} | all-to-all | bytes 196608 | tf_op jit(solution)/shard_map/all_to_all | solution.py:261
  87.7 0.7 fusion
  (8 shorter events, 0.0 us)
Async XLA Ops:
  20.6 3.9 %copy-start = (f32[1,4,16,16,128]{4,3,2,1,0:T(8,128)S(1)}, f32[1,4,16,16,128]{4,3,2,1,0:T(8,128)}, u32[]{:S(2)}) copy-start(f32[1,4,16,16,128]{4,3,2,1,0:T(8,128)} %param.6) | copy-start | bytes 1572868
  20.6 24.3 %copy-start.4 = (s32[48,1,128]{2,1,0:T(1,128)S(1)}, s32[48,1,128]{2,1,0:T(1,128)}, u32[]{:S(2)}) copy-start(s32[48,1,128]{2,1,0:T(1,128)} %param.8) | copy-start | bytes 73732
  20.6 24.3 %copy-start.5 = (s32[48,1,128]{2,1,0:T(1,128)S(1)}, s32[48,1,128]{2,1,0:T(1,128)}, u32[]{:S(2)}) copy-start(s32[48,1,128]{2,1,0:T(1,128)} %param.9) | copy-start | bytes 73732
  20.6 24.3 %copy-start.6 = (s32[48,1]{0,1:T(1,128)S(1)}, s32[48,1]{0,1:T(1,128)}, u32[]{:S(2)}) copy-start(s32[48,1]{0,1:T(1,128)} %param.10) | copy-start | bytes 580
  20.6 20.0 %all-to-all-start.1 = ((bf16[4,4,288,128]{3,2,1,0:T(8,128)(2,1)}), bf16[4,4,288,128]{3,2,1,0:T(8,128)(2,1)S(1)}, u32[]{:S(2)}, u32[]{:S(2)}) async-start(bf16[4,4,288,128]{3,2,1,0:T(8,128)(2,1)} %spread.3), calls=%async_computation.1 | async-start | bytes 2359296 | tf_op jit(solution)/shard_map/all_to_all | solution.py:246
  25.4 10.4 %collective-permute-start = (f32[8,16,128]{2,1,0:T(8,128)}, f32[8,16,128]{2,1,0:T(8,128)S(1)}, u32[]{:S(2)}, u32[]{:S(2)}) collective-permute-start(f32[8,16,128]{2,1,0:T(8,128)} %pack.1), channel_id=1, source_target_pairs={{0,16},{16,0},{32,48},{48,32},{64,80},{80,64},{96,112},{112,96},{1... | collective-permute-start | bytes 196616 | tf_op jit(solution)/shard_map/ppermute | solution.py:251
  33.8 6.1 %collective-permute-start.1 = (f32[8,16,128]{2,1,0:T(8,128)}, f32[8,16,128]{2,1,0:T(8,128)S(1)}, u32[]{:S(2)}, u32[]{:S(2)}) collective-permute-start(f32[8,16,128]{2,1,0:T(8,128)} %pack.1), channel_id=1, source_target_pairs={{0,752},{16,32},{32,16},{48,64},{64,48},{80,96},{96,80},{112,128},... | collective-permute-start | bytes 196616 | tf_op jit(solution)/shard_map/ppermute | solution.py:250
  40.6 8.8 %copy-start.2 = (f32[4,16,128]{2,1,0:T(8,128)S(1)}, f32[4,16,128]{2,1,0:T(8,128)}, u32[]{:S(2)}) copy-start(f32[4,16,128]{2,1,0:T(8,128)} %get-tuple-element.10.halo_ref) | copy-start | bytes 98308
  40.6 8.8 %all-to-all-start.2 = ((bf16[4,4,16,128]{3,2,1,0:T(8,128)(2,1)}), bf16[4,4,16,128]{3,2,1,0:T(8,128)(2,1)S(1)}, u32[]{:S(2)}, u32[]{:S(2)}) async-start(bf16[4,4,16,128]{3,2,1,0:T(8,128)(2,1)} %get-tuple-element.13.side_ref), calls=%async_computation.2 | async-start | bytes 131072 | tf_op jit(solution)/shard_map/all_to_all | solution.py:255
  45.0 42.7 %copy-start.3 = (f32[1,48,4,128]{3,2,1,0:T(4,128)S(1)}, f32[1,48,4,128]{3,2,1,0:T(4,128)}, u32[]{:S(2)}) copy-start(f32[1,48,4,128]{3,2,1,0:T(4,128)} %param.11) | copy-start | bytes 294916
  49.4 0.9 %copy-start.1 = (f32[4,4,16,128]{3,2,1,0:T(8,128)S(1)}, f32[4,4,16,128]{3,2,1,0:T(8,128)}, u32[]{:S(2)}) copy-start(f32[4,4,16,128]{3,2,1,0:T(8,128)} %advance_own.1.own_ref) | copy-start | bytes 393220

commit v8 on v7

--- a/solution.py
+++ b/solution.py
@@ -164,10 +164,12 @@
 
 
 def main_kernel(
-    p_ref, halo_ref, own_ref, t_ref, side_ref, row_ref, col_ref, out_ref, val_ref, final_ref, table_ref, sem
+    p_ref, halo_ref, own_ref, t_ref, side_ref, row_ref, col_ref, out_ref, val_ref, final_ref, table_ref, sem, own_sem
 ):
     owners = row_ref.shape[0]
     here = axis_index("x")
+    bring = pltpu.make_async_copy(own_ref, final_ref.at[:, :, here], own_sem)
+    bring.start()
 
     def one_level(i, carry):
         y, x = lax.rem(i, 4), lax.rem(here + 1 + i // 4, 4)
@@ -179,9 +181,7 @@
         return carry
 
     lax.fori_loop(0, 12, one_level, 0, unroll=2)
-    for f in range(4):
-        for y in range(4):
-            final_ref[f, y, here] = own_ref[f, y]
+    bring.wait()
     move = pltpu.make_async_copy(final_ref, out_ref, sem)
     move.start()
 
@@ -223,15 +223,16 @@
             jax.ShapeDtypeStruct(state.shape, F32),
             jax.ShapeDtypeStruct((owners, 4, 128), F32),
         ),
-        in_specs=[VMEM] * 7,
+        in_specs=[VMEM, VMEM, HBM] + [VMEM] * 4,
         out_specs=(HBM, VMEM),
         scratch_shapes=[
             pltpu.VMEM(state.shape, F32),
             pltpu.VMEM((512, 512), BF16),
             pltpu.SemaphoreType.DMA,
+            pltpu.SemaphoreType.DMA,
         ],
         name="advance_and_pick",
-    )(*map(in_vmem, (state, halo, own, planes, sides, rows, cols)))
+    )(in_vmem(state), in_vmem(halo), own, *map(in_vmem, (planes, sides, rows, cols)))
 
 
 def on_device(perturbation, trajectory, site_col, site_lev, obs_counts, obs_weights):
@@ -251,7 +252,7 @@
     near = lax.ppermute(edge, "space", pairs)
     halo, side = fill(near, far)
     own = advance_own(state, halo, first, side)
-    side, planes = lax.optimization_barrier((side, planes))
+    side, planes, own = lax.optimization_barrier((side, planes, own))
     sides = lax.all_to_all(side, "x", 0, 0, tiled=True)
 
     live = jnp.arange(slots, dtype=jnp.int32)[None, :] < obs_counts

time: 89.2 us -> 88.7 us (level)
  waiting for transfers between devices: 6.18 us -> 8.55 us
  blocking collectives: 46.6 us -> 45 us
  local copies, waits for them, and re-layouts: 0.94 us -> 0.02 us
    all_to_all x1, waiting for transfers between devices: 2.02 us -> 4.39 us  [on_device(): sides = lax.all_to_all(side, 'x', 0, 0, tiled=True)]
    all_to_all x1, blocking collectives: 29.4 us -> 27.7 us  [on_device(): received = lax.all_to_all(values, 'space', 0, 0, tiled=True)]
    unnamed x14 -> x12, local copies, waits for them, and re-layouts: 0.94 us -> 0.02 us
where the time goes in v8:
time: 88.7 us; the launch traced here: 88.1 us
  blocking collectives  45 us (51%)
  starting transfers between devices  18.5 us (21%)
  Pallas kernels  14.6 us (16%)
  waiting for transfers between devices  8.55 us (10%)
    all_to_all x1, blocking collectives, on_device(): received = lax.all_to_all(values, 'space', 0, 0, tiled=True)  27.7 us
    all_to_all x1, blocking collectives, on_device(): first = lax.all_to_all(spread(local), 'yhi', 0, 0, tiled=True)  17.3 us
    ppermute x1, starting transfers between devices, on_device(): near = lax.ppermute(edge, 'space', pairs)  8.45 us
    pallas_call x1, Pallas kernels, advance_and_pick(): pl.pallas_call(main_kernel, out_shape=(jax.ShapeDtypeStruct(state.shape,...  8.02 us
    all_to_all x1, waiting for transfers between devices, on_device(): sides = lax.all_to_all(side, 'x', 0, 0, tiled=True)  4.39 us
    all_to_all x1, starting transfers between devices, on_device(): sides = lax.all_to_all(side, 'x', 0, 0, tiled=True)  4.29 us
    ppermute x1, waiting for transfers between devices, on_device(): far = lax.ppermute(edge, 'space', crossed)  4.15 us
    all_to_all x1, starting transfers between devices, on_device(): planes = lax.all_to_all(copies, 'x', 0, 0, tiled=True)  3.89 us
  transfers between devices with their start and end apart: 4, of which 2 were waited for; matrix products, arithmetic and copies ran while one was open for 0% of the time, Pallas kernels for 4%

profile of v8, /device:TPU:1, one launch (start us, length us, event | category | flops | bytes accessed | tf_op | source)
XLA Modules:
  0.0 88.1 jit_solution(6233452972574752656)
XLA Ops:
  0.6 1.6 %spread.2 = bf16[4,288,128]{2,1,0:T(8,128)(2,1)} custom-call(bf16[288,128]{1,0:T(8,128)(2,1)} %bitcast.16), custom_call_target="tpu_custom_call" | custom-call | tf_op jit(solution)/shard_map/spread/pallas_call | solution.py:39
  2.3 17.3 %all_to_all.20.t_ref = bf16[4,288,128]{2,1,0:T(8,128)(2,1)S(1)} all-to-all(bf16[4,288,128]{2,1,0:T(8,128)(2,1)} %spread.2), channel_id=1, replica_groups=mesh['space'=48,'yhi'=4,'x'=4] {'yhi'}, dimensions={0} | all-to-all | bytes 589824 | tf_op jit(solution)/shard_map/all_to_all | solution.py:245
  19.5 1.1 %spread.3 = bf16[4,4,288,128]{3,2,1,0:T(8,128)(2,1)} custom-call(bf16[4,288,128]{2,1,0:T(8,128)(2,1)S(1)} %all_to_all.20.t_ref), custom_call_target="tpu_custom_call" | custom-call | tf_op jit(solution)/shard_map/spread/pallas_call | solution.py:39
  20.6 0.0 copy-start
  20.6 3.9 %all-to-all-start.1 = ((bf16[4,4,288,128]{3,2,1,0:T(8,128)(2,1)}), bf16[4,4,288,128]{3,2,1,0:T(8,128)(2,1)S(1)}, u32[]{:S(2)}, u32[]{:S(2)}) async-start(bf16[4,4,288,128]{3,2,1,0:T(8,128)(2,1)} %spread.3), calls=%async_computation.1 | async-start | bytes 2359296 | tf_op jit(solution)/shard_map/all_to_all | solution.py:247
  24.5 0.0 copy-done
  24.5 0.9 %pack.1 = f32[8,16,128]{2,1,0:T(8,128)} custom-call(f32[4,4,4,16,128]{4,3,2,1,0:T(8,128)S(1)} %bitcast.13, bf16[4,288,128]{2,1,0:T(8,128)(2,1)S(1)} %all_to_all.20.t_ref), custom_call_target="tpu_custom_call" | custom-call | tf_op jit(solution)/shard_map/pack/pallas_call | solution.py:66
  25.4 8.4 %collective-permute-start = (f32[8,16,128]{2,1,0:T(8,128)}, f32[8,16,128]{2,1,0:T(8,128)S(1)}, u32[]{:S(2)}, u32[]{:S(2)}) collective-permute-start(f32[8,16,128]{2,1,0:T(8,128)} %pack.1), channel_id=1, source_target_pairs={{0,16},{16,0},{32,48},{48,32},{64,80},{80,64},{96,112},{112,96},{1... | collective-permute-start | bytes 196616 | tf_op jit(solution)/shard_map/ppermute | solution.py:252
  33.9 1.9 %collective-permute-start.1 = (f32[8,16,128]{2,1,0:T(8,128)}, f32[8,16,128]{2,1,0:T(8,128)S(1)}, u32[]{:S(2)}, u32[]{:S(2)}) collective-permute-start(f32[8,16,128]{2,1,0:T(8,128)} %pack.1), channel_id=1, source_target_pairs={{0,752},{16,32},{32,16},{48,64},{64,48},{80,96},{96,80},{112,128},... | collective-permute-start | bytes 196616 | tf_op jit(solution)/shard_map/ppermute | solution.py:251
  35.8 0.0 collective-permute-done.near_ref
  35.8 4.2 %collective-permute-done.1.far_ref = f32[8,16,128]{2,1,0:T(8,128)S(1)} collective-permute-done((f32[8,16,128]{2,1,0:T(8,128)}, f32[8,16,128]{2,1,0:T(8,128)S(1)}, u32[]{:S(2)}, u32[]{:S(2)}) %collective-permute-start.1) | collective-permute-done | bytes 65568 | tf_op jit(solution)/shard_map/ppermute | solution.py:251
  39.9 0.7 fill.1
  40.6 2.3 %advance_own.1.own_ref = f32[4,4,16,128]{3,2,1,0:T(8,128)} custom-call(f32[4,4,4,16,128]{4,3,2,1,0:T(8,128)S(1)} %bitcast.14, f32[4,16,128]{2,1,0:T(8,128)} %get-tuple-element.11.halo_ref, bf16[4,288,128]{2,1,0:T(8,128)(2,1)S(1)} %all_to_all.20.t_ref, bf16[4,4,16,128]{3,2,1,0:T(8,128)(2,1)} %get-tuple-element.15.side_ref), custom_call_target="tpu_custom_call" | custom-call | tf_op jit(solution)/shard_map/advance_own/pallas_call | solution.py:157
  42.9 0.0 all-to-all-done.1.t_ref
  42.9 4.3 %all-to-all-start.2 = ((bf16[4,4,16,128]{3,2,1,0:T(8,128)(2,1)}), bf16[4,4,16,128]{3,2,1,0:T(8,128)(2,1)S(1)}, u32[]{:S(2)}, u32[]{:S(2)}) async-start(bf16[4,4,16,128]{3,2,1,0:T(8,128)(2,1)} %get-tuple-element.15.side_ref), calls=%async_computation.2 | async-start | bytes 131072 | tf_op jit(solution)/shard_map/all_to_all | solution.py:256
  47.2 0.0 copy-done.3
  47.2 0.0 copy-done.4
  47.2 0.0 copy-done.5
  47.2 0.1 add_select_fusion
  47.3 4.4 %all-to-all-done.2.side_ref = bf16[4,4,16,128]{3,2,1,0:T(8,128)(2,1)S(1)} async-done(((bf16[4,4,16,128]{3,2,1,0:T(8,128)(2,1)}), bf16[4,4,16,128]{3,2,1,0:T(8,128)(2,1)S(1)}, u32[]{:S(2)}, u32[]{:S(2)}) %all-to-all-start.2) | async-done | bytes 65568 | tf_op jit(solution)/shard_map/all_to_all | solution.py:256
  51.7 0.0 copy-done.1
  51.7 8.0 %advance_and_pick.1 = (f32[4,4,4,16,128]{4,3,2,1,0:T(8,128)}, f32[48,4,128]{2,1,0:T(4,128)}) custom-call(f32[4,4,4,16,128]{4,3,2,1,0:T(8,128)S(1)} %bitcast.15, f32[4,16,128]{2,1,0:T(8,128)S(1)} %copy-done.1, f32[4,4,16,128]{3,2,1,0:T(8,128)} %advance_own.1.own_ref, bf16[4,4,288,128]{3,2,1,0:T(8,128)(2,1)S(1)} %all-to-all-done.1.t_ref, ...), custom_call_target="tpu_custom_call" | custom-call | tf_op jit(solution)/shard_map/advance_and_pick/pallas_call | solution.py:220
  59.7 27.7 %all_to_all.21 = f32[48,4,128]{2,1,0:T(4,128)S(1)} all-to-all(f32[48,4,128]{2,1,0:T(4,128)} %get-tuple-element.17), channel_id=1, replica_groups=mesh['space'=48,'yhi'=4,'x'=4] {'space'}, dimensions={0} | all-to-all | bytes 196608 | tf_op jit(solution)/shard_map/all_to_all | solution.py:262
  87.4 0.7 fusion
  (6 shorter events, 0.0 us)
Async XLA Ops:
  20.6 3.9 %copy-start = (f32[1,4,16,16,128]{4,3,2,1,0:T(8,128)S(1)}, f32[1,4,16,16,128]{4,3,2,1,0:T(8,128)}, u32[]{:S(2)}) copy-start(f32[1,4,16,16,128]{4,3,2,1,0:T(8,128)} %param.6) | copy-start | bytes 1572868
  20.6 22.3 %all-to-all-start.1 = ((bf16[4,4,288,128]{3,2,1,0:T(8,128)(2,1)}), bf16[4,4,288,128]{3,2,1,0:T(8,128)(2,1)S(1)}, u32[]{:S(2)}, u32[]{:S(2)}) async-start(bf16[4,4,288,128]{3,2,1,0:T(8,128)(2,1)} %spread.3), calls=%async_computation.1 | async-start | bytes 2359296 | tf_op jit(solution)/shard_map/all_to_all | solution.py:247
  24.5 22.7 %copy-start.3 = (s32[48,1,128]{2,1,0:T(1,128)S(1)}, s32[48,1,128]{2,1,0:T(1,128)}, u32[]{:S(2)}) copy-start(s32[48,1,128]{2,1,0:T(1,128)} %param.8) | copy-start | bytes 73732
  24.5 22.7 %copy-start.4 = (s32[48,1,128]{2,1,0:T(1,128)S(1)}, s32[48,1,128]{2,1,0:T(1,128)}, u32[]{:S(2)}) copy-start(s32[48,1,128]{2,1,0:T(1,128)} %param.9) | copy-start | bytes 73732
  24.5 22.7 %copy-start.5 = (s32[48,1]{0,1:T(1,128)S(1)}, s32[48,1]{0,1:T(1,128)}, u32[]{:S(2)}) copy-start(s32[48,1]{0,1:T(1,128)} %param.10) | copy-start | bytes 580
  25.4 10.4 %collective-permute-start = (f32[8,16,128]{2,1,0:T(8,128)}, f32[8,16,128]{2,1,0:T(8,128)S(1)}, u32[]{:S(2)}, u32[]{:S(2)}) collective-permute-start(f32[8,16,128]{2,1,0:T(8,128)} %pack.1), channel_id=1, source_target_pairs={{0,16},{16,0},{32,48},{48,32},{64,80},{80,64},{96,112},{112,96},{1... | collective-permute-start | bytes 196616 | tf_op jit(solution)/shard_map/ppermute | solution.py:252
  33.9 6.1 %collective-permute-start.1 = (f32[8,16,128]{2,1,0:T(8,128)}, f32[8,16,128]{2,1,0:T(8,128)S(1)}, u32[]{:S(2)}, u32[]{:S(2)}) collective-permute-start(f32[8,16,128]{2,1,0:T(8,128)} %pack.1), channel_id=1, source_target_pairs={{0,752},{16,32},{32,16},{48,64},{64,48},{80,96},{96,80},{112,128},... | collective-permute-start | bytes 196616 | tf_op jit(solution)/shard_map/ppermute | solution.py:251
  40.6 11.1 %copy-start.1 = (f32[4,16,128]{2,1,0:T(8,128)S(1)}, f32[4,16,128]{2,1,0:T(8,128)}, u32[]{:S(2)}) copy-start(f32[4,16,128]{2,1,0:T(8,128)} %get-tuple-element.11.halo_ref) | copy-start | bytes 98308
  42.9 44.5 %copy-start.2 = (f32[1,48,4,128]{3,2,1,0:T(4,128)S(1)}, f32[1,48,4,128]{3,2,1,0:T(4,128)}, u32[]{:S(2)}) copy-start(f32[1,48,4,128]{3,2,1,0:T(4,128)} %param.11) | copy-start | bytes 294916
  42.9 8.8 %all-to-all-start.2 = ((bf16[4,4,16,128]{3,2,1,0:T(8,128)(2,1)}), bf16[4,4,16,128]{3,2,1,0:T(8,128)(2,1)S(1)}, u32[]{:S(2)}, u32[]{:S(2)}) async-start(bf16[4,4,16,128]{3,2,1,0:T(8,128)(2,1)} %get-tuple-element.15.side_ref), calls=%async_computation.2 | async-start | bytes 131072 | tf_op jit(solution)/shard_map/all_to_all | solution.py:256

commit v9 on v8

--- a/solution.py
+++ b/solution.py
@@ -12,6 +12,7 @@
 F32 = jnp.float32
 BF16 = jnp.bfloat16
 VMEM = pl.BlockSpec(memory_space=pltpu.VMEM)
+SMEM = pl.BlockSpec(memory_space=pltpu.SMEM)
 HBM = pl.BlockSpec(memory_space=pltpu.HBM)
 TILE = (16, 128)
 
@@ -77,21 +78,21 @@
     return jnp.where((lane_of(near.shape) % 8 < 3) == (odd == 1), near, far)
 
 
-def fill_kernel(near_ref, far_ref, halo_ref, side_ref):
+def fill_kernel(far_ref, near_ref, halo_ref, side_ref):
     edge = merge(near_ref[...], far_ref[...])
     halo_ref[...] = edge[0:4]
     for i in range(4):
         side_ref[i] = edge[4:8].astype(BF16)
 
 
-def fill(near, far):
+def fill(far, near):
     return pl.pallas_call(
         fill_kernel,
         out_shape=(jax.ShapeDtypeStruct((4,) + TILE, F32), jax.ShapeDtypeStruct((4, 4) + TILE, BF16)),
         in_specs=[VMEM, VMEM],
         out_specs=(VMEM, VMEM),
         name="fill",
-    )(in_vmem(near), in_vmem(far))
+    )(in_vmem(far), in_vmem(near))
 
 
 def weights_of(planes, first, last):
@@ -164,7 +165,7 @@
 
 
 def main_kernel(
-    p_ref, halo_ref, own_ref, t_ref, side_ref, row_ref, col_ref, out_ref, val_ref, final_ref, table_ref, sem, own_sem
+    p_ref, halo_ref, own_ref, t_ref, side_ref, row_ref, col_ref, count_ref, out_ref, val_ref, final_ref, table_ref, list_ref, sem, own_sem
 ):
     owners = row_ref.shape[0]
     here = axis_index("x")
@@ -195,27 +196,58 @@
 
     line = lax.broadcasted_iota(jnp.int32, (256, 128), 0)
     lon = lax.broadcasted_iota(jnp.int32, (128, 128), 0)
-
-    def four_owners(i, carry):
-        picks = []
-        for o in range(4):
-            hit = line == row_ref[pl.ds(4 * i + o, 1), :]
-            picks.append(jnp.where(hit, 1.0, 0.0).astype(BF16))
+    low_lanes = lane_of((1, 128)) < 64
+
+    def halves(ref, a, b, second):
+        one, two = ref[pl.ds(a, 1), :], ref[pl.ds(b, 1), :]
+        if second:
+            one = pltpu.roll(one, 64, 1)
+        else:
+            two = pltpu.roll(two, 64, 1)
+        return jnp.where(low_lanes, one, two)
+
+    def eight_owners(owners, second):
+        pairs = [(owners[2 * i], owners[2 * i + 1]) for i in range(4)]
+        picks = [jnp.where(line == halves(row_ref, a, b, second), 1.0, 0.0).astype(BF16) for a, b in pairs]
         pick = jnp.concatenate(picks, axis=1)
         pick = jnp.concatenate([pick, pick], axis=0)
         lines = jnp.dot(table_ref[...], pick, preferred_element_type=F32)
-        for o in range(4):
-            hit = lon == col_ref[pl.ds(4 * i + o, 1), :]
+        for i, (a, b) in enumerate(pairs):
+            hit = lon == halves(col_ref, a, b, second)
+            values = []
             for f in range(4):
-                part = lines[f * 128 : f * 128 + 128, o * 128 : o * 128 + 128]
-                val_ref[4 * i + o, f : f + 1, :] = jnp.sum(jnp.where(hit, part, 0.0), axis=0, keepdims=True)
+                part = lines[f * 128 : f * 128 + 128, i * 128 : i * 128 + 128]
+                values.append(jnp.sum(jnp.where(hit, part, 0.0), axis=0, keepdims=True))
+            values = jnp.concatenate(values, axis=0)
+            turned = pltpu.roll(values, 64, 1)
+            if second:
+                val_ref[a, :, 64:128] = turned[:, 64:128]
+                val_ref[b, :, 64:128] = values[:, 64:128]
+            else:
+                val_ref[a, :, 0:64] = values[:, 0:64]
+                val_ref[b, :, 0:64] = turned[:, 0:64]
+
+    def note(o, found):
+        list_ref[found] = o
+        return found + (count_ref[o] > 64).astype(jnp.int32)
+
+    found = lax.fori_loop(0, owners, note, 0)
+    last = list_ref[jnp.maximum(found - 1, 0)]
+    for i in range(7):
+        list_ref[found + i] = last
+    val_ref[...] = jnp.zeros(val_ref.shape, F32)
+    for i in range(owners // 8):
+        eight_owners([8 * i + o for o in range(8)], False)
+
+    def second_halves(i, carry):
+        eight_owners([list_ref[8 * i + o] for o in range(8)], True)
         return carry
 
-    lax.fori_loop(0, owners // 4, four_owners, 0, unroll=2)
+    lax.fori_loop(0, (found + 7) // 8, second_halves, 0)
     move.wait()
 
 
-def advance_and_pick(state, halo, own, planes, sides, rows, cols):
+def advance_and_pick(state, halo, own, planes, sides, rows, cols, counts):
     owners = rows.shape[0]
     return pl.pallas_call(
         main_kernel,
@@ -223,16 +255,17 @@
             jax.ShapeDtypeStruct(state.shape, F32),
             jax.ShapeDtypeStruct((owners, 4, 128), F32),
         ),
-        in_specs=[VMEM, VMEM, HBM] + [VMEM] * 4,
+        in_specs=[VMEM, VMEM, HBM] + [VMEM] * 4 + [SMEM],
         out_specs=(HBM, VMEM),
         scratch_shapes=[
             pltpu.VMEM(state.shape, F32),
             pltpu.VMEM((512, 512), BF16),
+            pltpu.SMEM((owners + 8,), jnp.int32),
             pltpu.SemaphoreType.DMA,
             pltpu.SemaphoreType.DMA,
         ],
         name="advance_and_pick",
-    )(in_vmem(state), in_vmem(halo), own, *map(in_vmem, (planes, sides, rows, cols)))
+    )(in_vmem(state), in_vmem(halo), own, *map(in_vmem, (planes, sides, rows, cols)), counts)
 
 
 def on_device(perturbation, trajectory, site_col, site_lev, obs_counts, obs_weights):
@@ -250,7 +283,7 @@
     edge = pack(state, late)
     far = lax.ppermute(edge, "space", crossed)
     near = lax.ppermute(edge, "space", pairs)
-    halo, side = fill(near, far)
+    halo, side = fill(far, near)
     own = advance_own(state, halo, first, side)
     side, planes, own = lax.optimization_barrier((side, planes, own))
     sides = lax.all_to_all(side, "x", 0, 0, tiled=True)
@@ -258,7 +291,7 @@
     live = jnp.arange(slots, dtype=jnp.int32)[None, :] < obs_counts
     rows = jnp.where(live, site_lev[:, 0, :] * 16 + site_col[:, 0, :] // 128, -1)
     cols = site_col[:, 0, :] % 128
-    final, values = advance_and_pick(state, halo, own, planes, sides, rows, cols)
+    final, values = advance_and_pick(state, halo, own, planes, sides, rows, cols, obs_counts[:, 0])
     received = lax.all_to_all(values, "space", 0, 0, tiled=True)
     summed = jnp.sum(obs_weights[0] * received, axis=1)
     return (final.reshape(perturbation.shape), summed.reshape(1, 1, tiles, slots))

time: 88.7 us -> 88 us (level)
  starting transfers between devices: 18.5 us -> 25.1 us
  blocking collectives: 45 us -> 40.7 us
  waiting for transfers between devices: 8.55 us -> 5.47 us
    ppermute x1, starting transfers between devices: 1.92 us -> 6.46 us  [on_device(): far = lax.ppermute(edge, 'space', crossed)]
    all_to_all x1, blocking collectives: 27.7 us -> 23.5 us  [on_device(): received = lax.all_to_all(values, 'space', 0, 0, tiled=True)]
    ppermute x1, waiting for transfers between devices: 4.15 us -> 0.01 us  [on_device(): far = lax.ppermute(edge, 'space', crossed)]
    ppermute x1, starting transfers between devices: 8.45 us -> 10.4 us  [on_device(): near = lax.ppermute(edge, 'space', pairs)]
    ppermute x1, waiting for transfers between devices: 0.01 us -> 1.08 us  [on_device(): near = lax.ppermute(edge, 'space', pairs)]
where the time goes in v9:
time: 88 us; the launch traced here: 87.2 us
  blocking collectives  40.7 us (46%)
  starting transfers between devices  25.1 us (29%)
  Pallas kernels  14.4 us (16%)
  waiting for transfers between devices  5.47 us (6%)
    all_to_all x1, blocking collectives, on_device(): received = lax.all_to_all(values, 'space', 0, 0, tiled=True)  23.5 us
    all_to_all x1, blocking collectives, on_device(): first = lax.all_to_all(spread(local), 'yhi', 0, 0, tiled=True)  17.3 us
    ppermute x1, starting transfers between devices, on_device(): near = lax.ppermute(edge, 'space', pairs)  10.4 us
    pallas_call x1, Pallas kernels, advance_and_pick(): pl.pallas_call(main_kernel, out_shape=(jax.ShapeDtypeStruct(state.shape,...  7.85 us
    ppermute x1, starting transfers between devices, on_device(): far = lax.ppermute(edge, 'space', crossed)  6.46 us
    all_to_all x1, waiting for transfers between devices, on_device(): sides = lax.all_to_all(side, 'x', 0, 0, tiled=True)  4.39 us
    all_to_all x1, starting transfers between devices, on_device(): sides = lax.all_to_all(side, 'x', 0, 0, tiled=True)  4.36 us
    all_to_all x1, starting transfers between devices, on_device(): planes = lax.all_to_all(copies, 'x', 0, 0, tiled=True)  3.89 us
  transfers between devices with their start and end apart: 4, of which 2 were waited for; matrix products, arithmetic and copies ran while one was open for 0% of the time, Pallas kernels for 4%

profile of v9, /device:TPU:1, one launch (start us, length us, event | category | flops | bytes accessed | tf_op | source)
XLA Modules:
  0.0 87.2 jit_solution(12359890016381100757)
XLA Ops:
  0.6 1.6 %spread.2 = bf16[4,288,128]{2,1,0:T(8,128)(2,1)} custom-call(bf16[288,128]{1,0:T(8,128)(2,1)} %bitcast.16), custom_call_target="tpu_custom_call" | custom-call | tf_op jit(solution)/shard_map/spread/pallas_call | solution.py:40
  2.3 17.3 %all_to_all.20.t_ref = bf16[4,288,128]{2,1,0:T(8,128)(2,1)S(1)} all-to-all(bf16[4,288,128]{2,1,0:T(8,128)(2,1)} %spread.2), channel_id=1, replica_groups=mesh['space'=48,'yhi'=4,'x'=4] {'yhi'}, dimensions={0} | all-to-all | bytes 589824 | tf_op jit(solution)/shard_map/all_to_all | solution.py:278
  19.5 1.1 %spread.3 = bf16[4,4,288,128]{3,2,1,0:T(8,128)(2,1)} custom-call(bf16[4,288,128]{2,1,0:T(8,128)(2,1)S(1)} %all_to_all.20.t_ref), custom_call_target="tpu_custom_call" | custom-call | tf_op jit(solution)/shard_map/spread/pallas_call | solution.py:40
  20.6 0.0 copy-start
  20.6 3.9 %all-to-all-start.1 = ((bf16[4,4,288,128]{3,2,1,0:T(8,128)(2,1)}), bf16[4,4,288,128]{3,2,1,0:T(8,128)(2,1)S(1)}, u32[]{:S(2)}, u32[]{:S(2)}) async-start(bf16[4,4,288,128]{3,2,1,0:T(8,128)(2,1)} %spread.3), calls=%async_computation.1 | async-start | bytes 2359296 | tf_op jit(solution)/shard_map/all_to_all | solution.py:280
  24.5 0.0 copy-done
  24.5 0.9 %pack.1 = f32[8,16,128]{2,1,0:T(8,128)} custom-call(f32[4,4,4,16,128]{4,3,2,1,0:T(8,128)S(1)} %bitcast.13, bf16[4,288,128]{2,1,0:T(8,128)(2,1)S(1)} %all_to_all.20.t_ref), custom_call_target="tpu_custom_call" | custom-call | tf_op jit(solution)/shard_map/pack/pallas_call | solution.py:67
  25.4 6.5 %collective-permute-start = (f32[8,16,128]{2,1,0:T(8,128)}, f32[8,16,128]{2,1,0:T(8,128)S(1)}, u32[]{:S(2)}, u32[]{:S(2)}) collective-permute-start(f32[8,16,128]{2,1,0:T(8,128)} %pack.1), channel_id=1, source_target_pairs={{0,752},{16,32},{32,16},{48,64},{64,48},{80,96},{96,80},{112,128},... | collective-permute-start | bytes 196616 | tf_op jit(solution)/shard_map/ppermute | solution.py:284
  31.9 10.4 %collective-permute-start.1 = (f32[8,16,128]{2,1,0:T(8,128)}, f32[8,16,128]{2,1,0:T(8,128)S(1)}, u32[]{:S(2)}, u32[]{:S(2)}) collective-permute-start(f32[8,16,128]{2,1,0:T(8,128)} %pack.1), channel_id=1, source_target_pairs={{0,16},{16,0},{32,48},{48,32},{64,80},{80,64},{96,112},{112,96},{1... | collective-permute-start | bytes 196616 | tf_op jit(solution)/shard_map/ppermute | solution.py:285
  42.3 0.0 collective-permute-done.far_ref
  42.3 1.1 %collective-permute-done.1.near_ref = f32[8,16,128]{2,1,0:T(8,128)S(1)} collective-permute-done((f32[8,16,128]{2,1,0:T(8,128)}, f32[8,16,128]{2,1,0:T(8,128)S(1)}, u32[]{:S(2)}, u32[]{:S(2)}) %collective-permute-start.1) | collective-permute-done | bytes 65568 | tf_op jit(solution)/shard_map/ppermute | solution.py:285
  43.4 0.7 fill.1
  44.1 2.3 %advance_own.1.own_ref = f32[4,4,16,128]{3,2,1,0:T(8,128)} custom-call(f32[4,4,4,16,128]{4,3,2,1,0:T(8,128)S(1)} %bitcast.14, f32[4,16,128]{2,1,0:T(8,128)} %get-tuple-element.11.halo_ref, bf16[4,288,128]{2,1,0:T(8,128)(2,1)S(1)} %all_to_all.20.t_ref, bf16[4,4,16,128]{3,2,1,0:T(8,128)(2,1)} %get-tuple-element.15.side_ref), custom_call_target="tpu_custom_call" | custom-call | tf_op jit(solution)/shard_map/advance_own/pallas_call | solution.py:158
  46.4 0.0 all-to-all-done.1.t_ref
  46.4 4.4 %all-to-all-start.2 = ((bf16[4,4,16,128]{3,2,1,0:T(8,128)(2,1)}), bf16[4,4,16,128]{3,2,1,0:T(8,128)(2,1)S(1)}, u32[]{:S(2)}, u32[]{:S(2)}) async-start(bf16[4,4,16,128]{3,2,1,0:T(8,128)(2,1)} %get-tuple-element.15.side_ref), calls=%async_computation.2 | async-start | bytes 131072 | tf_op jit(solution)/shard_map/all_to_all | solution.py:289
  50.8 0.0 copy-done.3
  50.8 0.0 copy-done.4
  50.8 0.0 copy-done.5
  50.8 0.1 add_select_fusion
  50.8 4.4 %all-to-all-done.2.side_ref = bf16[4,4,16,128]{3,2,1,0:T(8,128)(2,1)S(1)} async-done(((bf16[4,4,16,128]{3,2,1,0:T(8,128)(2,1)}), bf16[4,4,16,128]{3,2,1,0:T(8,128)(2,1)S(1)}, u32[]{:S(2)}, u32[]{:S(2)}) %all-to-all-start.2) | async-done | bytes 65568 | tf_op jit(solution)/shard_map/all_to_all | solution.py:289
  55.2 0.0 copy-done.1
  55.2 7.9 %advance_and_pick.1 = (f32[4,4,4,16,128]{4,3,2,1,0:T(8,128)}, f32[48,4,128]{2,1,0:T(4,128)}) custom-call(f32[4,4,4,16,128]{4,3,2,1,0:T(8,128)S(1)} %bitcast.15, f32[4,16,128]{2,1,0:T(8,128)S(1)} %copy-done.1, f32[4,4,16,128]{3,2,1,0:T(8,128)} %advance_own.1.own_ref, bf16[4,4,288,128]{3,2,1,0:T(8,128)(2,1)S(1)} %all-to-all-done.1.t_ref, ...), custom_call_target="tpu_custom_call" | custom-call | tf_op jit(solution)/shard_map/advance_and_pick/pallas_call | solution.py:252
  63.1 23.5 %all_to_all.21 = f32[48,4,128]{2,1,0:T(4,128)S(1)} all-to-all(f32[48,4,128]{2,1,0:T(4,128)} %get-tuple-element.17), channel_id=1, replica_groups=mesh['space'=48,'yhi'=4,'x'=4] {'space'}, dimensions={0} | all-to-all | bytes 196608 | tf_op jit(solution)/shard_map/all_to_all | solution.py:295
  86.6 0.7 fusion
  (6 shorter events, 0.0 us)
Async XLA Ops:
  20.6 3.9 %copy-start = (f32[1,4,16,16,128]{4,3,2,1,0:T(8,128)S(1)}, f32[1,4,16,16,128]{4,3,2,1,0:T(8,128)}, u32[]{:S(2)}) copy-start(f32[1,4,16,16,128]{4,3,2,1,0:T(8,128)} %param.6) | copy-start | bytes 1572868
  20.6 25.8 %all-to-all-start.1 = ((bf16[4,4,288,128]{3,2,1,0:T(8,128)(2,1)}), bf16[4,4,288,128]{3,2,1,0:T(8,128)(2,1)S(1)}, u32[]{:S(2)}, u32[]{:S(2)}) async-start(bf16[4,4,288,128]{3,2,1,0:T(8,128)(2,1)} %spread.3), calls=%async_computation.1 | async-start | bytes 2359296 | tf_op jit(solution)/shard_map/all_to_all | solution.py:280
  24.5 26.3 %copy-start.3 = (s32[48,1,128]{2,1,0:T(1,128)S(1)}, s32[48,1,128]{2,1,0:T(1,128)}, u32[]{:S(2)}) copy-start(s32[48,1,128]{2,1,0:T(1,128)} %param.8) | copy-start | bytes 73732
  24.5 26.3 %copy-start.4 = (s32[48,1,128]{2,1,0:T(1,128)S(1)}, s32[48,1,128]{2,1,0:T(1,128)}, u32[]{:S(2)}) copy-start(s32[48,1,128]{2,1,0:T(1,128)} %param.9) | copy-start | bytes 73732
  24.5 26.3 %copy-start.5 = (s32[48,1]{0,1:T(1,128)S(1)}, s32[48,1]{0,1:T(1,128)}, u32[]{:S(2)}) copy-start(s32[48,1]{0,1:T(1,128)} %param.10) | copy-start | bytes 580
  25.4 16.9 %collective-permute-start = (f32[8,16,128]{2,1,0:T(8,128)}, f32[8,16,128]{2,1,0:T(8,128)S(1)}, u32[]{:S(2)}, u32[]{:S(2)}) collective-permute-start(f32[8,16,128]{2,1,0:T(8,128)} %pack.1), channel_id=1, source_target_pairs={{0,752},{16,32},{32,16},{48,64},{64,48},{80,96},{96,80},{112,128},... | collective-permute-start | bytes 196616 | tf_op jit(solution)/shard_map/ppermute | solution.py:284
  31.9 11.5 %collective-permute-start.1 = (f32[8,16,128]{2,1,0:T(8,128)}, f32[8,16,128]{2,1,0:T(8,128)S(1)}, u32[]{:S(2)}, u32[]{:S(2)}) collective-permute-start(f32[8,16,128]{2,1,0:T(8,128)} %pack.1), channel_id=1, source_target_pairs={{0,16},{16,0},{32,48},{48,32},{64,80},{80,64},{96,112},{112,96},{1... | collective-permute-start | bytes 196616 | tf_op jit(solution)/shard_map/ppermute | solution.py:285
  44.1 11.2 %copy-start.1 = (f32[4,16,128]{2,1,0:T(8,128)S(1)}, f32[4,16,128]{2,1,0:T(8,128)}, u32[]{:S(2)}) copy-start(f32[4,16,128]{2,1,0:T(8,128)} %get-tuple-element.11.halo_ref) | copy-start | bytes 98308
  46.4 40.2 %copy-start.2 = (f32[1,48,4,128]{3,2,1,0:T(4,128)S(1)}, f32[1,48,4,128]{3,2,1,0:T(4,128)}, u32[]{:S(2)}) copy-start(f32[1,48,4,128]{3,2,1,0:T(4,128)} %param.11) | copy-start | bytes 294916
  46.4 8.8 %all-to-all-start.2 = ((bf16[4,4,16,128]{3,2,1,0:T(8,128)(2,1)}), bf16[4,4,16,128]{3,2,1,0:T(8,128)(2,1)S(1)}, u32[]{:S(2)}, u32[]{:S(2)}) async-start(bf16[4,4,16,128]{3,2,1,0:T(8,128)(2,1)} %get-tuple-element.15.side_ref), calls=%async_computation.2 | async-start | bytes 131072 | tf_op jit(solution)/shard_map/all_to_all | solution.py:289

commit v10 on v6

--- a/solution.py
+++ b/solution.py
@@ -74,7 +74,7 @@
     return jnp.where((lane_of(near.shape) % 8 < 3) == (odd == 1), near, far)
 
 
-def fill_kernel(near_ref, far_ref, c_in, c_ref, side_ref, sem):
+def fill_kernel(far_ref, near_ref, c_in, c_ref, side_ref, sem):
     edge = merge(near_ref[...].astype(F32), far_ref[...].astype(F32)).astype(BF16)
     for i in range(4):
         side_ref[i] = edge
@@ -87,7 +87,7 @@
     return pltpu.with_memory_space_constraint(x, pltpu.VMEM)
 
 
-def fill(near, far, copies):
+def fill(far, near, copies):
     return pl.pallas_call(
         fill_kernel,
         out_shape=jax.ShapeDtypeStruct(copies.shape, BF16),
@@ -96,7 +96,7 @@
         scratch_shapes=[pltpu.VMEM((4,) + TILE, BF16), pltpu.SemaphoreType.DMA],
         input_output_aliases={2: 0},
         name="fill",
-    )(in_vmem(near), in_vmem(far), copies)
+    )(in_vmem(far), in_vmem(near), copies)
 
 
 def pack_kernel(p_ref, edge_ref):
@@ -157,24 +157,59 @@
     return state
 
 
-def main_kernel(p_ref, near_ref, far_ref, t_ref, row_ref, col_ref, out_ref, val_ref, edge_ref, final_ref, table_ref, sem):
+def advance_at(y, x, p_ref, halo_ref, planes):
+    shift = lax.rem(253 - (4 * y + x) * 8, 128)
+    return advance_level(
+        lambda i: planes[i * 16 : i * 16 + 16, :].astype(F32),
+        planes[288:304, :].astype(F32),
+        [p_ref[f, y, x] for f in range(4)],
+        [pltpu.roll(halo_ref[f], shift, 1) for f in range(4)],
+    )
+
+
+def own_kernel(far_ref, near_ref, p_ref, t_ref, out_ref, halo_ref):
+    x = axis_index("x")
+    halo_ref[...] = merge(near_ref[...], far_ref[...])
+
+    def one_level(y, carry):
+        state = advance_at(y, x, p_ref, halo_ref, t_ref.at[y])
+        for f in range(4):
+            out_ref[f, y] = state[f]
+        return carry
+
+    lax.fori_loop(0, 4, one_level, 0, unroll=2)
+
+
+def advance_own(far, near, state, planes):
+    return pl.pallas_call(
+        own_kernel,
+        out_shape=jax.ShapeDtypeStruct((4, 4) + TILE, F32),
+        in_specs=[VMEM] * 4,
+        out_specs=VMEM,
+        scratch_shapes=[pltpu.VMEM((4,) + TILE, F32)],
+        name="advance_own",
+    )(in_vmem(far), in_vmem(near), in_vmem(state), in_vmem(planes))
+
+
+def main_kernel(
+    far_ref, near_ref, p_ref, own_ref, t_ref, row_ref, col_ref,
+    out_ref, val_ref, halo_ref, final_ref, table_ref, sem, own_sem,
+):
     owners = row_ref.shape[0]
-    edge_ref[...] = merge(near_ref[...], far_ref[...])
-
-    def one_level(level, carry):
-        y, x = level // 4, lax.rem(level, 4)
-        shift = lax.rem(253 - level * 8, 128)
-        state = advance_level(
-            lambda i: t_ref[x, y, i * 16 : i * 16 + 16, :].astype(F32),
-            t_ref[x, y, 288:304, :].astype(F32),
-            [p_ref[f, y, x] for f in range(4)],
-            [pltpu.roll(edge_ref[f], shift, 1) for f in range(4)],
-        )
+    halo_ref[...] = merge(near_ref[...], far_ref[...])
+    here = axis_index("x")
+    bring = pltpu.make_async_copy(own_ref, final_ref.at[:, :, here], own_sem)
+    bring.start()
+
+    def one_level(i, carry):
+        y, x = lax.rem(i, 4), lax.rem(here + 1 + i // 4, 4)
+        state = advance_at(y, x, p_ref, halo_ref, t_ref.at[x, y])
         for f in range(4):
             final_ref[f, y, x] = state[f]
         return carry
 
-    lax.fori_loop(0, 16, one_level, 0, unroll=2)
+    lax.fori_loop(0, 12, one_level, 0, unroll=2)
+    bring.wait()
     move = pltpu.make_async_copy(final_ref, out_ref, sem)
     move.start()
 
@@ -204,11 +239,11 @@
                 val_ref[4 * i + o, f : f + 1, :] = jnp.sum(jnp.where(hit, part, 0.0), axis=0, keepdims=True)
         return carry
 
-    lax.fori_loop(0, owners // 4, four_owners, 0, unroll=2)
+    lax.fori_loop(0, owners // 4, four_owners, 0, unroll=6)
     move.wait()
 
 
-def advance_and_pick(state, near, far, planes, rows, cols):
+def advance_and_pick(far, near, state, own, planes, rows, cols):
     owners = rows.shape[0]
     return pl.pallas_call(
         main_kernel,
@@ -216,16 +251,17 @@
             jax.ShapeDtypeStruct(state.shape, F32),
             jax.ShapeDtypeStruct((owners, 4, 128), F32),
         ),
-        in_specs=[VMEM] * 6,
+        in_specs=[VMEM, VMEM, VMEM, HBM] + [VMEM] * 3,
         out_specs=(HBM, VMEM),
         scratch_shapes=[
             pltpu.VMEM((4,) + TILE, F32),
             pltpu.VMEM(state.shape, F32),
             pltpu.VMEM((512, 512), BF16),
             pltpu.SemaphoreType.DMA,
+            pltpu.SemaphoreType.DMA,
         ],
         name="advance_and_pick",
-    )(in_vmem(state), in_vmem(near), in_vmem(far), in_vmem(planes), in_vmem(rows), in_vmem(cols))
+    )(in_vmem(far), in_vmem(near), in_vmem(state), own, *map(in_vmem, (planes, rows, cols)))
 
 
 def on_device(perturbation, trajectory, site_col, site_lev, obs_counts, obs_weights):
@@ -238,19 +274,21 @@
     copies, edge = send(local)
     far = lax.ppermute(edge, "space", crossed)
     near = lax.ppermute(edge, "space", pairs)
-    copies = fill(near, far, copies)
-    planes = lax.all_to_all(copies, "yhi", 0, 0, tiled=True)
+    copies = fill(far, near, copies)
+    first = lax.all_to_all(copies, "yhi", 0, 0, tiled=True)
+    copies = spread(first)
+    planes = lax.all_to_all(copies, "x", 0, 0, tiled=True)
 
     late, _ = lax.optimization_barrier((state, copies))
     edge = pack(late)
     far = lax.ppermute(edge, "space", crossed)
     near = lax.ppermute(edge, "space", pairs)
-    planes = lax.all_to_all(spread(planes), "x", 0, 0, tiled=True)
+    own = advance_own(far, near, state, first)
 
     live = jnp.arange(slots, dtype=jnp.int32)[None, :] < obs_counts
     rows = jnp.where(live, site_lev[:, 0, :] * 16 + site_col[:, 0, :] // 128, -1)
     cols = site_col[:, 0, :] % 128
-    final, values = advance_and_pick(state, near, far, planes, rows, cols)
+    final, values = advance_and_pick(far, near, state, own, planes, rows, cols)
     received = lax.all_to_all(values, "space", 0, 0, tiled=True)
     summed = jnp.sum(obs_weights[0] * received, axis=1)
     return (final.reshape(perturbation.shape), summed.reshape(1, 1, tiles, slots))

time: 92.6 us -> 90.2 us (0.974)
  waiting for transfers between devices: 6.91 us -> 3.52 us
  starting transfers between devices: 29.7 us -> 31.6 us
  blocking collectives: 40.4 us -> 39.4 us
    ppermute x2, waiting for transfers between devices: 6.9 us -> 0.01 us  [on_device(): far = lax.ppermute(edge, 'space', crossed)]
    all_to_all x1, blocking collectives: 28 us -> 24.1 us  [on_device(): received = lax.all_to_all(values, 'space', 0, 0, tiled=True)]
    all_to_all x1, blocking collectives: 12.4 us -> 15.3 us  [on_device(): first = lax.all_to_all(copies, 'yhi', 0, 0, tiled=True)]
    ppermute x2, starting transfers between devices: 3.84 us -> 6.5 us  [on_device(): far = lax.ppermute(edge, 'space', crossed)]
    ppermute x2, waiting for transfers between devices: 0.01 us -> 1.94 us  [on_device(): near = lax.ppermute(edge, 'space', pairs)]
    all_to_all x1, waiting for transfers between devices: 0.01 us -> 1.57 us  [on_device(): planes = lax.all_to_all(copies, 'x', 0, 0, tiled=True)]
    pallas_call x0 -> x1, Pallas kernels: none -> 1.48 us  [advance_own(): pl.pallas_call(own_kernel, out_shape=jax.ShapeDtypeStruct((4, 4) + TILE,...]
    pallas_call x1, Pallas kernels: 8.79 us -> 7.36 us  [advance_and_pick(): pl.pallas_call(main_kernel, out_shape=(jax.ShapeDtypeStruct(state.shape,...]
  transfers between devices with their start and end apart: 5 -> 5, of which waited for: 2 -> 3; matrix products, arithmetic and copies ran while one was open for 0% -> 0% of each run, Pallas kernels for 1% -> 3%
where the time goes in v10:
time: 90.2 us; the launch traced here: 89.7 us
  blocking collectives  39.4 us (44%)
  starting transfers between devices  31.6 us (35%)
  Pallas kernels  13.6 us (15%)
  waiting for transfers between devices  3.52 us (4%)
    all_to_all x1, blocking collectives, on_device(): received = lax.all_to_all(values, 'space', 0, 0, tiled=True)  24.1 us
    ppermute x2, starting transfers between devices, on_device(): near = lax.ppermute(edge, 'space', pairs)  21 us
    all_to_all x1, blocking collectives, on_device(): first = lax.all_to_all(copies, 'yhi', 0, 0, tiled=True)  15.3 us
    pallas_call x1, Pallas kernels, advance_and_pick(): pl.pallas_call(main_kernel, out_shape=(jax.ShapeDtypeStruct(state.shape,...  7.36 us
    ppermute x2, starting transfers between devices, on_device(): far = lax.ppermute(edge, 'space', crossed)  6.5 us
    all_to_all x1, starting transfers between devices, on_device(): planes = lax.all_to_all(copies, 'x', 0, 0, tiled=True)  4.16 us
    pallas_call x1, Pallas kernels, send(): pl.pallas_call(send_kernel, out_shape=(jax.ShapeDtypeStruct((4, 304, 128)...  2.21 us
    ppermute x2, waiting for transfers between devices, on_device(): near = lax.ppermute(edge, 'space', pairs)  1.94 us
  transfers between devices with their start and end apart: 5, of which 3 were waited for; matrix products, arithmetic and copies ran while one was open for 0% of the time, Pallas kernels for 3%

profile of v10, /device:TPU:1, one launch (start us, length us, event | category | flops | bytes accessed | tf_op | source)
XLA Modules:
  0.0 89.7 jit_solution(1619007444607957249)
XLA Ops:
  0.6 2.2 %send.1 = (bf16[4,304,128]{2,1,0:T(8,128)(2,1)}, bf16[16,128]{1,0:T(8,128)(2,1)}) custom-call(bf16[288,128]{1,0:T(8,128)(2,1)} %bitcast.16), custom_call_target="tpu_custom_call" | custom-call | tf_op jit(solution)/shard_map/send/pallas_call | solution.py:43
  2.9 4.6 %collective-permute-start = (bf16[16,128]{1,0:T(8,128)(2,1)}, bf16[16,128]{1,0:T(8,128)(2,1)S(1)}, u32[]{:S(2)}, u32[]{:S(2)}) collective-permute-start(bf16[16,128]{1,0:T(8,128)(2,1)} %get-tuple-element.7), channel_id=1, source_target_pairs={{0,752},{16,32},{32,16},{48,64},{64,48},{80,96},{96,80},{112,128},... | collective-permute-start | bytes 12296 | tf_op jit(solution)/shard_map/ppermute | solution.py:275
  7.5 13.9 %collective-permute-start.1 = (bf16[16,128]{1,0:T(8,128)(2,1)}, bf16[16,128]{1,0:T(8,128)(2,1)S(1)}, u32[]{:S(2)}, u32[]{:S(2)}) collective-permute-start(bf16[16,128]{1,0:T(8,128)(2,1)} %get-tuple-element.7), channel_id=1, source_target_pairs={{0,16},{16,0},{32,48},{48,32},{64,80},{80,64},{96,112},{112,96},{1... | collective-permute-start | bytes 12296 | tf_op jit(solution)/shard_map/ppermute | solution.py:276
  21.3 0.0 collective-permute-done.far_ref
  21.3 1.0 %collective-permute-done.1.near_ref = bf16[16,128]{1,0:T(8,128)(2,1)S(1)} collective-permute-done((bf16[16,128]{1,0:T(8,128)(2,1)}, bf16[16,128]{1,0:T(8,128)(2,1)S(1)}, u32[]{:S(2)}, u32[]{:S(2)}) %collective-permute-start.1) | collective-permute-done | bytes 4128 | tf_op jit(solution)/shard_map/ppermute | solution.py:276
  22.3 0.6 fill.1
  23.0 15.3 %all_to_all.15.t_ref = bf16[4,304,128]{2,1,0:T(8,128)(2,1)S(1)} all-to-all(bf16[4,304,128]{2,1,0:T(8,128)(2,1)} %fill.1), channel_id=1, replica_groups=mesh['space'=48,'yhi'=4,'x'=4] {'yhi'}, dimensions={0} | all-to-all | bytes 622592 | tf_op jit(solution)/shard_map/all_to_all | solution.py:278
  38.3 1.1 %spread.1 = bf16[4,4,304,128]{3,2,1,0:T(8,128)(2,1)} custom-call(bf16[4,304,128]{2,1,0:T(8,128)(2,1)S(1)} %all_to_all.15.t_ref), custom_call_target="tpu_custom_call" | custom-call | tf_op jit(solution)/shard_map/spread/pallas_call | solution.py:62
  39.4 0.0 copy-start
  39.4 0.0 copy-start.2
  39.4 0.0 copy-start.3
  39.4 0.0 copy-start.4
  39.4 4.2 %all-to-all-start.1 = ((bf16[4,4,304,128]{3,2,1,0:T(8,128)(2,1)}), bf16[4,4,304,128]{3,2,1,0:T(8,128)(2,1)S(1)}, u32[]{:S(2)}, u32[]{:S(2)}) async-start(bf16[4,4,304,128]{3,2,1,0:T(8,128)(2,1)} %spread.1), calls=%async_computation.1 | async-start | bytes 2490368 | tf_op jit(solution)/shard_map/all_to_all | solution.py:280
  43.6 0.8 pack.1
  44.4 1.9 %collective-permute-start.2 = (f32[4,16,128]{2,1,0:T(8,128)}, f32[4,16,128]{2,1,0:T(8,128)S(1)}, u32[]{:S(2)}, u32[]{:S(2)}) collective-permute-start(f32[4,16,128]{2,1,0:T(8,128)} %pack.1), channel_id=1, source_target_pairs={{0,752},{16,32},{32,16},{48,64},{64,48},{80,96},{96,80},{112,128},... | collective-permute-start | bytes 98312 | tf_op jit(solution)/shard_map/ppermute | solution.py:284
  46.3 7.1 %collective-permute-start.3 = (f32[4,16,128]{2,1,0:T(8,128)}, f32[4,16,128]{2,1,0:T(8,128)S(1)}, u32[]{:S(2)}, u32[]{:S(2)}) collective-permute-start(f32[4,16,128]{2,1,0:T(8,128)} %pack.1), channel_id=1, source_target_pairs={{0,16},{16,0},{32,48},{48,32},{64,80},{80,64},{96,112},{112,96},{1... | collective-permute-start | bytes 98312 | tf_op jit(solution)/shard_map/ppermute | solution.py:285
  53.5 0.1 add_select_fusion
  53.6 0.0 collective-permute-done.2.far_ref
  53.6 0.9 %collective-permute-done.3.near_ref = f32[4,16,128]{2,1,0:T(8,128)S(1)} collective-permute-done((f32[4,16,128]{2,1,0:T(8,128)}, f32[4,16,128]{2,1,0:T(8,128)S(1)}, u32[]{:S(2)}, u32[]{:S(2)}) %collective-permute-start.3) | collective-permute-done | bytes 32800 | tf_op jit(solution)/shard_map/ppermute | solution.py:285
  54.5 1.5 %advance_own.1.own_ref = f32[4,4,16,128]{3,2,1,0:T(8,128)} custom-call(f32[4,16,128]{2,1,0:T(8,128)S(1)} %collective-permute-done.2.far_ref, f32[4,16,128]{2,1,0:T(8,128)S(1)} %collective-permute-done.3.near_ref, f32[4,4,4,16,128]{4,3,2,1,0:T(8,128)S(1)} %bitcast.14, bf16[4,304,128]{2,1,0:T(8,128)(2,1)S(1)} %all_to_all.15.t_ref), custom_call_target="tpu_custom_call" | custom-call | tf_op jit(solution)/shard_map/advance_own/pallas_call | solution.py:184
  56.0 1.6 %all-to-all-done.1.t_ref = bf16[4,4,304,128]{3,2,1,0:T(8,128)(2,1)S(1)} async-done(((bf16[4,4,304,128]{3,2,1,0:T(8,128)(2,1)}), bf16[4,4,304,128]{3,2,1,0:T(8,128)(2,1)S(1)}, u32[]{:S(2)}, u32[]{:S(2)}) %all-to-all-start.1) | async-done | bytes 1245216 | tf_op jit(solution)/shard_map/all_to_all | solution.py:280
  57.6 7.4 %advance_and_pick.1 = (f32[4,4,4,16,128]{4,3,2,1,0:T(8,128)}, f32[48,4,128]{2,1,0:T(4,128)}) custom-call(f32[4,16,128]{2,1,0:T(8,128)S(1)} %collective-permute-done.2.far_ref, f32[4,16,128]{2,1,0:T(8,128)S(1)} %collective-permute-done.3.near_ref, f32[4,4,4,16,128]{4,3,2,1,0:T(8,128)S(1)} %bitcast.15, f32[4,4,16,128]{3,2,1,0:T(8,128)} %advance_own.1.own_ref, ...), custom_call_target="tpu_custom_call" | custom-call | tf_op jit(solution)/shard_map/advance_and_pick/pallas_call | solution.py:248
  64.9 24.1 %all_to_all.16 = f32[48,4,128]{2,1,0:T(4,128)S(1)} all-to-all(f32[48,4,128]{2,1,0:T(4,128)} %get-tuple-element.11), channel_id=1, replica_groups=mesh['space'=48,'yhi'=4,'x'=4] {'space'}, dimensions={0} | all-to-all | bytes 196608 | tf_op jit(solution)/shard_map/all_to_all | solution.py:292
  89.0 0.7 fusion
  (6 shorter events, 0.0 us)
Async XLA Ops:
  2.9 18.5 %collective-permute-start = (bf16[16,128]{1,0:T(8,128)(2,1)}, bf16[16,128]{1,0:T(8,128)(2,1)S(1)}, u32[]{:S(2)}, u32[]{:S(2)}) collective-permute-start(bf16[16,128]{1,0:T(8,128)(2,1)} %get-tuple-element.7), channel_id=1, source_target_pairs={{0,752},{16,32},{32,16},{48,64},{64,48},{80,96},{96,80},{112,128},... | collective-permute-start | bytes 12296 | tf_op jit(solution)/shard_map/ppermute | solution.py:275
  7.5 14.9 %collective-permute-start.1 = (bf16[16,128]{1,0:T(8,128)(2,1)}, bf16[16,128]{1,0:T(8,128)(2,1)S(1)}, u32[]{:S(2)}, u32[]{:S(2)}) collective-permute-start(bf16[16,128]{1,0:T(8,128)(2,1)} %get-tuple-element.7), channel_id=1, source_target_pairs={{0,16},{16,0},{32,48},{48,32},{64,80},{80,64},{96,112},{112,96},{1... | collective-permute-start | bytes 12296 | tf_op jit(solution)/shard_map/ppermute | solution.py:276
  39.4 4.2 %copy-start = (f32[1,4,16,16,128]{4,3,2,1,0:T(8,128)S(1)}, f32[1,4,16,16,128]{4,3,2,1,0:T(8,128)}, u32[]{:S(2)}) copy-start(f32[1,4,16,16,128]{4,3,2,1,0:T(8,128)} %param.6) | copy-start | bytes 1572868
  39.4 14.1 %copy-start.2 = (s32[48,1,128]{2,1,0:T(1,128)S(1)}, s32[48,1,128]{2,1,0:T(1,128)}, u32[]{:S(2)}) copy-start(s32[48,1,128]{2,1,0:T(1,128)} %param.8) | copy-start | bytes 73732
  39.4 14.1 %copy-start.3 = (s32[48,1,128]{2,1,0:T(1,128)S(1)}, s32[48,1,128]{2,1,0:T(1,128)}, u32[]{:S(2)}) copy-start(s32[48,1,128]{2,1,0:T(1,128)} %param.9) | copy-start | bytes 73732
  39.4 14.1 %copy-start.4 = (s32[48,1]{0,1:T(1,128)S(1)}, s32[48,1]{0,1:T(1,128)}, u32[]{:S(2)}) copy-start(s32[48,1]{0,1:T(1,128)} %param.10) | copy-start | bytes 580
  39.4 18.1 %all-to-all-start.1 = ((bf16[4,4,304,128]{3,2,1,0:T(8,128)(2,1)}), bf16[4,4,304,128]{3,2,1,0:T(8,128)(2,1)S(1)}, u32[]{:S(2)}, u32[]{:S(2)}) async-start(bf16[4,4,304,128]{3,2,1,0:T(8,128)(2,1)} %spread.1), calls=%async_computation.1 | async-start | bytes 2490368 | tf_op jit(solution)/shard_map/all_to_all | solution.py:280
  44.4 9.2 %collective-permute-start.2 = (f32[4,16,128]{2,1,0:T(8,128)}, f32[4,16,128]{2,1,0:T(8,128)S(1)}, u32[]{:S(2)}, u32[]{:S(2)}) collective-permute-start(f32[4,16,128]{2,1,0:T(8,128)} %pack.1), channel_id=1, source_target_pairs={{0,752},{16,32},{32,16},{48,64},{64,48},{80,96},{96,80},{112,128},... | collective-permute-start | bytes 98312 | tf_op jit(solution)/shard_map/ppermute | solution.py:284
  46.3 8.2 %collective-permute-start.3 = (f32[4,16,128]{2,1,0:T(8,128)}, f32[4,16,128]{2,1,0:T(8,128)S(1)}, u32[]{:S(2)}, u32[]{:S(2)}) collective-permute-start(f32[4,16,128]{2,1,0:T(8,128)} %pack.1), channel_id=1, source_target_pairs={{0,16},{16,0},{32,48},{48,32},{64,80},{80,64},{96,112},{112,96},{1... | collective-permute-start | bytes 98312 | tf_op jit(solution)/shard_map/ppermute | solution.py:285
  56.0 33.1 %copy-start.1 = (f32[1,48,4,128]{3,2,1,0:T(4,128)S(1)}, f32[1,48,4,128]{3,2,1,0:T(4,128)}, u32[]{:S(2)}) copy-start(f32[1,48,4,128]{3,2,1,0:T(4,128)} %param.11) | copy-start | bytes 294916

commit v11 on v8

--- a/solution.py
+++ b/solution.py
@@ -77,21 +77,21 @@
     return jnp.where((lane_of(near.shape) % 8 < 3) == (odd == 1), near, far)
 
 
-def fill_kernel(near_ref, far_ref, halo_ref, side_ref):
+def fill_kernel(far_ref, near_ref, halo_ref, side_ref):
     edge = merge(near_ref[...], far_ref[...])
     halo_ref[...] = edge[0:4]
     for i in range(4):
         side_ref[i] = edge[4:8].astype(BF16)
 
 
-def fill(near, far):
+def fill(far, near):
     return pl.pallas_call(
         fill_kernel,
         out_shape=(jax.ShapeDtypeStruct((4,) + TILE, F32), jax.ShapeDtypeStruct((4, 4) + TILE, BF16)),
         in_specs=[VMEM, VMEM],
         out_specs=(VMEM, VMEM),
         name="fill",
-    )(in_vmem(near), in_vmem(far))
+    )(in_vmem(far), in_vmem(near))
 
 
 def weights_of(planes, first, last):
@@ -211,7 +211,7 @@
                 val_ref[4 * i + o, f : f + 1, :] = jnp.sum(jnp.where(hit, part, 0.0), axis=0, keepdims=True)
         return carry
 
-    lax.fori_loop(0, owners // 4, four_owners, 0, unroll=2)
+    lax.fori_loop(0, owners // 4, four_owners, 0, unroll=6)
     move.wait()
 
 
@@ -250,7 +250,7 @@
     edge = pack(state, late)
     far = lax.ppermute(edge, "space", crossed)
     near = lax.ppermute(edge, "space", pairs)
-    halo, side = fill(near, far)
+    halo, side = fill(far, near)
     own = advance_own(state, halo, first, side)
     side, planes, own = lax.optimization_barrier((side, planes, own))
     sides = lax.all_to_all(side, "x", 0, 0, tiled=True)

time: 88.7 us -> 87.5 us (0.986)
  starting transfers between devices: 18.5 us -> 25.1 us
  blocking collectives: 45 us -> 40.7 us
  waiting for transfers between devices: 8.55 us -> 5.47 us
    ppermute x1, starting transfers between devices: 1.92 us -> 6.46 us  [on_device(): far = lax.ppermute(edge, 'space', crossed)]
    all_to_all x1, blocking collectives: 27.7 us -> 23.5 us  [on_device(): received = lax.all_to_all(values, 'space', 0, 0, tiled=True)]
    ppermute x1, waiting for transfers between devices: 4.15 us -> 0.01 us  [on_device(): far = lax.ppermute(edge, 'space', crossed)]
    ppermute x1, starting transfers between devices: 8.45 us -> 10.4 us  [on_device(): near = lax.ppermute(edge, 'space', pairs)]
    ppermute x1, waiting for transfers between devices: 0.01 us -> 1.08 us  [on_device(): near = lax.ppermute(edge, 'space', pairs)]
where the time goes in v11:
time: 87.5 us; the launch traced here: 86.8 us
  blocking collectives  40.7 us (47%)
  starting transfers between devices  25.1 us (29%)
  Pallas kernels  13.9 us (16%)
  waiting for transfers between devices  5.47 us (6%)
    all_to_all x1, blocking collectives, on_device(): received = lax.all_to_all(values, 'space', 0, 0, tiled=True)  23.5 us
    all_to_all x1, blocking collectives, on_device(): first = lax.all_to_all(spread(local), 'yhi', 0, 0, tiled=True)  17.3 us
    ppermute x1, starting transfers between devices, on_device(): near = lax.ppermute(edge, 'space', pairs)  10.4 us
    pallas_call x1, Pallas kernels, advance_and_pick(): pl.pallas_call(main_kernel, out_shape=(jax.ShapeDtypeStruct(state.shape,...  7.35 us
    ppermute x1, starting transfers between devices, on_device(): far = lax.ppermute(edge, 'space', crossed)  6.46 us
    all_to_all x1, waiting for transfers between devices, on_device(): sides = lax.all_to_all(side, 'x', 0, 0, tiled=True)  4.39 us
    all_to_all x1, starting transfers between devices, on_device(): sides = lax.all_to_all(side, 'x', 0, 0, tiled=True)  4.36 us
    all_to_all x1, starting transfers between devices, on_device(): planes = lax.all_to_all(copies, 'x', 0, 0, tiled=True)  3.89 us
  transfers between devices with their start and end apart: 4, of which 2 were waited for; matrix products, arithmetic and copies ran while one was open for 0% of the time, Pallas kernels for 4%

profile of v11, /device:TPU:1, one launch (start us, length us, event | category | flops | bytes accessed | tf_op | source)
XLA Modules:
  0.0 86.8 jit_solution(11196341063226956670)
XLA Ops:
  0.6 1.6 %spread.2 = bf16[4,288,128]{2,1,0:T(8,128)(2,1)} custom-call(bf16[288,128]{1,0:T(8,128)(2,1)} %bitcast.16), custom_call_target="tpu_custom_call" | custom-call | tf_op jit(solution)/shard_map/spread/pallas_call | solution.py:39
  2.3 17.3 %all_to_all.20.t_ref = bf16[4,288,128]{2,1,0:T(8,128)(2,1)S(1)} all-to-all(bf16[4,288,128]{2,1,0:T(8,128)(2,1)} %spread.2), channel_id=1, replica_groups=mesh['space'=48,'yhi'=4,'x'=4] {'yhi'}, dimensions={0} | all-to-all | bytes 589824 | tf_op jit(solution)/shard_map/all_to_all | solution.py:245
  19.5 1.1 %spread.3 = bf16[4,4,288,128]{3,2,1,0:T(8,128)(2,1)} custom-call(bf16[4,288,128]{2,1,0:T(8,128)(2,1)S(1)} %all_to_all.20.t_ref), custom_call_target="tpu_custom_call" | custom-call | tf_op jit(solution)/shard_map/spread/pallas_call | solution.py:39
  20.6 0.0 copy-start
  20.6 3.9 %all-to-all-start.1 = ((bf16[4,4,288,128]{3,2,1,0:T(8,128)(2,1)}), bf16[4,4,288,128]{3,2,1,0:T(8,128)(2,1)S(1)}, u32[]{:S(2)}, u32[]{:S(2)}) async-start(bf16[4,4,288,128]{3,2,1,0:T(8,128)(2,1)} %spread.3), calls=%async_computation.1 | async-start | bytes 2359296 | tf_op jit(solution)/shard_map/all_to_all | solution.py:247
  24.5 0.0 copy-done
  24.5 0.9 %pack.1 = f32[8,16,128]{2,1,0:T(8,128)} custom-call(f32[4,4,4,16,128]{4,3,2,1,0:T(8,128)S(1)} %bitcast.13, bf16[4,288,128]{2,1,0:T(8,128)(2,1)S(1)} %all_to_all.20.t_ref), custom_call_target="tpu_custom_call" | custom-call | tf_op jit(solution)/shard_map/pack/pallas_call | solution.py:66
  25.4 6.5 %collective-permute-start = (f32[8,16,128]{2,1,0:T(8,128)}, f32[8,16,128]{2,1,0:T(8,128)S(1)}, u32[]{:S(2)}, u32[]{:S(2)}) collective-permute-start(f32[8,16,128]{2,1,0:T(8,128)} %pack.1), channel_id=1, source_target_pairs={{0,752},{16,32},{32,16},{48,64},{64,48},{80,96},{96,80},{112,128},... | collective-permute-start | bytes 196616 | tf_op jit(solution)/shard_map/ppermute | solution.py:251
  31.9 10.4 %collective-permute-start.1 = (f32[8,16,128]{2,1,0:T(8,128)}, f32[8,16,128]{2,1,0:T(8,128)S(1)}, u32[]{:S(2)}, u32[]{:S(2)}) collective-permute-start(f32[8,16,128]{2,1,0:T(8,128)} %pack.1), channel_id=1, source_target_pairs={{0,16},{16,0},{32,48},{48,32},{64,80},{80,64},{96,112},{112,96},{1... | collective-permute-start | bytes 196616 | tf_op jit(solution)/shard_map/ppermute | solution.py:252
  42.3 0.0 collective-permute-done.far_ref
  42.3 1.1 %collective-permute-done.1.near_ref = f32[8,16,128]{2,1,0:T(8,128)S(1)} collective-permute-done((f32[8,16,128]{2,1,0:T(8,128)}, f32[8,16,128]{2,1,0:T(8,128)S(1)}, u32[]{:S(2)}, u32[]{:S(2)}) %collective-permute-start.1) | collective-permute-done | bytes 65568 | tf_op jit(solution)/shard_map/ppermute | solution.py:252
  43.4 0.7 fill.1
  44.1 2.3 %advance_own.1.own_ref = f32[4,4,16,128]{3,2,1,0:T(8,128)} custom-call(f32[4,4,4,16,128]{4,3,2,1,0:T(8,128)S(1)} %bitcast.14, f32[4,16,128]{2,1,0:T(8,128)} %get-tuple-element.11.halo_ref, bf16[4,288,128]{2,1,0:T(8,128)(2,1)S(1)} %all_to_all.20.t_ref, bf16[4,4,16,128]{3,2,1,0:T(8,128)(2,1)} %get-tuple-element.15.side_ref), custom_call_target="tpu_custom_call" | custom-call | tf_op jit(solution)/shard_map/advance_own/pallas_call | solution.py:157
  46.4 0.0 all-to-all-done.1.t_ref
  46.4 4.4 %all-to-all-start.2 = ((bf16[4,4,16,128]{3,2,1,0:T(8,128)(2,1)}), bf16[4,4,16,128]{3,2,1,0:T(8,128)(2,1)S(1)}, u32[]{:S(2)}, u32[]{:S(2)}) async-start(bf16[4,4,16,128]{3,2,1,0:T(8,128)(2,1)} %get-tuple-element.15.side_ref), calls=%async_computation.2 | async-start | bytes 131072 | tf_op jit(solution)/shard_map/all_to_all | solution.py:256
  50.8 0.0 copy-done.3
  50.8 0.0 copy-done.4
  50.8 0.0 copy-done.5
  50.8 0.1 add_select_fusion
  50.8 4.4 %all-to-all-done.2.side_ref = bf16[4,4,16,128]{3,2,1,0:T(8,128)(2,1)S(1)} async-done(((bf16[4,4,16,128]{3,2,1,0:T(8,128)(2,1)}), bf16[4,4,16,128]{3,2,1,0:T(8,128)(2,1)S(1)}, u32[]{:S(2)}, u32[]{:S(2)}) %all-to-all-start.2) | async-done | bytes 65568 | tf_op jit(solution)/shard_map/all_to_all | solution.py:256
  55.2 0.0 copy-done.1
  55.2 7.4 %advance_and_pick.1 = (f32[4,4,4,16,128]{4,3,2,1,0:T(8,128)}, f32[48,4,128]{2,1,0:T(4,128)}) custom-call(f32[4,4,4,16,128]{4,3,2,1,0:T(8,128)S(1)} %bitcast.15, f32[4,16,128]{2,1,0:T(8,128)S(1)} %copy-done.1, f32[4,4,16,128]{3,2,1,0:T(8,128)} %advance_own.1.own_ref, bf16[4,4,288,128]{3,2,1,0:T(8,128)(2,1)S(1)} %all-to-all-done.1.t_ref, ...), custom_call_target="tpu_custom_call" | custom-call | tf_op jit(solution)/shard_map/advance_and_pick/pallas_call | solution.py:220
  62.6 23.5 %all_to_all.21 = f32[48,4,128]{2,1,0:T(4,128)S(1)} all-to-all(f32[48,4,128]{2,1,0:T(4,128)} %get-tuple-element.17), channel_id=1, replica_groups=mesh['space'=48,'yhi'=4,'x'=4] {'space'}, dimensions={0} | all-to-all | bytes 196608 | tf_op jit(solution)/shard_map/all_to_all | solution.py:262
  86.1 0.7 fusion
  (6 shorter events, 0.0 us)
Async XLA Ops:
  20.6 3.9 %copy-start = (f32[1,4,16,16,128]{4,3,2,1,0:T(8,128)S(1)}, f32[1,4,16,16,128]{4,3,2,1,0:T(8,128)}, u32[]{:S(2)}) copy-start(f32[1,4,16,16,128]{4,3,2,1,0:T(8,128)} %param.6) | copy-start | bytes 1572868
  20.6 25.8 %all-to-all-start.1 = ((bf16[4,4,288,128]{3,2,1,0:T(8,128)(2,1)}), bf16[4,4,288,128]{3,2,1,0:T(8,128)(2,1)S(1)}, u32[]{:S(2)}, u32[]{:S(2)}) async-start(bf16[4,4,288,128]{3,2,1,0:T(8,128)(2,1)} %spread.3), calls=%async_computation.1 | async-start | bytes 2359296 | tf_op jit(solution)/shard_map/all_to_all | solution.py:247
  24.5 26.3 %copy-start.3 = (s32[48,1,128]{2,1,0:T(1,128)S(1)}, s32[48,1,128]{2,1,0:T(1,128)}, u32[]{:S(2)}) copy-start(s32[48,1,128]{2,1,0:T(1,128)} %param.8) | copy-start | bytes 73732
  24.5 26.3 %copy-start.4 = (s32[48,1,128]{2,1,0:T(1,128)S(1)}, s32[48,1,128]{2,1,0:T(1,128)}, u32[]{:S(2)}) copy-start(s32[48,1,128]{2,1,0:T(1,128)} %param.9) | copy-start | bytes 73732
  24.5 26.3 %copy-start.5 = (s32[48,1]{0,1:T(1,128)S(1)}, s32[48,1]{0,1:T(1,128)}, u32[]{:S(2)}) copy-start(s32[48,1]{0,1:T(1,128)} %param.10) | copy-start | bytes 580
  25.4 16.9 %collective-permute-start = (f32[8,16,128]{2,1,0:T(8,128)}, f32[8,16,128]{2,1,0:T(8,128)S(1)}, u32[]{:S(2)}, u32[]{:S(2)}) collective-permute-start(f32[8,16,128]{2,1,0:T(8,128)} %pack.1), channel_id=1, source_target_pairs={{0,752},{16,32},{32,16},{48,64},{64,48},{80,96},{96,80},{112,128},... | collective-permute-start | bytes 196616 | tf_op jit(solution)/shard_map/ppermute | solution.py:251
  31.9 11.5 %collective-permute-start.1 = (f32[8,16,128]{2,1,0:T(8,128)}, f32[8,16,128]{2,1,0:T(8,128)S(1)}, u32[]{:S(2)}, u32[]{:S(2)}) collective-permute-start(f32[8,16,128]{2,1,0:T(8,128)} %pack.1), channel_id=1, source_target_pairs={{0,16},{16,0},{32,48},{48,32},{64,80},{80,64},{96,112},{112,96},{1... | collective-permute-start | bytes 196616 | tf_op jit(solution)/shard_map/ppermute | solution.py:252
  44.1 11.2 %copy-start.1 = (f32[4,16,128]{2,1,0:T(8,128)S(1)}, f32[4,16,128]{2,1,0:T(8,128)}, u32[]{:S(2)}) copy-start(f32[4,16,128]{2,1,0:T(8,128)} %get-tuple-element.11.halo_ref) | copy-start | bytes 98308
  46.4 39.7 %copy-start.2 = (f32[1,48,4,128]{3,2,1,0:T(4,128)S(1)}, f32[1,48,4,128]{3,2,1,0:T(4,128)}, u32[]{:S(2)}) copy-start(f32[1,48,4,128]{3,2,1,0:T(4,128)} %param.11) | copy-start | bytes 294916
  46.4 8.8 %all-to-all-start.2 = ((bf16[4,4,16,128]{3,2,1,0:T(8,128)(2,1)}), bf16[4,4,16,128]{3,2,1,0:T(8,128)(2,1)S(1)}, u32[]{:S(2)}, u32[]{:S(2)}) async-start(bf16[4,4,16,128]{3,2,1,0:T(8,128)(2,1)} %get-tuple-element.15.side_ref), calls=%async_computation.2 | async-start | bytes 131072 | tf_op jit(solution)/shard_map/all_to_all | solution.py:256

commit v12 on v11

--- a/solution.py
+++ b/solution.py
@@ -80,14 +80,13 @@
 def fill_kernel(far_ref, near_ref, halo_ref, side_ref):
     edge = merge(near_ref[...], far_ref[...])
     halo_ref[...] = edge[0:4]
-    for i in range(4):
-        side_ref[i] = edge[4:8].astype(BF16)
+    side_ref[...] = edge[4:8].astype(BF16)
 
 
 def fill(far, near):
     return pl.pallas_call(
         fill_kernel,
-        out_shape=(jax.ShapeDtypeStruct((4,) + TILE, F32), jax.ShapeDtypeStruct((4, 4) + TILE, BF16)),
+        out_shape=(jax.ShapeDtypeStruct((4,) + TILE, F32), jax.ShapeDtypeStruct((4,) + TILE, BF16)),
         in_specs=[VMEM, VMEM],
         out_specs=(VMEM, VMEM),
         name="fill",
@@ -144,7 +143,7 @@
 
     def one_level(y, carry):
         state = advance_at(
-            y, x, p_ref, halo_ref, lambda i: t_ref[y, i * 16 : i * 16 + 16, :].astype(F32), side_ref[0, y]
+            y, x, p_ref, halo_ref, lambda i: t_ref[y, i * 16 : i * 16 + 16, :].astype(F32), side_ref[y]
         )
         for f in range(4):
             out_ref[f, y] = state[f]
@@ -164,17 +163,20 @@
 
 
 def main_kernel(
-    p_ref, halo_ref, own_ref, t_ref, side_ref, row_ref, col_ref, out_ref, val_ref, final_ref, table_ref, sem, own_sem
+    p_ref, halo_ref, own_ref, t_ref, side1_ref, side2_ref, side3_ref, row_ref, col_ref,
+    out_ref, val_ref, side_ref, final_ref, table_ref, sem, own_sem,
 ):
     owners = row_ref.shape[0]
     here = axis_index("x")
     bring = pltpu.make_async_copy(own_ref, final_ref.at[:, :, here], own_sem)
     bring.start()
+    for k, ref in enumerate((side1_ref, side2_ref, side3_ref)):
+        side_ref[k] = ref[...]
 
     def one_level(i, carry):
         y, x = lax.rem(i, 4), lax.rem(here + 1 + i // 4, 4)
         state = advance_at(
-            y, x, p_ref, halo_ref, lambda j: t_ref[x, y, j * 16 : j * 16 + 16, :].astype(F32), side_ref[x, y]
+            y, x, p_ref, halo_ref, lambda j: t_ref[x, y, j * 16 : j * 16 + 16, :].astype(F32), side_ref[i // 4, y]
         )
         for f in range(4):
             final_ref[f, y, x] = state[f]
@@ -223,16 +225,17 @@
             jax.ShapeDtypeStruct(state.shape, F32),
             jax.ShapeDtypeStruct((owners, 4, 128), F32),
         ),
-        in_specs=[VMEM, VMEM, HBM] + [VMEM] * 4,
+        in_specs=[VMEM, VMEM, HBM] + [VMEM] * 6,
         out_specs=(HBM, VMEM),
         scratch_shapes=[
+            pltpu.VMEM((3, 4) + TILE, BF16),
             pltpu.VMEM(state.shape, F32),
             pltpu.VMEM((512, 512), BF16),
             pltpu.SemaphoreType.DMA,
             pltpu.SemaphoreType.DMA,
         ],
         name="advance_and_pick",
-    )(in_vmem(state), in_vmem(halo), own, *map(in_vmem, (planes, sides, rows, cols)))
+    )(in_vmem(state), in_vmem(halo), own, *map(in_vmem, (planes, *sides, rows, cols)))
 
 
 def on_device(perturbation, trajectory, site_col, site_lev, obs_counts, obs_weights):
@@ -252,8 +255,7 @@
     near = lax.ppermute(edge, "space", pairs)
     halo, side = fill(far, near)
     own = advance_own(state, halo, first, side)
-    side, planes, own = lax.optimization_barrier((side, planes, own))
-    sides = lax.all_to_all(side, "x", 0, 0, tiled=True)
+    sides = [lax.ppermute(side, "x", [((i + k) % 4, i) for i in range(4)]) for k in (1, 2, 3)]
 
     live = jnp.arange(slots, dtype=jnp.int32)[None, :] < obs_counts
     rows = jnp.where(live, site_lev[:, 0, :] * 16 + site_col[:, 0, :] // 128, -1)

time: 87.5 us -> 89 us (1.017)
  starting transfers between devices: 25.1 us -> 30.3 us
  waiting for transfers between devices: 5.47 us -> 2.13 us
  blocking collectives: 40.7 us -> 39.8 us
    ppermute x0 -> x3, starting transfers between devices: none -> 9.54 us  [on_device(): lax.ppermute(side, 'x', [((i + k) % 4, i) for i in range(4)])]
    all_to_all x1 -> x0, waiting for transfers between devices: 4.39 us -> none  [on_device(): sides = lax.all_to_all(side, 'x', 0, 0, tiled=True)]
    all_to_all x1 -> x0, starting transfers between devices: 4.36 us -> none  [on_device(): sides = lax.all_to_all(side, 'x', 0, 0, tiled=True)]
    ppermute x0 -> x3, waiting for transfers between devices: none -> 1.04 us  [on_device(): lax.ppermute(side, 'x', [((i + k) % 4, i) for i in range(4)])]
    all_to_all x1, blocking collectives: 23.5 us -> 22.6 us  [on_device(): received = lax.all_to_all(values, 'space', 0, 0, tiled=True)]
  transfers between devices with their start and end apart: 4 -> 6, of which waited for: 2 -> 2; matrix products, arithmetic and copies ran while one was open for 0% -> 0% of each run, Pallas kernels for 4% -> 4%
where the time goes in v12:
time: 89 us; the launch traced here: 88.4 us
  blocking collectives  39.8 us (45%)
  starting transfers between devices  30.3 us (34%)
  Pallas kernels  13.8 us (16%)
  waiting for transfers between devices  2.13 us (2%)
    all_to_all x1, blocking collectives, on_device(): received = lax.all_to_all(values, 'space', 0, 0, tiled=True)  22.6 us
    all_to_all x1, blocking collectives, on_device(): first = lax.all_to_all(spread(local), 'yhi', 0, 0, tiled=True)  17.3 us
    ppermute x1, starting transfers between devices, on_device(): near = lax.ppermute(edge, 'space', pairs)  10.4 us
    ppermute x3, starting transfers between devices, on_device(): lax.ppermute(side, 'x', [((i + k) % 4, i) for i in range(4)])  9.54 us
    pallas_call x1, Pallas kernels, advance_and_pick(): pl.pallas_call(main_kernel, out_shape=(jax.ShapeDtypeStruct(state.shape,...  7.33 us
    ppermute x1, starting transfers between devices, on_device(): far = lax.ppermute(edge, 'space', crossed)  6.46 us
    all_to_all x1, starting transfers between devices, on_device(): planes = lax.all_to_all(copies, 'x', 0, 0, tiled=True)  3.89 us
    pallas_call x2, Pallas kernels, spread(): pl.pallas_call(spread_kernel, out_shape=jax.ShapeDtypeStruct((4,) + plane...  2.68 us
  transfers between devices with their start and end apart: 6, of which 2 were waited for; matrix products, arithmetic and copies ran while one was open for 0% of the time, Pallas kernels for 4%

profile of v12, /device:TPU:1, one launch (start us, length us, event | category | flops | bytes accessed | tf_op | source)
XLA Modules:
  0.0 88.4 jit_solution(12637899761803018619)
XLA Ops:
  0.6 1.6 %spread.2 = bf16[4,288,128]{2,1,0:T(8,128)(2,1)} custom-call(bf16[288,128]{1,0:T(8,128)(2,1)} %bitcast.16), custom_call_target="tpu_custom_call" | custom-call | tf_op jit(solution)/shard_map/spread/pallas_call | solution.py:39
  2.3 17.3 %all_to_all.15.t_ref = bf16[4,288,128]{2,1,0:T(8,128)(2,1)S(1)} all-to-all(bf16[4,288,128]{2,1,0:T(8,128)(2,1)} %spread.2), channel_id=1, replica_groups=mesh['space'=48,'yhi'=4,'x'=4] {'yhi'}, dimensions={0} | all-to-all | bytes 589824 | tf_op jit(solution)/shard_map/all_to_all | solution.py:248
  19.5 1.1 %spread.3 = bf16[4,4,288,128]{3,2,1,0:T(8,128)(2,1)} custom-call(bf16[4,288,128]{2,1,0:T(8,128)(2,1)S(1)} %all_to_all.15.t_ref), custom_call_target="tpu_custom_call" | custom-call | tf_op jit(solution)/shard_map/spread/pallas_call | solution.py:39
  20.6 0.0 copy-start
  20.6 0.0 copy-start.3
  20.6 0.0 copy-start.4
  20.6 0.0 copy-start.5
  20.6 3.9 %all-to-all-start.1 = ((bf16[4,4,288,128]{3,2,1,0:T(8,128)(2,1)}), bf16[4,4,288,128]{3,2,1,0:T(8,128)(2,1)S(1)}, u32[]{:S(2)}, u32[]{:S(2)}) async-start(bf16[4,4,288,128]{3,2,1,0:T(8,128)(2,1)} %spread.3), calls=%async_computation.1 | async-start | bytes 2359296 | tf_op jit(solution)/shard_map/all_to_all | solution.py:250
  24.5 0.9 pack.1
  25.4 6.5 %collective-permute-start = (f32[8,16,128]{2,1,0:T(8,128)}, f32[8,16,128]{2,1,0:T(8,128)S(1)}, u32[]{:S(2)}, u32[]{:S(2)}) collective-permute-start(f32[8,16,128]{2,1,0:T(8,128)} %pack.1), channel_id=1, source_target_pairs={{0,752},{16,32},{32,16},{48,64},{64,48},{80,96},{96,80},{112,128},... | collective-permute-start | bytes 196616 | tf_op jit(solution)/shard_map/ppermute | solution.py:254
  31.9 10.4 %collective-permute-start.1 = (f32[8,16,128]{2,1,0:T(8,128)}, f32[8,16,128]{2,1,0:T(8,128)S(1)}, u32[]{:S(2)}, u32[]{:S(2)}) collective-permute-start(f32[8,16,128]{2,1,0:T(8,128)} %pack.1), channel_id=1, source_target_pairs={{0,16},{16,0},{32,48},{48,32},{64,80},{80,64},{96,112},{112,96},{1... | collective-permute-start | bytes 196616 | tf_op jit(solution)/shard_map/ppermute | solution.py:255
  42.3 0.0 collective-permute-done.far_ref
  42.3 1.1 %collective-permute-done.1.near_ref = f32[8,16,128]{2,1,0:T(8,128)S(1)} collective-permute-done((f32[8,16,128]{2,1,0:T(8,128)}, f32[8,16,128]{2,1,0:T(8,128)S(1)}, u32[]{:S(2)}, u32[]{:S(2)}) %collective-permute-start.1) | collective-permute-done | bytes 65568 | tf_op jit(solution)/shard_map/ppermute | solution.py:255
  43.4 0.6 fill.1
  44.0 4.6 %collective-permute-start.2 = (bf16[4,16,128]{2,1,0:T(8,128)(2,1)}, bf16[4,16,128]{2,1,0:T(8,128)(2,1)S(1)}, u32[]{:S(2)}, u32[]{:S(2)}) collective-permute-start(bf16[4,16,128]{2,1,0:T(8,128)(2,1)} %get-tuple-element.9.side_ref), channel_id=1, source_target_pairs={{1,0},{2,1},{3,2},{0,3},{5,4},{6,5},{7,6},{4,7},{9,8},{10,9},{11,1... | collective-permute-start | bytes 49160 | tf_op jit(solution)/shard_map/ppermute | solution.py:258
  48.6 2.5 %collective-permute-start.3 = (bf16[4,16,128]{2,1,0:T(8,128)(2,1)}, bf16[4,16,128]{2,1,0:T(8,128)(2,1)S(1)}, u32[]{:S(2)}, u32[]{:S(2)}) collective-permute-start(bf16[4,16,128]{2,1,0:T(8,128)(2,1)} %get-tuple-element.9.side_ref), channel_id=1, source_target_pairs={{2,0},{3,1},{0,2},{1,3},{6,4},{7,5},{4,6},{5,7},{10,8},{11,9},{8,1... | collective-permute-start | bytes 49160 | tf_op jit(solution)/shard_map/ppermute | solution.py:258
  51.1 2.5 %collective-permute-start.4 = (bf16[4,16,128]{2,1,0:T(8,128)(2,1)}, bf16[4,16,128]{2,1,0:T(8,128)(2,1)S(1)}, u32[]{:S(2)}, u32[]{:S(2)}) collective-permute-start(bf16[4,16,128]{2,1,0:T(8,128)(2,1)} %get-tuple-element.9.side_ref), channel_id=1, source_target_pairs={{3,0},{0,1},{1,2},{2,3},{7,4},{4,5},{5,6},{6,7},{11,8},{8,9},{9,10... | collective-permute-start | bytes 49160 | tf_op jit(solution)/shard_map/ppermute | solution.py:258
  53.6 0.1 add_select_fusion
  53.7 2.3 %advance_own.1.own_ref = f32[4,4,16,128]{3,2,1,0:T(8,128)} custom-call(f32[4,4,4,16,128]{4,3,2,1,0:T(8,128)S(1)} %bitcast.14, f32[4,16,128]{2,1,0:T(8,128)} %get-tuple-element.8.halo_ref, bf16[4,288,128]{2,1,0:T(8,128)(2,1)S(1)} %all_to_all.15.t_ref, bf16[4,16,128]{2,1,0:T(8,128)(2,1)} %get-tuple-element.9.side_ref), custom_call_target="tpu_custom_call" | custom-call | tf_op jit(solution)/shard_map/advance_own/pallas_call | solution.py:156
  56.0 1.0 %collective-permute-done.4.side3_ref = bf16[4,16,128]{2,1,0:T(8,128)(2,1)S(1)} collective-permute-done((bf16[4,16,128]{2,1,0:T(8,128)(2,1)}, bf16[4,16,128]{2,1,0:T(8,128)(2,1)S(1)}, u32[]{:S(2)}, u32[]{:S(2)}) %collective-permute-start.4) | collective-permute-done | bytes 16416 | tf_op jit(solution)/shard_map/ppermute | solution.py:258
  57.0 0.8 copy-done.1
  57.8 7.3 %advance_and_pick.1 = (f32[4,4,4,16,128]{4,3,2,1,0:T(8,128)}, f32[48,4,128]{2,1,0:T(4,128)}) custom-call(f32[4,4,4,16,128]{4,3,2,1,0:T(8,128)S(1)} %bitcast.15, f32[4,16,128]{2,1,0:T(8,128)S(1)} %copy-done.1, f32[4,4,16,128]{3,2,1,0:T(8,128)} %advance_own.1.own_ref, bf16[4,4,288,128]{3,2,1,0:T(8,128)(2,1)S(1)} %all-to-all-done.1.t_ref, ...), custom_call_target="tpu_custom_call" | custom-call | tf_op jit(solution)/shard_map/advance_and_pick/pallas_call | solution.py:222
  65.1 22.6 %all_to_all.16 = f32[48,4,128]{2,1,0:T(4,128)S(1)} all-to-all(f32[48,4,128]{2,1,0:T(4,128)} %get-tuple-element.11), channel_id=1, replica_groups=mesh['space'=48,'yhi'=4,'x'=4] {'space'}, dimensions={0} | all-to-all | bytes 196608 | tf_op jit(solution)/shard_map/all_to_all | solution.py:264
  87.7 0.7 fusion
  (10 shorter events, 0.0 us)
Async XLA Ops:
  20.6 3.9 %copy-start = (f32[1,4,16,16,128]{4,3,2,1,0:T(8,128)S(1)}, f32[1,4,16,16,128]{4,3,2,1,0:T(8,128)}, u32[]{:S(2)}) copy-start(f32[1,4,16,16,128]{4,3,2,1,0:T(8,128)} %param.6) | copy-start | bytes 1572868
  20.6 33.0 %copy-start.3 = (s32[48,1,128]{2,1,0:T(1,128)S(1)}, s32[48,1,128]{2,1,0:T(1,128)}, u32[]{:S(2)}) copy-start(s32[48,1,128]{2,1,0:T(1,128)} %param.8) | copy-start | bytes 73732
  20.6 33.0 %copy-start.4 = (s32[48,1,128]{2,1,0:T(1,128)S(1)}, s32[48,1,128]{2,1,0:T(1,128)}, u32[]{:S(2)}) copy-start(s32[48,1,128]{2,1,0:T(1,128)} %param.9) | copy-start | bytes 73732
  20.6 33.0 %copy-start.5 = (s32[48,1]{0,1:T(1,128)S(1)}, s32[48,1]{0,1:T(1,128)}, u32[]{:S(2)}) copy-start(s32[48,1]{0,1:T(1,128)} %param.10) | copy-start | bytes 580
  20.6 36.4 %all-to-all-start.1 = ((bf16[4,4,288,128]{3,2,1,0:T(8,128)(2,1)}), bf16[4,4,288,128]{3,2,1,0:T(8,128)(2,1)S(1)}, u32[]{:S(2)}, u32[]{:S(2)}) async-start(bf16[4,4,288,128]{3,2,1,0:T(8,128)(2,1)} %spread.3), calls=%async_computation.1 | async-start | bytes 2359296 | tf_op jit(solution)/shard_map/all_to_all | solution.py:250
  25.4 16.9 %collective-permute-start = (f32[8,16,128]{2,1,0:T(8,128)}, f32[8,16,128]{2,1,0:T(8,128)S(1)}, u32[]{:S(2)}, u32[]{:S(2)}) collective-permute-start(f32[8,16,128]{2,1,0:T(8,128)} %pack.1), channel_id=1, source_target_pairs={{0,752},{16,32},{32,16},{48,64},{64,48},{80,96},{96,80},{112,128},... | collective-permute-start | bytes 196616 | tf_op jit(solution)/shard_map/ppermute | solution.py:254
  31.9 11.5 %collective-permute-start.1 = (f32[8,16,128]{2,1,0:T(8,128)}, f32[8,16,128]{2,1,0:T(8,128)S(1)}, u32[]{:S(2)}, u32[]{:S(2)}) collective-permute-start(f32[8,16,128]{2,1,0:T(8,128)} %pack.1), channel_id=1, source_target_pairs={{0,16},{16,0},{32,48},{48,32},{64,80},{80,64},{96,112},{112,96},{1... | collective-permute-start | bytes 196616 | tf_op jit(solution)/shard_map/ppermute | solution.py:255
  44.0 11.9 %collective-permute-start.2 = (bf16[4,16,128]{2,1,0:T(8,128)(2,1)}, bf16[4,16,128]{2,1,0:T(8,128)(2,1)S(1)}, u32[]{:S(2)}, u32[]{:S(2)}) collective-permute-start(bf16[4,16,128]{2,1,0:T(8,128)(2,1)} %get-tuple-element.9.side_ref), channel_id=1, source_target_pairs={{1,0},{2,1},{3,2},{0,3},{5,4},{6,5},{7,6},{4,7},{9,8},{10,9},{11,1... | collective-permute-start | bytes 49160 | tf_op jit(solution)/shard_map/ppermute | solution.py:258
  48.6 7.4 %collective-permute-start.3 = (bf16[4,16,128]{2,1,0:T(8,128)(2,1)}, bf16[4,16,128]{2,1,0:T(8,128)(2,1)S(1)}, u32[]{:S(2)}, u32[]{:S(2)}) collective-permute-start(bf16[4,16,128]{2,1,0:T(8,128)(2,1)} %get-tuple-element.9.side_ref), channel_id=1, source_target_pairs={{2,0},{3,1},{0,2},{1,3},{6,4},{7,5},{4,6},{5,7},{10,8},{11,9},{8,1... | collective-permute-start | bytes 49160 | tf_op jit(solution)/shard_map/ppermute | solution.py:258
  51.1 5.9 %collective-permute-start.4 = (bf16[4,16,128]{2,1,0:T(8,128)(2,1)}, bf16[4,16,128]{2,1,0:T(8,128)(2,1)S(1)}, u32[]{:S(2)}, u32[]{:S(2)}) collective-permute-start(bf16[4,16,128]{2,1,0:T(8,128)(2,1)} %get-tuple-element.9.side_ref), channel_id=1, source_target_pairs={{3,0},{0,1},{1,2},{2,3},{7,4},{4,5},{5,6},{6,7},{11,8},{8,9},{9,10... | collective-permute-start | bytes 49160 | tf_op jit(solution)/shard_map/ppermute | solution.py:258
  53.7 34.0 %copy-start.2 = (f32[1,48,4,128]{3,2,1,0:T(4,128)S(1)}, f32[1,48,4,128]{3,2,1,0:T(4,128)}, u32[]{:S(2)}) copy-start(f32[1,48,4,128]{3,2,1,0:T(4,128)} %param.11) | copy-start | bytes 294916
  57.0 0.8 copy-start.1

commit v13 on v12

--- a/solution.py
+++ b/solution.py
@@ -163,8 +163,8 @@
 
 
 def main_kernel(
-    p_ref, halo_ref, own_ref, t_ref, side1_ref, side2_ref, side3_ref, row_ref, col_ref,
-    out_ref, val_ref, side_ref, final_ref, table_ref, sem, own_sem,
+    p_ref, far_ref, near_ref, own_ref, t_ref, side1_ref, side2_ref, side3_ref, row_ref, col_ref,
+    out_ref, val_ref, halo_ref, side_ref, final_ref, table_ref, sem, own_sem,
 ):
     owners = row_ref.shape[0]
     here = axis_index("x")
@@ -172,6 +172,7 @@
     bring.start()
     for k, ref in enumerate((side1_ref, side2_ref, side3_ref)):
         side_ref[k] = ref[...]
+    halo_ref[...] = merge(near_ref[0:4], far_ref[0:4])
 
     def one_level(i, carry):
         y, x = lax.rem(i, 4), lax.rem(here + 1 + i // 4, 4)
@@ -217,7 +218,7 @@
     move.wait()
 
 
-def advance_and_pick(state, halo, own, planes, sides, rows, cols):
+def advance_and_pick(state, far, near, own, planes, sides, rows, cols):
     owners = rows.shape[0]
     return pl.pallas_call(
         main_kernel,
@@ -225,9 +226,10 @@
             jax.ShapeDtypeStruct(state.shape, F32),
             jax.ShapeDtypeStruct((owners, 4, 128), F32),
         ),
-        in_specs=[VMEM, VMEM, HBM] + [VMEM] * 6,
+        in_specs=[VMEM, VMEM, VMEM, HBM] + [VMEM] * 6,
         out_specs=(HBM, VMEM),
         scratch_shapes=[
+            pltpu.VMEM((4,) + TILE, F32),
             pltpu.VMEM((3, 4) + TILE, BF16),
             pltpu.VMEM(state.shape, F32),
             pltpu.VMEM((512, 512), BF16),
@@ -235,7 +237,7 @@
             pltpu.SemaphoreType.DMA,
         ],
         name="advance_and_pick",
-    )(in_vmem(state), in_vmem(halo), own, *map(in_vmem, (planes, *sides, rows, cols)))
+    )(in_vmem(state), in_vmem(far), in_vmem(near), own, *map(in_vmem, (planes, *sides, rows, cols)))
 
 
 def on_device(perturbation, trajectory, site_col, site_lev, obs_counts, obs_weights):
@@ -260,7 +262,7 @@
     live = jnp.arange(slots, dtype=jnp.int32)[None, :] < obs_counts
     rows = jnp.where(live, site_lev[:, 0, :] * 16 + site_col[:, 0, :] // 128, -1)
     cols = site_col[:, 0, :] % 128
-    final, values = advance_and_pick(state, halo, own, planes, sides, rows, cols)
+    final, values = advance_and_pick(state, far, near, own, planes, sides, rows, cols)
     received = lax.all_to_all(values, "space", 0, 0, tiled=True)
     summed = jnp.sum(obs_weights[0] * received, axis=1)
     return (final.reshape(perturbation.shape), summed.reshape(1, 1, tiles, slots))

time: 89 us -> 88.2 us (level)
  no operation moved by 1% of the time
where the time goes in v13:
time: 88.2 us; the launch traced here: 87.6 us
  blocking collectives  39.8 us (45%)
  starting transfers between devices  30.3 us (34%)
  Pallas kernels  13.8 us (16%)
  waiting for transfers between devices  2.15 us (2%)
    all_to_all x1, blocking collectives, on_device(): received = lax.all_to_all(values, 'space', 0, 0, tiled=True)  22.6 us
    all_to_all x1, blocking collectives, on_device(): first = lax.all_to_all(spread(local), 'yhi', 0, 0, tiled=True)  17.3 us
    ppermute x1, starting transfers between devices, on_device(): near = lax.ppermute(edge, 'space', pairs)  10.4 us
    ppermute x3, starting transfers between devices, on_device(): lax.ppermute(side, 'x', [((i + k) % 4, i) for i in range(4)])  9.54 us
    pallas_call x1, Pallas kernels, advance_and_pick(): pl.pallas_call(main_kernel, out_shape=(jax.ShapeDtypeStruct(state.shape,...  7.36 us
    ppermute x1, starting transfers between devices, on_device(): far = lax.ppermute(edge, 'space', crossed)  6.46 us
    all_to_all x1, starting transfers between devices, on_device(): planes = lax.all_to_all(copies, 'x', 0, 0, tiled=True)  3.89 us
    pallas_call x2, Pallas kernels, spread(): pl.pallas_call(spread_kernel, out_shape=jax.ShapeDtypeStruct((4,) + plane...  2.69 us
  transfers between devices with their start and end apart: 6, of which 2 were waited for; matrix products, arithmetic and copies ran while one was open for 0% of the time, Pallas kernels for 4%

profile of v13, /device:TPU:1, one launch (start us, length us, event | category | flops | bytes accessed | tf_op | source)
XLA Modules:
  0.0 87.6 jit_solution(7706237717843926592)
XLA Ops:
  0.6 1.6 %spread.2 = bf16[4,288,128]{2,1,0:T(8,128)(2,1)} custom-call(bf16[288,128]{1,0:T(8,128)(2,1)} %bitcast.16), custom_call_target="tpu_custom_call" | custom-call | tf_op jit(solution)/shard_map/spread/pallas_call | solution.py:39
  2.3 17.3 %all_to_all.15.t_ref = bf16[4,288,128]{2,1,0:T(8,128)(2,1)S(1)} all-to-all(bf16[4,288,128]{2,1,0:T(8,128)(2,1)} %spread.2), channel_id=1, replica_groups=mesh['space'=48,'yhi'=4,'x'=4] {'yhi'}, dimensions={0} | all-to-all | bytes 589824 | tf_op jit(solution)/shard_map/all_to_all | solution.py:250
  19.5 1.1 %spread.3 = bf16[4,4,288,128]{3,2,1,0:T(8,128)(2,1)} custom-call(bf16[4,288,128]{2,1,0:T(8,128)(2,1)S(1)} %all_to_all.15.t_ref), custom_call_target="tpu_custom_call" | custom-call | tf_op jit(solution)/shard_map/spread/pallas_call | solution.py:39
  20.6 0.0 copy-start
  20.6 0.0 copy-start.2
  20.6 0.0 copy-start.3
  20.6 0.0 copy-start.4
  20.6 3.9 %all-to-all-start.1 = ((bf16[4,4,288,128]{3,2,1,0:T(8,128)(2,1)}), bf16[4,4,288,128]{3,2,1,0:T(8,128)(2,1)S(1)}, u32[]{:S(2)}, u32[]{:S(2)}) async-start(bf16[4,4,288,128]{3,2,1,0:T(8,128)(2,1)} %spread.3), calls=%async_computation.1 | async-start | bytes 2359296 | tf_op jit(solution)/shard_map/all_to_all | solution.py:252
  24.5 0.9 %pack.1 = f32[8,16,128]{2,1,0:T(8,128)} custom-call(f32[4,4,4,16,128]{4,3,2,1,0:T(8,128)S(1)} %bitcast.13, bf16[4,288,128]{2,1,0:T(8,128)(2,1)S(1)} %all_to_all.15.t_ref), custom_call_target="tpu_custom_call" | custom-call | tf_op jit(solution)/shard_map/pack/pallas_call | solution.py:66
  25.4 6.5 %collective-permute-start = (f32[8,16,128]{2,1,0:T(8,128)}, f32[8,16,128]{2,1,0:T(8,128)S(1)}, u32[]{:S(2)}, u32[]{:S(2)}) collective-permute-start(f32[8,16,128]{2,1,0:T(8,128)} %pack.1), channel_id=1, source_target_pairs={{0,752},{16,32},{32,16},{48,64},{64,48},{80,96},{96,80},{112,128},... | collective-permute-start | bytes 196616 | tf_op jit(solution)/shard_map/ppermute | solution.py:256
  31.9 10.4 %collective-permute-start.1 = (f32[8,16,128]{2,1,0:T(8,128)}, f32[8,16,128]{2,1,0:T(8,128)S(1)}, u32[]{:S(2)}, u32[]{:S(2)}) collective-permute-start(f32[8,16,128]{2,1,0:T(8,128)} %pack.1), channel_id=1, source_target_pairs={{0,16},{16,0},{32,48},{48,32},{64,80},{80,64},{96,112},{112,96},{1... | collective-permute-start | bytes 196616 | tf_op jit(solution)/shard_map/ppermute | solution.py:257
  42.3 0.0 collective-permute-done.far_ref
  42.3 1.1 %collective-permute-done.1.near_ref = f32[8,16,128]{2,1,0:T(8,128)S(1)} collective-permute-done((f32[8,16,128]{2,1,0:T(8,128)}, f32[8,16,128]{2,1,0:T(8,128)S(1)}, u32[]{:S(2)}, u32[]{:S(2)}) %collective-permute-start.1) | collective-permute-done | bytes 65568 | tf_op jit(solution)/shard_map/ppermute | solution.py:257
  43.4 0.6 fill.1
  44.0 4.6 %collective-permute-start.2 = (bf16[4,16,128]{2,1,0:T(8,128)(2,1)}, bf16[4,16,128]{2,1,0:T(8,128)(2,1)S(1)}, u32[]{:S(2)}, u32[]{:S(2)}) collective-permute-start(bf16[4,16,128]{2,1,0:T(8,128)(2,1)} %get-tuple-element.9.side_ref), channel_id=1, source_target_pairs={{1,0},{2,1},{3,2},{0,3},{5,4},{6,5},{7,6},{4,7},{9,8},{10,9},{11,1... | collective-permute-start | bytes 49160 | tf_op jit(solution)/shard_map/ppermute | solution.py:260
  48.6 2.5 %collective-permute-start.3 = (bf16[4,16,128]{2,1,0:T(8,128)(2,1)}, bf16[4,16,128]{2,1,0:T(8,128)(2,1)S(1)}, u32[]{:S(2)}, u32[]{:S(2)}) collective-permute-start(bf16[4,16,128]{2,1,0:T(8,128)(2,1)} %get-tuple-element.9.side_ref), channel_id=1, source_target_pairs={{2,0},{3,1},{0,2},{1,3},{6,4},{7,5},{4,6},{5,7},{10,8},{11,9},{8,1... | collective-permute-start | bytes 49160 | tf_op jit(solution)/shard_map/ppermute | solution.py:260
  51.1 2.5 %collective-permute-start.4 = (bf16[4,16,128]{2,1,0:T(8,128)(2,1)}, bf16[4,16,128]{2,1,0:T(8,128)(2,1)S(1)}, u32[]{:S(2)}, u32[]{:S(2)}) collective-permute-start(bf16[4,16,128]{2,1,0:T(8,128)(2,1)} %get-tuple-element.9.side_ref), channel_id=1, source_target_pairs={{3,0},{0,1},{1,2},{2,3},{7,4},{4,5},{5,6},{6,7},{11,8},{8,9},{9,10... | collective-permute-start | bytes 49160 | tf_op jit(solution)/shard_map/ppermute | solution.py:260
  53.6 0.1 add_select_fusion
  53.7 2.2 %advance_own.1.own_ref = f32[4,4,16,128]{3,2,1,0:T(8,128)} custom-call(f32[4,4,4,16,128]{4,3,2,1,0:T(8,128)S(1)} %bitcast.14, f32[4,16,128]{2,1,0:T(8,128)} %get-tuple-element.8.halo_ref, bf16[4,288,128]{2,1,0:T(8,128)(2,1)S(1)} %all_to_all.15.t_ref, bf16[4,16,128]{2,1,0:T(8,128)(2,1)} %get-tuple-element.9.side_ref), custom_call_target="tpu_custom_call" | custom-call | tf_op jit(solution)/shard_map/advance_own/pallas_call | solution.py:156
  56.0 1.1 %collective-permute-done.4.side3_ref = bf16[4,16,128]{2,1,0:T(8,128)(2,1)S(1)} collective-permute-done((bf16[4,16,128]{2,1,0:T(8,128)(2,1)}, bf16[4,16,128]{2,1,0:T(8,128)(2,1)S(1)}, u32[]{:S(2)}, u32[]{:S(2)}) %collective-permute-start.4) | collective-permute-done | bytes 16416 | tf_op jit(solution)/shard_map/ppermute | solution.py:260
  57.0 0.0 all-to-all-done.1.t_ref
  57.0 7.4 %advance_and_pick.1 = (f32[4,4,4,16,128]{4,3,2,1,0:T(8,128)}, f32[48,4,128]{2,1,0:T(4,128)}) custom-call(f32[4,4,4,16,128]{4,3,2,1,0:T(8,128)S(1)} %bitcast.15, f32[8,16,128]{2,1,0:T(8,128)S(1)} %collective-permute-done.far_ref, f32[8,16,128]{2,1,0:T(8,128)S(1)} %collective-permute-done.1.near_ref, f32[4,4,16,128]{3,2,1,0:T(8,128)} %advance_own.1.own_ref, ...), custom_call_target="tpu_custom_call" | custom-call | tf_op jit(solution)/shard_map/advance_and_pick/pallas_call | solution.py:223
  64.4 22.6 %all_to_all.16 = f32[48,4,128]{2,1,0:T(4,128)S(1)} all-to-all(f32[48,4,128]{2,1,0:T(4,128)} %get-tuple-element.11), channel_id=1, replica_groups=mesh['space'=48,'yhi'=4,'x'=4] {'space'}, dimensions={0} | all-to-all | bytes 196608 | tf_op jit(solution)/shard_map/all_to_all | solution.py:266
  87.0 0.7 fusion
  (8 shorter events, 0.0 us)
Async XLA Ops:
  20.6 3.9 %copy-start = (f32[1,4,16,16,128]{4,3,2,1,0:T(8,128)S(1)}, f32[1,4,16,16,128]{4,3,2,1,0:T(8,128)}, u32[]{:S(2)}) copy-start(f32[1,4,16,16,128]{4,3,2,1,0:T(8,128)} %param.6) | copy-start | bytes 1572868
  20.6 33.0 %copy-start.2 = (s32[48,1,128]{2,1,0:T(1,128)S(1)}, s32[48,1,128]{2,1,0:T(1,128)}, u32[]{:S(2)}) copy-start(s32[48,1,128]{2,1,0:T(1,128)} %param.8) | copy-start | bytes 73732
  20.6 33.0 %copy-start.3 = (s32[48,1,128]{2,1,0:T(1,128)S(1)}, s32[48,1,128]{2,1,0:T(1,128)}, u32[]{:S(2)}) copy-start(s32[48,1,128]{2,1,0:T(1,128)} %param.9) | copy-start | bytes 73732
  20.6 33.0 %copy-start.4 = (s32[48,1]{0,1:T(1,128)S(1)}, s32[48,1]{0,1:T(1,128)}, u32[]{:S(2)}) copy-start(s32[48,1]{0,1:T(1,128)} %param.10) | copy-start | bytes 580
  20.6 36.4 %all-to-all-start.1 = ((bf16[4,4,288,128]{3,2,1,0:T(8,128)(2,1)}), bf16[4,4,288,128]{3,2,1,0:T(8,128)(2,1)S(1)}, u32[]{:S(2)}, u32[]{:S(2)}) async-start(bf16[4,4,288,128]{3,2,1,0:T(8,128)(2,1)} %spread.3), calls=%async_computation.1 | async-start | bytes 2359296 | tf_op jit(solution)/shard_map/all_to_all | solution.py:252
  25.4 16.9 %collective-permute-start = (f32[8,16,128]{2,1,0:T(8,128)}, f32[8,16,128]{2,1,0:T(8,128)S(1)}, u32[]{:S(2)}, u32[]{:S(2)}) collective-permute-start(f32[8,16,128]{2,1,0:T(8,128)} %pack.1), channel_id=1, source_target_pairs={{0,752},{16,32},{32,16},{48,64},{64,48},{80,96},{96,80},{112,128},... | collective-permute-start | bytes 196616 | tf_op jit(solution)/shard_map/ppermute | solution.py:256
  31.9 11.5 %collective-permute-start.1 = (f32[8,16,128]{2,1,0:T(8,128)}, f32[8,16,128]{2,1,0:T(8,128)S(1)}, u32[]{:S(2)}, u32[]{:S(2)}) collective-permute-start(f32[8,16,128]{2,1,0:T(8,128)} %pack.1), channel_id=1, source_target_pairs={{0,16},{16,0},{32,48},{48,32},{64,80},{80,64},{96,112},{112,96},{1... | collective-permute-start | bytes 196616 | tf_op jit(solution)/shard_map/ppermute | solution.py:257
  44.0 11.9 %collective-permute-start.2 = (bf16[4,16,128]{2,1,0:T(8,128)(2,1)}, bf16[4,16,128]{2,1,0:T(8,128)(2,1)S(1)}, u32[]{:S(2)}, u32[]{:S(2)}) collective-permute-start(bf16[4,16,128]{2,1,0:T(8,128)(2,1)} %get-tuple-element.9.side_ref), channel_id=1, source_target_pairs={{1,0},{2,1},{3,2},{0,3},{5,4},{6,5},{7,6},{4,7},{9,8},{10,9},{11,1... | collective-permute-start | bytes 49160 | tf_op jit(solution)/shard_map/ppermute | solution.py:260
  48.6 7.3 %collective-permute-start.3 = (bf16[4,16,128]{2,1,0:T(8,128)(2,1)}, bf16[4,16,128]{2,1,0:T(8,128)(2,1)S(1)}, u32[]{:S(2)}, u32[]{:S(2)}) collective-permute-start(bf16[4,16,128]{2,1,0:T(8,128)(2,1)} %get-tuple-element.9.side_ref), channel_id=1, source_target_pairs={{2,0},{3,1},{0,2},{1,3},{6,4},{7,5},{4,6},{5,7},{10,8},{11,9},{8,1... | collective-permute-start | bytes 49160 | tf_op jit(solution)/shard_map/ppermute | solution.py:260
  51.1 5.9 %collective-permute-start.4 = (bf16[4,16,128]{2,1,0:T(8,128)(2,1)}, bf16[4,16,128]{2,1,0:T(8,128)(2,1)S(1)}, u32[]{:S(2)}, u32[]{:S(2)}) collective-permute-start(bf16[4,16,128]{2,1,0:T(8,128)(2,1)} %get-tuple-element.9.side_ref), channel_id=1, source_target_pairs={{3,0},{0,1},{1,2},{2,3},{7,4},{4,5},{5,6},{6,7},{11,8},{8,9},{9,10... | collective-permute-start | bytes 49160 | tf_op jit(solution)/shard_map/ppermute | solution.py:260
  55.9 31.0 %copy-start.1 = (f32[1,48,4,128]{3,2,1,0:T(4,128)S(1)}, f32[1,48,4,128]{3,2,1,0:T(4,128)}, u32[]{:S(2)}) copy-start(f32[1,48,4,128]{3,2,1,0:T(4,128)} %param.11) | copy-start | bytes 294916

commit v14 on v11

--- a/solution.py
+++ b/solution.py
@@ -150,7 +150,7 @@
             out_ref[f, y] = state[f]
         return carry
 
-    lax.fori_loop(0, 4, one_level, 0, unroll=2)
+    lax.fori_loop(0, 4, one_level, 0, unroll=4)
 
 
 def advance_own(state, halo, planes, side):
@@ -180,7 +180,7 @@
             final_ref[f, y, x] = state[f]
         return carry
 
-    lax.fori_loop(0, 12, one_level, 0, unroll=2)
+    lax.fori_loop(0, 12, one_level, 0, unroll=3)
     bring.wait()
     move = pltpu.make_async_copy(final_ref, out_ref, sem)
     move.start()

time: 87.5 us -> 87.5 us (level)
  transfers between devices with their start and end apart: 4 -> 4, of which waited for: 2 -> 2; matrix products, arithmetic and copies ran while one was open for 0% -> 0% of each run, Pallas kernels for 4% -> 5%
where the time goes in v14:
time: 87.5 us; the launch traced here: 86.7 us
  blocking collectives  40.7 us (47%)
  starting transfers between devices  25.1 us (29%)
  Pallas kernels  13.9 us (16%)
  waiting for transfers between devices  5.47 us (6%)
    all_to_all x1, blocking collectives, on_device(): received = lax.all_to_all(values, 'space', 0, 0, tiled=True)  23.4 us
    all_to_all x1, blocking collectives, on_device(): first = lax.all_to_all(spread(local), 'yhi', 0, 0, tiled=True)  17.3 us
    ppermute x1, starting transfers between devices, on_device(): near = lax.ppermute(edge, 'space', pairs)  10.4 us
    pallas_call x1, Pallas kernels, advance_and_pick(): pl.pallas_call(main_kernel, out_shape=(jax.ShapeDtypeStruct(state.shape,...  7.33 us
    ppermute x1, starting transfers between devices, on_device(): far = lax.ppermute(edge, 'space', crossed)  6.46 us
    all_to_all x1, waiting for transfers between devices, on_device(): sides = lax.all_to_all(side, 'x', 0, 0, tiled=True)  4.39 us
    all_to_all x1, starting transfers between devices, on_device(): sides = lax.all_to_all(side, 'x', 0, 0, tiled=True)  4.36 us
    all_to_all x1, starting transfers between devices, on_device(): planes = lax.all_to_all(copies, 'x', 0, 0, tiled=True)  3.89 us
  transfers between devices with their start and end apart: 4, of which 2 were waited for; matrix products, arithmetic and copies ran while one was open for 0% of the time, Pallas kernels for 5%

profile of v14, /device:TPU:1, one launch (start us, length us, event | category | flops | bytes accessed | tf_op | source)
XLA Modules:
  0.0 86.7 jit_solution(3411388633605769348)
XLA Ops:
  0.6 1.6 %spread.2 = bf16[4,288,128]{2,1,0:T(8,128)(2,1)} custom-call(bf16[288,128]{1,0:T(8,128)(2,1)} %bitcast.16), custom_call_target="tpu_custom_call" | custom-call | tf_op jit(solution)/shard_map/spread/pallas_call | solution.py:39
  2.3 17.3 %all_to_all.20.t_ref = bf16[4,288,128]{2,1,0:T(8,128)(2,1)S(1)} all-to-all(bf16[4,288,128]{2,1,0:T(8,128)(2,1)} %spread.2), channel_id=1, replica_groups=mesh['space'=48,'yhi'=4,'x'=4] {'yhi'}, dimensions={0} | all-to-all | bytes 589824 | tf_op jit(solution)/shard_map/all_to_all | solution.py:245
  19.5 1.1 %spread.3 = bf16[4,4,288,128]{3,2,1,0:T(8,128)(2,1)} custom-call(bf16[4,288,128]{2,1,0:T(8,128)(2,1)S(1)} %all_to_all.20.t_ref), custom_call_target="tpu_custom_call" | custom-call | tf_op jit(solution)/shard_map/spread/pallas_call | solution.py:39
  20.6 0.0 copy-start
  20.6 3.9 %all-to-all-start.1 = ((bf16[4,4,288,128]{3,2,1,0:T(8,128)(2,1)}), bf16[4,4,288,128]{3,2,1,0:T(8,128)(2,1)S(1)}, u32[]{:S(2)}, u32[]{:S(2)}) async-start(bf16[4,4,288,128]{3,2,1,0:T(8,128)(2,1)} %spread.3), calls=%async_computation.1 | async-start | bytes 2359296 | tf_op jit(solution)/shard_map/all_to_all | solution.py:247
  24.5 0.0 copy-done
  24.5 0.9 %pack.1 = f32[8,16,128]{2,1,0:T(8,128)} custom-call(f32[4,4,4,16,128]{4,3,2,1,0:T(8,128)S(1)} %bitcast.13, bf16[4,288,128]{2,1,0:T(8,128)(2,1)S(1)} %all_to_all.20.t_ref), custom_call_target="tpu_custom_call" | custom-call | tf_op jit(solution)/shard_map/pack/pallas_call | solution.py:66
  25.4 6.5 %collective-permute-start = (f32[8,16,128]{2,1,0:T(8,128)}, f32[8,16,128]{2,1,0:T(8,128)S(1)}, u32[]{:S(2)}, u32[]{:S(2)}) collective-permute-start(f32[8,16,128]{2,1,0:T(8,128)} %pack.1), channel_id=1, source_target_pairs={{0,752},{16,32},{32,16},{48,64},{64,48},{80,96},{96,80},{112,128},... | collective-permute-start | bytes 196616 | tf_op jit(solution)/shard_map/ppermute | solution.py:251
  31.9 10.4 %collective-permute-start.1 = (f32[8,16,128]{2,1,0:T(8,128)}, f32[8,16,128]{2,1,0:T(8,128)S(1)}, u32[]{:S(2)}, u32[]{:S(2)}) collective-permute-start(f32[8,16,128]{2,1,0:T(8,128)} %pack.1), channel_id=1, source_target_pairs={{0,16},{16,0},{32,48},{48,32},{64,80},{80,64},{96,112},{112,96},{1... | collective-permute-start | bytes 196616 | tf_op jit(solution)/shard_map/ppermute | solution.py:252
  42.3 0.0 collective-permute-done.far_ref
  42.3 1.1 %collective-permute-done.1.near_ref = f32[8,16,128]{2,1,0:T(8,128)S(1)} collective-permute-done((f32[8,16,128]{2,1,0:T(8,128)}, f32[8,16,128]{2,1,0:T(8,128)S(1)}, u32[]{:S(2)}, u32[]{:S(2)}) %collective-permute-start.1) | collective-permute-done | bytes 65568 | tf_op jit(solution)/shard_map/ppermute | solution.py:252
  43.4 0.7 fill.1
  44.1 2.4 %advance_own.1.own_ref = f32[4,4,16,128]{3,2,1,0:T(8,128)} custom-call(f32[4,4,4,16,128]{4,3,2,1,0:T(8,128)S(1)} %bitcast.14, f32[4,16,128]{2,1,0:T(8,128)} %get-tuple-element.11.halo_ref, bf16[4,288,128]{2,1,0:T(8,128)(2,1)S(1)} %all_to_all.20.t_ref, bf16[4,4,16,128]{3,2,1,0:T(8,128)(2,1)} %get-tuple-element.15.side_ref), custom_call_target="tpu_custom_call" | custom-call | tf_op jit(solution)/shard_map/advance_own/pallas_call | solution.py:157
  46.4 0.0 all-to-all-done.1.t_ref
  46.4 4.4 %all-to-all-start.2 = ((bf16[4,4,16,128]{3,2,1,0:T(8,128)(2,1)}), bf16[4,4,16,128]{3,2,1,0:T(8,128)(2,1)S(1)}, u32[]{:S(2)}, u32[]{:S(2)}) async-start(bf16[4,4,16,128]{3,2,1,0:T(8,128)(2,1)} %get-tuple-element.15.side_ref), calls=%async_computation.2 | async-start | bytes 131072 | tf_op jit(solution)/shard_map/all_to_all | solution.py:256
  50.8 0.0 copy-done.3
  50.8 0.0 copy-done.4
  50.8 0.0 copy-done.5
  50.8 0.1 add_select_fusion
  50.9 4.4 %all-to-all-done.2.side_ref = bf16[4,4,16,128]{3,2,1,0:T(8,128)(2,1)S(1)} async-done(((bf16[4,4,16,128]{3,2,1,0:T(8,128)(2,1)}), bf16[4,4,16,128]{3,2,1,0:T(8,128)(2,1)S(1)}, u32[]{:S(2)}, u32[]{:S(2)}) %all-to-all-start.2) | async-done | bytes 65568 | tf_op jit(solution)/shard_map/all_to_all | solution.py:256
  55.3 0.0 copy-done.1
  55.3 7.3 %advance_and_pick.1 = (f32[4,4,4,16,128]{4,3,2,1,0:T(8,128)}, f32[48,4,128]{2,1,0:T(4,128)}) custom-call(f32[4,4,4,16,128]{4,3,2,1,0:T(8,128)S(1)} %bitcast.15, f32[4,16,128]{2,1,0:T(8,128)S(1)} %copy-done.1, f32[4,4,16,128]{3,2,1,0:T(8,128)} %advance_own.1.own_ref, bf16[4,4,288,128]{3,2,1,0:T(8,128)(2,1)S(1)} %all-to-all-done.1.t_ref, ...), custom_call_target="tpu_custom_call" | custom-call | tf_op jit(solution)/shard_map/advance_and_pick/pallas_call | solution.py:220
  62.6 23.4 %all_to_all.21 = f32[48,4,128]{2,1,0:T(4,128)S(1)} all-to-all(f32[48,4,128]{2,1,0:T(4,128)} %get-tuple-element.17), channel_id=1, replica_groups=mesh['space'=48,'yhi'=4,'x'=4] {'space'}, dimensions={0} | all-to-all | bytes 196608 | tf_op jit(solution)/shard_map/all_to_all | solution.py:262
  86.1 0.7 fusion
  (6 shorter events, 0.0 us)
Async XLA Ops:
  20.6 3.9 %copy-start = (f32[1,4,16,16,128]{4,3,2,1,0:T(8,128)S(1)}, f32[1,4,16,16,128]{4,3,2,1,0:T(8,128)}, u32[]{:S(2)}) copy-start(f32[1,4,16,16,128]{4,3,2,1,0:T(8,128)} %param.6) | copy-start | bytes 1572868
  20.6 25.8 %all-to-all-start.1 = ((bf16[4,4,288,128]{3,2,1,0:T(8,128)(2,1)}), bf16[4,4,288,128]{3,2,1,0:T(8,128)(2,1)S(1)}, u32[]{:S(2)}, u32[]{:S(2)}) async-start(bf16[4,4,288,128]{3,2,1,0:T(8,128)(2,1)} %spread.3), calls=%async_computation.1 | async-start | bytes 2359296 | tf_op jit(solution)/shard_map/all_to_all | solution.py:247
  24.5 26.3 %copy-start.3 = (s32[48,1,128]{2,1,0:T(1,128)S(1)}, s32[48,1,128]{2,1,0:T(1,128)}, u32[]{:S(2)}) copy-start(s32[48,1,128]{2,1,0:T(1,128)} %param.8) | copy-start | bytes 73732
  24.5 26.3 %copy-start.4 = (s32[48,1,128]{2,1,0:T(1,128)S(1)}, s32[48,1,128]{2,1,0:T(1,128)}, u32[]{:S(2)}) copy-start(s32[48,1,128]{2,1,0:T(1,128)} %param.9) | copy-start | bytes 73732
  24.5 26.3 %copy-start.5 = (s32[48,1]{0,1:T(1,128)S(1)}, s32[48,1]{0,1:T(1,128)}, u32[]{:S(2)}) copy-start(s32[48,1]{0,1:T(1,128)} %param.10) | copy-start | bytes 580
  25.4 16.9 %collective-permute-start = (f32[8,16,128]{2,1,0:T(8,128)}, f32[8,16,128]{2,1,0:T(8,128)S(1)}, u32[]{:S(2)}, u32[]{:S(2)}) collective-permute-start(f32[8,16,128]{2,1,0:T(8,128)} %pack.1), channel_id=1, source_target_pairs={{0,752},{16,32},{32,16},{48,64},{64,48},{80,96},{96,80},{112,128},... | collective-permute-start | bytes 196616 | tf_op jit(solution)/shard_map/ppermute | solution.py:251
  31.9 11.5 %collective-permute-start.1 = (f32[8,16,128]{2,1,0:T(8,128)}, f32[8,16,128]{2,1,0:T(8,128)S(1)}, u32[]{:S(2)}, u32[]{:S(2)}) collective-permute-start(f32[8,16,128]{2,1,0:T(8,128)} %pack.1), channel_id=1, source_target_pairs={{0,16},{16,0},{32,48},{48,32},{64,80},{80,64},{96,112},{112,96},{1... | collective-permute-start | bytes 196616 | tf_op jit(solution)/shard_map/ppermute | solution.py:252
  44.1 11.2 %copy-start.1 = (f32[4,16,128]{2,1,0:T(8,128)S(1)}, f32[4,16,128]{2,1,0:T(8,128)}, u32[]{:S(2)}) copy-start(f32[4,16,128]{2,1,0:T(8,128)} %get-tuple-element.11.halo_ref) | copy-start | bytes 98308
  46.4 39.6 %copy-start.2 = (f32[1,48,4,128]{3,2,1,0:T(4,128)S(1)}, f32[1,48,4,128]{3,2,1,0:T(4,128)}, u32[]{:S(2)}) copy-start(f32[1,48,4,128]{3,2,1,0:T(4,128)} %param.11) | copy-start | bytes 294916
  46.4 8.8 %all-to-all-start.2 = ((bf16[4,4,16,128]{3,2,1,0:T(8,128)(2,1)}), bf16[4,4,16,128]{3,2,1,0:T(8,128)(2,1)S(1)}, u32[]{:S(2)}, u32[]{:S(2)}) async-start(bf16[4,4,16,128]{3,2,1,0:T(8,128)(2,1)} %get-tuple-element.15.side_ref), calls=%async_computation.2 | async-start | bytes 131072 | tf_op jit(solution)/shard_map/all_to_all | solution.py:256
